TPU v7x, 32 devices: a whole 2x2x4 slice. The times are simulated.
32 devices in a mesh: src: 4 (over y, core), rcv: 8 (over z, x).
Axes of the slice: x: 2, y: 2, z: 4, core: 2. Of those that a mesh axis runs over, the one named last changes fastest.
Arguments:
- data: bfloat16 [2, 4096, 4096], P(None, ('src', 'rcv')), may hold values from -0.8984375 to 0.8984375
- fill_mask: int32 [4096, 4096], P(('src', 'rcv')), may hold values 0 or 1
- obliquity: float32 [4096], replicated, may hold values from 0.25 to 4
- aperture: int32 [8, 8, 8], P('src'), may hold values from 0 to 7, as said below
- lengths: int32 [8, 8], P('src', 'rcv'), may hold values from 1 to 8, as said below
Outputs:
- predicted: float32 [2, 4096, 4096], P(None, 'src', 'rcv')
Inputs may be any that keep to these rules, and one draw needn't show every extreme that they name: `aperture`: every entry is a tile index; the 8 entries of one output tile are distinct; only the first lengths entries of a list are used. `lengths`: some output tile uses all 8 entries of its list.
All inputs are finite; a program needn't handle non-finite values. No bound on the sum of `fill_mask` on one device may be relied on, other than what follows from the above.
Results may differ from a plain program's by a relative error of at most 0.0028.
Values may be sent and summed in bfloat16 or wider, within the bound.
No kernel may reach another device: no remote copies, remote signals or barrier semaphores. Data moves between devices by JAX's collectives and lax.ppermute only.
A program may use at most 128 MiB of HBM per device.

v0:
```python
import jax
import jax.numpy as jnp
import numpy as np
from jax import lax
from jax.experimental import pallas as pl
from jax.experimental.pallas import tpu as pltpu
from jax.sharding import PartitionSpec as P


TILE_SIZE = 512
AHEAD = 2


def ring_order(count):
    return list(range(0, count, 2)) + list(range(1, count, 2))[::-1]


def split_kernel(data_ref, *out_refs):
    rows = data_ref.shape[1]
    for part, out_ref in enumerate(out_refs):
        for block in range(out_ref.shape[0]):
            out_ref[block] = data_ref[part, :, block * rows : (block + 1) * rows].T


def transposed_blocks(data, devices):
    _, rows, _ = data.shape
    if rows % 128:
        return tuple(jnp.transpose(p.reshape(rows, devices, rows), (1, 0, 2)) for p in data)
    group = 8
    return pl.pallas_call(
        split_kernel,
        out_shape=(jax.ShapeDtypeStruct((devices, rows, rows), data.dtype),) * 2,
        grid=(devices // group,),
        in_specs=[pl.BlockSpec((2, rows, group * rows), lambda i: (0, 0, i))],
        out_specs=(pl.BlockSpec((group, rows, rows), lambda i: (i, 0, 0)),) * 2,
    )(data)


def fill_kernel(data_ref, mask_ref, arrived_ref, out_ref):
    rows = data_ref.shape[0]
    for block in range(arrived_ref.shape[0]):
        span = slice(block * rows, (block + 1) * rows)
        out_ref[:, span] = jnp.where(
            mask_ref[:, span] == 1, data_ref[:, span], arrived_ref[block]
        )


def fill(data, mask, arrived, part):
    _, rows, total = data.shape
    devices = arrived.shape[0]
    if rows % 128:
        transposed = jnp.transpose(arrived, (2, 0, 1)).reshape(rows, total)
        return jnp.where(mask == 1, data[part], transposed)
    group = 8
    return pl.pallas_call(
        fill_kernel,
        out_shape=jax.ShapeDtypeStruct((rows, total), data.dtype),
        grid=(devices // group,),
        in_specs=[
            pl.BlockSpec((None, rows, group * rows), lambda i: (part, 0, i)),
            pl.BlockSpec((rows, group * rows), lambda i: (0, i)),
            pl.BlockSpec((group, rows, rows), lambda i: (i, 0, 0)),
        ],
        out_specs=pl.BlockSpec((rows, group * rows), lambda i: (0, i)),
    )(data, mask, arrived)


def product_kernel(rows, plan_ref, used_ref, *refs):
    (row_refs, piece_refs), out_ref, scratch = refs[0], refs[1], refs[2:]
    left, right, row_sem, piece_sem = scratch
    inner_tiles = right.shape[0]
    out_tiles = out_ref.shape[1] // TILE_SIZE

    def piece_copies():
        copies = []
        at = len(row_refs)
        for ref in piece_refs:
            for index in range(ref.shape[0]):
                first = plan_ref[at]
                tile, offset = first // TILE_SIZE, first % TILE_SIZE
                for part in range(2):
                    row = pl.multiple_of(offset + (1 - part) * TILE_SIZE, rows)
                    copies.append(
                        pltpu.make_async_copy(
                            ref.at[index, part],
                            right.at[tile, pl.ds(row, rows), :],
                            piece_sem,
                        )
                    )
                at += 1
        return copies

    def start_rows(tile):
        for index, (ref, part) in enumerate(row_refs):
            row = pl.multiple_of(plan_ref[index], rows)
            column = pl.multiple_of(tile * 2 * TILE_SIZE + part * TILE_SIZE, TILE_SIZE)
            pltpu.make_async_copy(
                ref.at[:, pl.ds(pl.multiple_of(tile * TILE_SIZE, TILE_SIZE), TILE_SIZE)],
                left.at[pl.ds(row, rows), pl.ds(column, TILE_SIZE)],
                row_sem.at[tile],
            ).start()

    for copy in piece_copies():
        copy.start()

    @pl.loop(0, inner_tiles)
    def _(tile):
        start_rows(tile)

    out_ref[...] = jnp.zeros_like(out_ref)
    pltpu.make_async_copy(
        right.at[:, pl.ds(0, 2 * TILE_SIZE), :], right.at[:, pl.ds(0, 2 * TILE_SIZE), :], piece_sem
    ).wait()

    @pl.loop(0, inner_tiles)
    def _(tile):
        columns = pl.ds(pl.multiple_of(tile * 2 * TILE_SIZE, 2 * TILE_SIZE), 2 * TILE_SIZE)
        pltpu.make_async_copy(left.at[:, columns], left.at[:, columns], row_sem.at[tile]).wait()
        right[tile, 2 * TILE_SIZE :, :] = -right[tile, :TILE_SIZE, :]

        @pl.loop(0, out_tiles)
        def _(out_tile):
            @pl.when(used_ref[out_tile, tile] == 1)
            def _():
                span = pl.ds(pl.multiple_of(out_tile * TILE_SIZE, TILE_SIZE), TILE_SIZE)
                lhs = left[span, columns]
                for part in range(2):
                    rhs = right[tile, pl.ds((1 - part) * TILE_SIZE, 2 * TILE_SIZE), :]
                    out_ref[part, span, :] += jnp.dot(lhs, rhs, preferred_element_type=jnp.float32)


def product(row_buffers, row_starts, pieces, piece_starts, used, span, total):
    rows = row_buffers[0][0].shape[0]
    parts = [part for _, part in row_buffers]
    arrays = [array for array, _ in row_buffers] + list(pieces)
    plan = jnp.stack(row_starts + piece_starts).astype(jnp.int32)

    def kernel(plan_ref, used_ref, *refs):
        ins = refs[: len(arrays)]
        row_refs = list(zip(ins[: len(parts)], parts))
        product_kernel(
            rows, plan_ref, used_ref, (row_refs, ins[len(parts) :]), *refs[len(arrays) :]
        )

    inner_tiles = total // TILE_SIZE
    return pl.pallas_call(
        kernel,
        out_shape=jax.ShapeDtypeStruct((2, span, TILE_SIZE), jnp.float32),
        grid_spec=pltpu.PrefetchScalarGridSpec(
            num_scalar_prefetch=2,
            grid=(1,),
            in_specs=[pl.BlockSpec(memory_space=pl.ANY)] * len(arrays),
            out_specs=pl.BlockSpec((2, span, TILE_SIZE), lambda i, *_: (0, 0, 0), pipeline_mode=pl.Buffered(1)),
            scratch_shapes=[
                pltpu.VMEM((span, 2 * total), jnp.bfloat16),
                pltpu.VMEM((inner_tiles, 3 * TILE_SIZE, TILE_SIZE), jnp.bfloat16),
                pltpu.SemaphoreType.DMA((inner_tiles,)),
                pltpu.SemaphoreType.DMA,
            ],
        ),
        compiler_params=pltpu.CompilerParams(vmem_limit_bytes=67_000_000),
    )(plan, used, *arrays)


def cut_kernel(device_ref, place_ref, *refs):
    ins, out_ref = refs[:-1], refs[-1]
    blocks, parts = out_ref.shape[:2]
    for block in range(blocks):
        *planes, gain = ins[(parts + 1) * block : (parts + 1) * (block + 1)]
        for part, ref in enumerate(planes):
            out_ref[block, part] = (ref[...].astype(jnp.float32) * gain[...]).astype(jnp.bfloat16)


def cut(blocks, column, gains, device, parts=(0, 1)):
    rows = blocks[0][0][0].shape[0]
    place = np.stack([column] + [first for _, first in blocks], axis=1).astype(np.int32)
    specs, operands = [], []
    for index, (planes, _) in enumerate(blocks):
        spec = pl.BlockSpec((rows, TILE_SIZE), lambda i, me, place: (0, place[me[0], 0]))
        specs += [spec] * len(parts)
        specs.append(
            pl.BlockSpec((None, rows, 1), lambda i, me, place, at=index + 1: (place[me[0], at], 0, 0))
        )
        operands += [*(planes[part] for part in parts), gains]
    shape = (len(blocks), len(parts), rows, TILE_SIZE)
    return pl.pallas_call(
        cut_kernel,
        out_shape=jax.ShapeDtypeStruct(shape, jnp.bfloat16),
        grid_spec=pltpu.PrefetchScalarGridSpec(
            num_scalar_prefetch=2,
            grid=(1,),
            in_specs=specs,
            out_specs=pl.BlockSpec(shape, lambda i, me, place: (0, 0, 0, 0)),
        ),
    )(device, jnp.asarray(place), *operands)


class Job:
    def __init__(self, row_blocks, columns, absent=(), choice=None, pack=(), packed=(), splits=()):
        self.row_blocks, self.columns, self.absent = row_blocks, columns, list(absent)
        self.choice, self.pack, self.packed = choice, list(pack), list(packed)
        self.planes, self.plane_bands = [], []
        for plane in [] if packed else [p for planes, _ in row_blocks for p in planes]:
            self.plane_bands.append([])
            row = 0
            for array in plane if isinstance(plane, tuple) else (plane,):
                self.plane_bands[-1].append((len(self.planes), row, array.shape[0]))
                self.planes.append(array)
                row += array.shape[0]
        self.sources, self.source_at = [], []
        for pieces, *_ in columns:
            apart = isinstance(pieces, tuple)
            spots = []
            for part, array in enumerate(pieces if apart else (pieces, pieces)):
                if not any(array is source for source in self.sources):
                    self.sources.append(array)
                spots.append(([array is source for source in self.sources].index(True), 0 if apart else part))
            self.source_at.append(spots)
        self.rows = self.sources[0].shape[2]
        self.count = len(row_blocks)
        self.chunks = 1 if packed else 1 + max(column[3] for column in columns)
        bounds = [0, *splits, self.count]
        self.turns = list(zip(bounds[:-1], bounds[1:]))

    def numbers(self):
        listed = [first for _, first in self.row_blocks] + [column[2] for column in self.columns]
        listed += [first for first, _ in self.absent + self.pack]
        return listed + ([] if self.choice is None else [self.choice])

    def operands(self):
        return self.planes + self.sources + [array for array, _ in self.packed]

    def depth(self, total):
        return len(self.columns) * self.rows if self.packed else total

    def scratch(self, total):
        height, depth = self.count * self.rows, self.depth(total)
        shapes = [
            pltpu.VMEM((self.chunks, 2, height, depth // self.chunks), jnp.bfloat16),
            pltpu.VMEM((self.chunks, 2, depth // self.chunks, TILE_SIZE), jnp.bfloat16),
            pltpu.VMEM((2, height, TILE_SIZE), jnp.float32),
            pltpu.SemaphoreType.DMA((len(self.turns), self.chunks)),
            pltpu.SemaphoreType.DMA((self.chunks,)),
            pltpu.SemaphoreType.DMA((len(self.turns) + 1,)),
        ]
        if self.pack:
            shapes.append(pltpu.VMEM((2, height, len(self.pack) * self.rows), jnp.bfloat16))
            shapes.append(pltpu.SemaphoreType.DMA)
        return shapes

    def bind(self, number, used_ref, refs, out_ref, pack_ref, scratch, total):
        self.number, self.used_ref, self.out_ref, self.pack_ref = number, used_ref, out_ref, pack_ref
        self.plane_refs = refs[: len(self.planes)]
        self.source_refs = refs[len(self.planes) : len(self.planes) + len(self.sources)]
        self.packed_refs = refs[len(self.planes) + len(self.sources) :]
        self.left, self.right, self.held, self.left_sem, self.right_sem, self.held_sem = scratch[:6]
        self.packing = scratch[6:]
        self.chunk_depth = self.depth(total) // self.chunks
        self.members = [
            [at for at, column in enumerate(self.columns) if self.packed or column[3] == chunk]
            for chunk in range(self.chunks)
        ]

    def first_of(self, at):
        return pl.multiple_of(self.number(at), self.rows)

    def start_row(self, chunk):
        return self.number(self.count + self.members[chunk][0]) // self.chunk_depth * self.chunk_depth

    def within(self, at):
        return pl.multiple_of(self.number(at) % self.chunk_depth, self.rows)

    def held_copy(self, block, part, out, sem):
        here = self.held.at[part, pl.ds(block * self.rows, self.rows), :]
        there = self.out_ref.at[part, pl.ds(self.first_of(block), self.rows), :]
        return pltpu.make_async_copy(*((here, there) if out else (there, here)), sem)

    def start_right(self, chunk):
        for at in self.members[chunk]:
            row = at * self.rows if self.packed else self.within(self.count + at)
            for part in range(2):
                source, part_at = self.source_at[at][part]
                pltpu.make_async_copy(
                    self.source_refs[source].at[self.columns[at][1], part_at],
                    self.right.at[chunk, part, pl.ds(row, self.rows), :],
                    self.right_sem.at[chunk],
                ).start()

    def start_left(self, turn, chunk):
        sem = self.left_sem.at[turn, chunk]
        first, end = self.turns[turn]
        rows, base = self.rows, 0
        for ref, (_, blocks) in zip(self.packed_refs, self.packed):
            low, high = max(first, base), min(end, base + blocks)
            if low < high:
                pltpu.make_async_copy(
                    ref.at[:, pl.ds((low - base) * rows, (high - low) * rows), :],
                    self.left.at[chunk, :, pl.ds(low * rows, (high - low) * rows), :],
                    sem,
                ).start()
            base += blocks
        if self.packed:
            return
        inner = pl.ds(pl.multiple_of(self.start_row(chunk), self.chunk_depth), self.chunk_depth)
        for block in range(first, end):
            for part in range(2):
                candidates = 1 if self.choice is None else len(self.plane_bands) // 2
                for at in range(candidates):
                    for index, row, size in self.plane_bands[2 * (block + at) + part]:
                        copy = pltpu.make_async_copy(
                            self.plane_refs[index].at[:, inner],
                            self.left.at[chunk, part, pl.ds(block * rows + row, size), :],
                            sem,
                        )
                        if self.choice is None:
                            copy.start()
                        else:
                            pl.when(self.number(len(self.numbers()) - 1) == at)(copy.start)

    def steps(self):
        return [(self, turn, chunk) for turn in range(len(self.turns)) for chunk in range(self.chunks)]

    def start(self, turn, chunk):
        if turn == 0:
            self.start_right(chunk)
        self.start_left(turn, chunk)
        if self.packed:
            for block in range(*self.turns[turn]):
                for part in range(2):
                    self.held_copy(block, part, False, self.held_sem.at[turn]).start()

    def clear_absent(self, chunk):
        for at, (_, owner) in enumerate(self.absent):
            if owner == chunk:
                row = self.within(self.count + len(self.columns) + at)
                self.right[chunk, :, pl.ds(row, self.rows), :] = jnp.zeros(
                    (2, self.rows, TILE_SIZE), jnp.bfloat16
                )

    def wait(self, turn, chunk):
        first, end = self.turns[turn]
        height = (end - first) * self.rows
        views = [(self.left.at[chunk, :, pl.ds(0, height), :], self.left_sem.at[turn, chunk])]
        if turn == 0:
            rows = len(self.members[chunk]) * self.rows
            views.append((self.right.at[chunk, :, pl.ds(0, rows), :], self.right_sem.at[chunk]))
        if self.packed:
            views.append((self.held.at[:, pl.ds(0, height), :], self.held_sem.at[turn]))
        for view, sem in views:
            pltpu.make_async_copy(view, view, sem).wait()

    def mask(self, chunk, first, end):
        rows = self.rows
        for block in range(first, end):
            own_tile = self.number(block) // TILE_SIZE
            for offset in range(0, self.chunk_depth, TILE_SIZE):
                tile = (self.start_row(chunk) + offset) // TILE_SIZE

                @pl.when(self.used_ref[own_tile, tile] == 0)
                def _():
                    self.left[
                        chunk, :, block * rows : (block + 1) * rows, offset : offset + TILE_SIZE
                    ] = jnp.zeros((2, rows, TILE_SIZE), jnp.bfloat16)

    def write_packed(self, chunk, first, end):
        rows, (packing, sem) = self.rows, self.packing
        pack_at = self.count + len(self.columns) + len(self.absent)
        band = slice(first * rows, end * rows)
        for at, (_, owner) in enumerate(self.pack):
            if owner == chunk:
                to = slice(at * rows, (at + 1) * rows)
                packing[:, band, to] = self.left[chunk, :, band, pl.ds(self.within(pack_at + at), rows)]
                area = (slice(None), pl.ds(first * rows, (end - first) * rows), pl.ds(at * rows, rows))
                pltpu.make_async_copy(packing.at[area], self.pack_ref.at[area], sem).start()

    def products(self, chunk, band):
        by_part = ((0, 0, 1, 1), (0, 1, 1, 0))
        out = []
        for part, (a, b, c, d) in enumerate(by_part):
            first = jnp.dot(
                self.left[chunk, a, band], self.right[chunk, b], preferred_element_type=jnp.float32
            )
            second = jnp.dot(
                self.left[chunk, c, band], self.right[chunk, d], preferred_element_type=jnp.float32
            )
            out.append(first + second if part else first - second)
        return out

    def run(self, turn, chunk):
        rows, held = self.rows, self.held
        first, end = self.turns[turn]
        band = slice(first * rows, end * rows)
        if not self.packed:
            self.mask(chunk, first, end)
            if turn == 0:
                self.clear_absent(chunk)
        if self.pack:
            self.write_packed(chunk, first, end)
        sums = self.products(chunk, band)
        for part in range(2):
            if chunk == 0 and not self.packed:
                held[part, band] = sums[part]
            else:
                held[part, band] += sums[part]
            if chunk == self.chunks - 1:
                for block in range(first, end):
                    self.held_copy(block, part, True, self.held_sem.at[len(self.turns)]).start()

    def finish(self):
        if self.pack:
            pltpu.make_async_copy(self.packing[0], self.pack_ref, self.packing[1]).wait()
        pltpu.make_async_copy(self.held, self.held, self.held_sem.at[len(self.turns)]).wait()


def launch(device, base, jobs, used, span, total):
    plan = np.stack([n for job in jobs for n in job.numbers()], axis=1).astype(np.int32)
    operands = [array for job in jobs for array in job.operands()]
    operands += [] if base is None else [base]
    packing = [job for job in jobs if job.pack]
    scratch = [job.scratch(total) for job in jobs]
    out_shape = [jax.ShapeDtypeStruct((2, span, TILE_SIZE), jnp.float32)]
    for job in packing:
        shape = (2, job.count * job.rows, len(job.pack) * job.rows)
        out_shape.append(jax.ShapeDtypeStruct(shape, jnp.bfloat16))

    def kernel(device_ref, plan_ref, used_ref, *refs):
        outs = refs[len(operands) : len(operands) + len(out_shape)]
        spare = refs[len(operands) + len(out_shape) :]
        at, spare_at, plan_at = 0, 0, 0
        for job, shapes in zip(jobs, scratch):
            size = len(job.operands())
            job.bind(
                lambda n, plan_at=plan_at: plan_ref[device_ref[0], plan_at + n],
                used_ref,
                refs[at : at + size],
                outs[0],
                outs[1 + packing.index(job)] if job.pack else None,
                spare[spare_at : spare_at + len(shapes)],
                total,
            )
            at, spare_at, plan_at = at + size, spare_at + len(shapes), plan_at + len(job.numbers())
        steps = [step for job in jobs for step in job.steps()]
        for job, *step in steps[:AHEAD]:
            job.start(*step)
        for at, (job, *step) in enumerate(steps):
            job.wait(*step)
            for later, *later_step in steps[at + AHEAD : at + AHEAD + 1]:
                later.start(*later_step)
            job.run(*step)
        for job in jobs:
            job.finish()

    flops = sum(8 * job.count * job.rows * job.depth(total) * TILE_SIZE for job in jobs)
    return pl.pallas_call(
        kernel,
        out_shape=out_shape,
        grid_spec=pltpu.PrefetchScalarGridSpec(
            num_scalar_prefetch=3,
            grid=(1,),
            in_specs=[pl.BlockSpec(memory_space=pl.ANY)] * len(operands),
            out_specs=[pl.BlockSpec(memory_space=pl.ANY)] * len(out_shape),
            scratch_shapes=[shape for shapes in scratch for shape in shapes],
        ),
        input_output_aliases={} if base is None else {3 + len(operands) - 1: 0},
        cost_estimate=pl.CostEstimate(flops=flops, bytes_accessed=20 * span * total, transcendentals=0),
        compiler_params=pltpu.CompilerParams(vmem_limit_bytes=60 * 1024 * 1024),
    )(device, jnp.asarray(plan), used, *operands)


def used_tiles(aperture, lengths, rcv_index, total):
    lists = lax.dynamic_index_in_dim(aperture, rcv_index, 1, keepdims=False)
    slot = jnp.arange(lists.shape[1], dtype=jnp.int32)
    wanted = (slot[None, :] < lengths)[:, :, None]
    tiles = jnp.arange(total // TILE_SIZE, dtype=jnp.int32)
    return jnp.any(wanted & (lists[:, :, None] == tiles), axis=1).astype(jnp.int32)


def local(data, fill_mask, obliquity, aperture, lengths):
    _, rows, total = data.shape
    src_count = lax.axis_size("src")
    rcv_count = lax.axis_size("rcv")
    src_index = lax.axis_index("src")
    rcv_index = lax.axis_index("rcv")
    devices = src_count * rcv_count
    span = rows * rcv_count
    device = (src_index * rcv_count + rcv_index).reshape(1)
    phased = rows % 128 == 0 and rcv_count % 4 == 0 and rcv_count > 4

    order = ring_order(rcv_count)
    owner, mine = np.divmod(np.arange(devices), rcv_count)
    place = np.asarray([order.index(i) for i in range(rcv_count)])[mine]
    half = rcv_count // 2
    steps = (rcv_count - 1) // 2

    def origin(offset):
        return np.asarray(order)[(place + offset) % rcv_count]

    def here(numbers):
        return jnp.asarray(numbers, jnp.int32)[device[0]]

    forward = [(order[i], order[(i + 1) % rcv_count]) for i in range(rcv_count)]
    backward = [(b, a) for a, b in forward]

    def hop(planes, pairs):
        return tuple(lax.ppermute(p, "rcv", pairs) for p in planes)

    used = used_tiles(aperture, lengths, rcv_index, total)
    my_gains = -lax.dynamic_slice_in_dim(obliquity, src_index * span, span)
    gains = my_gains.reshape(rcv_count, rows, 1)

    def tiles_of(blocks, column):
        if phased:
            return cut(blocks, column, gains, device)
        out = []
        for planes, first in blocks:
            start = here(column) * TILE_SIZE
            cuts = [lax.dynamic_slice_in_dim(p, start, TILE_SIZE, 1) for p in planes]
            gain = lax.dynamic_index_in_dim(gains, here(first), 0, keepdims=True)
            out.append((jnp.stack(cuts).astype(jnp.float32) * gain).astype(jnp.bfloat16))
        return jnp.stack(out)

    columns = []

    def exchange(held):
        held_by = [(held, 0)]
        bit = src_count // 2
        while bit:
            swap = [(i, i ^ bit) for i in range(src_count)]
            held_by += [(lax.ppermute(x, "src", swap), mask ^ bit) for x, mask in held_by]
            bit //= 2
        return held_by

    def note(held_by, origins):
        for pieces, mask in held_by:
            for index, first in enumerate(origins):
                columns.append((pieces, index, (owner ^ mask) * span + first * rows, mask))

    def collect(blocks):
        tiles = tiles_of(blocks, mine)
        note(exchange(tiles), [first for _, first in blocks])

    def collect_apart(blocks):
        by_part = []
        for part in range(2):
            tiles = cut(blocks, mine, gains, device, (part,))
            by_part.append(exchange(tiles))
        pairs = [((first, second), mask) for (first, mask), (second, _) in zip(*by_part)]
        note(pairs, [first for _, first in blocks])

    blocks = transposed_blocks(data, devices)
    arrived = [
        lax.all_to_all(b, ("src", "rcv"), split_axis=0, concat_axis=0, tiled=True) for b in blocks
    ]
    own, ahead, behind = [], [], []
    for part in range(2):
        own.append(fill(data, fill_mask, arrived[part], part))
        ahead.append(lax.ppermute(own[part], "rcv", forward))
        behind.append(lax.ppermute(own[part], "rcv", backward))

    rows_of = {0: (own, origin(0)), -1: (ahead, origin(-1)), 1: (behind, origin(1))}
    far = origin(half)
    if not phased:
        collect([rows_of[0]])
        collect([rows_of[-1], rows_of[1]])
        for step in range(2, steps + 1):
            ahead, behind = hop(ahead, forward), hop(behind, backward)
            rows_of[-step], rows_of[step] = (ahead, origin(-step)), (behind, origin(step))
            collect([rows_of[-step], rows_of[step]])
        if rcv_count % 2 == 0:
            last = hop(ahead[:1], forward) + hop(behind[1:], backward)
            rows_of[half] = (last, far)
            collect([rows_of[half]])
        row_buffers, row_starts, pieces, starts = [], [], [], []
        for planes, first in rows_of.values():
            row_buffers += [(planes[0], 0), (planes[1], 1)]
            row_starts += [here(first * rows)] * 2
        for array, index, first, _ in columns:
            if index == 0:
                pieces.append(array)
            starts.append(here(first))
        return product(row_buffers, row_starts, pieces, starts, used, span, total)

    quarter = rcv_count // 4
    near = [quarter - 1, quarter, rcv_count - 1 - quarter, rcv_count - quarter]

    def from_mate(offset):
        pairs = []
        for i in near:
            mate = rcv_count - 1 - i
            if (mate + offset) % rcv_count == (i + half) % rcv_count:
                pairs.append((order[mate], order[i]))
        return pairs

    collect([rows_of[0]])
    inside = [0] + [o for step in range(1, steps) for o in (-step, step)]
    outside = [-steps, steps]

    def as_rows(offsets):
        return [(rows_of[o][0], rows_of[o][1] * rows) for o in offsets]

    for step in range(2, steps + 1):
        collect([rows_of[1 - step], rows_of[step - 1]])
        moved = []
        for part in range(2):
            moved.append(lax.ppermute(ahead[part], "rcv", forward))
            moved.append(lax.ppermute(behind[part], "rcv", backward))
        ahead, behind = moved[0::2], moved[1::2]
        rows_of[-step], rows_of[step] = (ahead, origin(-step)), (behind, origin(step))
    taken = [hop(rows_of[offset][0], from_mate(offset)) for offset in (-1, 1)]
    late_from = len(columns)
    collect_apart([rows_of[-steps], rows_of[steps]])
    across = [(order[i], order[(i + half) % rcv_count]) for i in range(rcv_count)]
    far_pieces = cut([(own, origin(0))], far, gains, device)
    far_pieces = lax.ppermute(far_pieces, "rcv", across)
    note(exchange(far_pieces), [far])
    early, late = columns[:late_from], columns[late_from:]
    absent = pack = [(c[2], c[3]) for c in late]
    jobs = [Job(as_rows(inside), early, absent, pack=pack)]
    out, packed_inside = launch(device, None, jobs, used, span, total)
    turns = [
        [(order[(i + d) % rcv_count], order[i]) for i in range(rcv_count) if i not in near]
        for d in (-1, 1)
    ]
    last = []
    for part in range(2):
        upper = lax.ppermute(ahead[part][: rows // 2], "rcv", turns[0])
        lower = lax.ppermute(behind[part][rows // 2 :], "rcv", turns[1])
        last.append((upper, lower))
    jobs = [Job(as_rows(outside), early, absent, pack=pack)]
    out, packed_outside = launch(device, out, jobs, used, span, total)
    chosen = np.zeros(devices)
    for number, offset in enumerate((-1, 1), start=1):
        for _, target in from_mate(offset):
            chosen[mine == target] = number
    candidates = (*last, *taken[0], *taken[1])
    packed = [(packed_inside, len(inside)), (packed_outside, len(outside))]
    splits = [len(inside) // 2, len(inside)]
    jobs = [Job(as_rows(inside + outside), late, packed=packed, splits=splits)]
    out = launch(device, out, jobs, used, span, total)[0]
    jobs = [Job([(candidates, far * rows)], columns, choice=chosen)]
    return launch(device, out, jobs, used, span, total)[0]


def solution(mesh):
    placed = (
        P(None, ("src", "rcv"), None),
        P(("src", "rcv"), None),
        P(),
        P("src", None, None),
        P("src", "rcv"),
    )

    return jax.shard_map(
        local, mesh=mesh, in_specs=placed, out_specs=P(None, "src", "rcv"), check_vma=False
    )
```

profile of v0, /device:TPU:0, one launch (start us, length us, event | category | flops | bytes accessed | tf_op | source)
XLA Modules:
  0.0 314.5 jit_solution(2715292027974247480)
XLA Ops:
  0.0 4.0 %shard_map.148 = (bf16[32,128,128]{2,1,0:T(8,128)(2,1)}, bf16[32,128,128]{2,1,0:T(8,128)(2,1)}) custom-call(bf16[2,128,4096]{2,1,0:T(8,128)(2,1)} %data_ref.5), custom_call_target="tpu_custom_call" | custom-call | tf_op jit(solution)/shard_map/pallas_call | solution.py:30
  4.0 34.9 %all_to_all.10.arrived_ref = bf16[32,128,128]{2,1,0:T(8,128)(2,1)} all-to-all(bf16[32,128,128]{2,1,0:T(8,128)(2,1)} %get-tuple-element.11), channel_id=1, replica_groups=mesh['src'=4,'rcv'=8] {'src','rcv'}, dimensions={0} | all-to-all | bytes 2097152 | tf_op jit(solution)/shard_map/all_to_all | solution.py:552
  38.9 2.6 all-to-all-start.1
  41.6 4.1 %shard_map.149.refs_0_ = bf16[128,4096]{1,0:T(8,128)(2,1)} custom-call(bf16[2,128,4096]{2,1,0:T(8,128)(2,1)} %data_ref.5, s32[128,4096]{1,0:T(8,128)} %mask_ref.3, bf16[32,128,128]{2,1,0:T(8,128)(2,1)} %all_to_all.10.arrived_ref), custom_call_target="tpu_custom_call" | custom-call | tf_op jit(solution)/shard_map/pallas_call | solution.py:55
  47.3 21.7 %all-to-all-done.1.arrived_ref = bf16[32,128,128]{2,1,0:T(8,128)(2,1)S(1)} async-done(((bf16[32,128,128]{2,1,0:T(8,128)(2,1)}), bf16[32,128,128]{2,1,0:T(8,128)(2,1)S(1)}, u32[]{:S(2)}, u32[]{:S(2)}) %all-to-all-start.1) | async-done | bytes 1048608 | tf_op jit(solution)/shard_map/all_to_all | solution.py:552
  70.0 4.1 %shard_map.150.refs_1_ = bf16[128,4096]{1,0:T(8,128)(2,1)} custom-call(bf16[2,128,4096]{2,1,0:T(8,128)(2,1)} %data_ref.5, s32[128,4096]{1,0:T(8,128)} %mask_ref.3, bf16[32,128,128]{2,1,0:T(8,128)(2,1)} %copy-done.2), custom_call_target="tpu_custom_call" | custom-call | tf_op jit(solution)/shard_map/pallas_call | solution.py:55
  78.6 2.7 shard_map.151.refs_10_.refs_4_.refs_8_
  81.9 7.2 %collective-permute-done.20.refs_11_.refs_5_.refs_9_ = bf16[1,2,128,512]{3,2,1,0:T(8,128)(2,1)S(1)} collective-permute-done((bf16[1,2,128,512]{3,2,1,0:T(8,128)(2,1)}, bf16[1,2,128,512]{3,2,1,0:T(8,128)(2,1)S(1)}, u32[]{:S(2)}, u32[]{:S(2)}) %collective-permute-start.20) | collective-permute-done | bytes 262176 | tf_op jit(solution)/shard_map/ppermute | solution.py:529
  89.1 2.7 shard_map.156
  93.5 6.9 %collective-permute-done.12.refs_4_.refs_5_ = bf16[128,4096]{1,0:T(8,128)(2,1)S(1)} collective-permute-done((bf16[128,4096]{1,0:T(8,128)(2,1)}, bf16[128,4096]{1,0:T(8,128)(2,1)S(1)}, u32[]{:S(2)}, u32[]{:S(2)}) %collective-permute-start.12) | collective-permute-done | bytes 1048608 | tf_op jit(solution)/shard_map/ppermute | solution.py:558
  101.1 27.3 %collective-permute-done.4.refs_3_.refs_4_ = bf16[128,4096]{1,0:T(8,128)(2,1)S(1)} collective-permute-done((bf16[128,4096]{1,0:T(8,128)(2,1)S(1)}, bf16[128,4096]{1,0:T(8,128)(2,1)S(1)}, u32[]{:S(2)}, u32[]{:S(2)}) %collective-permute-start.4) | collective-permute-done | bytes 1048608 | tf_op jit(solution)/shard_map/ppermute | solution.py:558
  130.9 3.0 shard_map.152.refs_14_.refs_8_.refs_12_
  133.9 3.5 %collective-permute-done.36.refs_9_.refs_29_ = bf16[1,2,128,512]{3,2,1,0:T(8,128)(2,1)} collective-permute-done((bf16[1,2,128,512]{3,2,1,0:T(8,128)(2,1)}, bf16[1,2,128,512]{3,2,1,0:T(8,128)(2,1)}, u32[]{:S(2)}, u32[]{:S(2)}) %collective-permute-start.36) | collective-permute-done | bytes 262176 | tf_op jit(solution)/shard_map/ppermute | solution.py:529
  139.2 11.3 %collective-permute-done.23.refs_15_.refs_9_.refs_13_ = bf16[2,2,128,512]{3,2,1,0:T(8,128)(2,1)} collective-permute-done((bf16[2,2,128,512]{3,2,1,0:T(8,128)(2,1)}, bf16[2,2,128,512]{3,2,1,0:T(8,128)(2,1)}, u32[]{:S(2)}, u32[]{:S(2)}) %collective-permute-start.23) | collective-permute-done | bytes 524320 | tf_op jit(solution)/shard_map/ppermute | solution.py:529
  151.0 21.5 %collective-permute-done.5.refs_3_.refs_8_ = bf16[128,4096]{1,0:T(8,128)(2,1)S(1)} collective-permute-done((bf16[128,4096]{1,0:T(8,128)(2,1)S(1)}, bf16[128,4096]{1,0:T(8,128)(2,1)S(1)}, u32[]{:S(2)}, u32[]{:S(2)}) %collective-permute-start.5) | collective-permute-done | bytes 1048608 | tf_op jit(solution)/shard_map/ppermute | solution.py:606
  173.5 3.0 shard_map.153.refs_18_.refs_12_.refs_16_
  177.9 5.5 %collective-permute-start.10 = (bf16[128,4096]{1,0:T(8,128)(2,1)}, bf16[128,4096]{1,0:T(8,128)(2,1)S(1)}, u32[]{:S(2)}, u32[]{:S(2)}) collective-permute-start(bf16[128,4096]{1,0:T(8,128)(2,1)} %collective-permute-done.9.refs_1_.refs_7_), channel_id=1, source_target_pairs={{0,2},{2,4},{4,6},{6,7},{7,5},{5,3},{3,1},{1,0},{8,10},{10,12},{12... | collective-permute-start | bytes 3145736 | tf_op jit(solution)/shard_map/ppermute | solution.py:605
  183.4 2.0 collective-permute-start.2
  185.5 4.9 %collective-permute-done.26.refs_19_.refs_13_.refs_17_ = bf16[2,2,128,512]{3,2,1,0:T(8,128)(2,1)} collective-permute-done((bf16[2,2,128,512]{3,2,1,0:T(8,128)(2,1)}, bf16[2,2,128,512]{3,2,1,0:T(8,128)(2,1)}, u32[]{:S(2)}, u32[]{:S(2)}) %collective-permute-start.26) | collective-permute-done | bytes 524320 | tf_op jit(solution)/shard_map/ppermute | solution.py:529
  192.1 15.2 %collective-permute-done.10.refs_0_.refs_1_ = bf16[128,4096]{1,0:T(8,128)(2,1)S(1)} collective-permute-done((bf16[128,4096]{1,0:T(8,128)(2,1)}, bf16[128,4096]{1,0:T(8,128)(2,1)S(1)}, u32[]{:S(2)}, u32[]{:S(2)}) %collective-permute-start.10) | collective-permute-done | bytes 1048608 | tf_op jit(solution)/shard_map/ppermute | solution.py:605
  207.2 2.4 collective-permute-done.14.refs_2_.refs_3_
  209.7 18.4 %collective-permute-done.2.refs_0_ = bf16[128,4096]{1,0:T(8,128)(2,1)S(1)} collective-permute-done((bf16[128,4096]{1,0:T(8,128)(2,1)}, bf16[128,4096]{1,0:T(8,128)(2,1)S(1)}, u32[]{:S(2)}, u32[]{:S(2)}) %collective-permute-start.2) | collective-permute-done | bytes 1048608 | tf_op jit(solution)/shard_map/ppermute | solution.py:605
  232.6 2.7 shard_map.154.refs_0_.refs_20_
  235.4 2.7 shard_map.155.refs_1_.refs_21_
  242.0 18.4 %shard_map.157 = (f32[2,1024,512]{2,1,0:T(8,128)}, bf16[2,640,1536]{2,1,0:T(8,128)(2,1)}) custom-call(s32[1]{0:T(128)} %bitcast.device_ref, s32[32,49]{1,0:T(8,128)} %constant.45.clone.plan_ref, s32[2,8]{1,0:T(2,128)} %convert_element_type.3.used_ref, bf16[128,4096]{1,0:T(8,128)(2,1)} %shard_map.149.refs_0_, bf16[128,4096]{1,0:T(8,128)(2,1)} %shard_map.150.refs_1_, ...), custom_call_target="tpu_custom_call" | custom-call | flops 10737418240 | bytes 83886080 | tf_op jit(solution)/shard_map/pallas_call | solution.py:454
  264.3 9.3 %shard_map.158 = (f32[2,1024,512]{2,1,0:T(8,128)}, bf16[2,256,1536]{2,1,0:T(8,128)(2,1)}) custom-call(s32[1]{0:T(128)} %bitcast.device_ref, s32[32,46]{1,0:T(8,128)} %constant.46.clone.plan_ref, s32[2,8]{1,0:T(2,128)} %convert_element_type.3.used_ref, bf16[128,4096]{1,0:T(8,128)(2,1)} %copy-done.7, ...), custom_call_target="tpu_custom_call", output_to_operand_aliasing={{0}: (19, {})} | custom-call | flops 4294967296 | bytes 83886080 | tf_op jit(solution)/shard_map/pallas_call | solution.py:454
  275.0 4.5 %collective-permute-start.15 = (bf16[64,4096]{1,0:T(8,128)(2,1)}, bf16[64,4096]{1,0:T(8,128)(2,1)S(1)}, u32[]{:S(2)}, u32[]{:S(2)}) collective-permute-start(bf16[64,4096]{1,0:T(8,128)(2,1)} %slice.19), channel_id=1, source_target_pairs={{2,0},{7,6},{5,7},{0,1},{10,8},{15,14},{13,15},{8,9},{18,16},{23,2... | collective-permute-start | bytes 1572872 | tf_op jit(solution)/shard_map/ppermute | solution.py:627
  280.9 4.6 %collective-permute-start.7 = (bf16[64,4096]{1,0:T(8,128)(2,1)S(1)}, bf16[64,4096]{1,0:T(8,128)(2,1)S(1)}, u32[]{:S(2)}, u32[]{:S(2)}) collective-permute-start(bf16[64,4096]{1,0:T(8,128)(2,1)S(1)} %slice.17), channel_id=1, source_target_pairs={{2,0},{7,6},{5,7},{0,1},{10,8},{15,14},{13,15},{8,9},{18,16},{23,2... | collective-permute-start | bytes 1572872 | tf_op jit(solution)/shard_map/ppermute | solution.py:627
  285.5 11.1 %shard_map.159.refs_32_ = f32[2,1024,512]{2,1,0:T(8,128)} custom-call(s32[1]{0:T(128)} %bitcast.device_ref, s32[32,19]{1,0:T(8,128)} %constant.47.clone.plan_ref, s32[2,8]{1,0:T(2,128)} %convert_element_type.3.used_ref, bf16[2,1,128,512]{3,2,1,0:T(8,128)(2,1)} %shard_map.154.refs_0_.refs_20_, ...), custom_call_target="tpu_custom_call", output_to_operand_aliasing={{}: (17, {})} | custom-call | flops 5637144576 | bytes 83886080 | tf_op jit(solution)/shard_map/pallas_call | solution.py:454
  296.6 4.4 %collective-permute-done.3.refs_0_ = bf16[64,4096]{1,0:T(8,128)(2,1)S(1)} collective-permute-done((bf16[64,4096]{1,0:T(8,128)(2,1)S(1)}, bf16[64,4096]{1,0:T(8,128)(2,1)S(1)}, u32[]{:S(2)}, u32[]{:S(2)}) %collective-permute-start.3) | collective-permute-done | bytes 524320 | tf_op jit(solution)/shard_map/ppermute | solution.py:626
  301.0 5.5 %collective-permute-done.7.refs_1_ = bf16[64,4096]{1,0:T(8,128)(2,1)S(1)} collective-permute-done((bf16[64,4096]{1,0:T(8,128)(2,1)S(1)}, bf16[64,4096]{1,0:T(8,128)(2,1)S(1)}, u32[]{:S(2)}, u32[]{:S(2)}) %collective-permute-start.7) | collective-permute-done | bytes 524320 | tf_op jit(solution)/shard_map/ppermute | solution.py:627
  307.3 7.0 %shard_map.160 = f32[2,1024,512]{2,1,0:T(8,128)} custom-call(s32[1]{0:T(128)} %bitcast.device_ref, s32[32,34]{1,0:T(8,128)} %constant.48.clone.plan_ref, s32[2,8]{1,0:T(2,128)} %convert_element_type.3.used_ref, bf16[64,4096]{1,0:T(8,128)(2,1)} %copy-done.16, bf16[64,4096]{1,0:T(8,128)(2,1)} %copy-done.17, ...), custom_call_target="tpu_custom_call", output_to_operand_aliasing={{}: (35, {})} | custom-call | flops 2147483648 | bytes 83886080 | tf_op jit(solution)/shard_map/pallas_call | solution.py:454
  (114 shorter events, 34.8 us)
Async XLA Ops:
  38.9 30.1 %all-to-all-start.1 = ((bf16[32,128,128]{2,1,0:T(8,128)(2,1)}), bf16[32,128,128]{2,1,0:T(8,128)(2,1)S(1)}, u32[]{:S(2)}, u32[]{:S(2)}) async-start(bf16[32,128,128]{2,1,0:T(8,128)(2,1)} %get-tuple-element.12), calls=%async_computation.1 | async-start | bytes 2097152 | tf_op jit(solution)/shard_map/all_to_all | solution.py:552
  45.6 47.8 %collective-permute-start = (bf16[128,4096]{1,0:T(8,128)(2,1)}, bf16[128,4096]{1,0:T(8,128)(2,1)}, u32[]{:S(2)}, u32[]{:S(2)}) collective-permute-start(bf16[128,4096]{1,0:T(8,128)(2,1)} %shard_map.149.refs_0_), channel_id=1, source_target_pairs={{0,2},{2,4},{4,6},{6,7},{7,5},{5,3},{3,1},{1,0},{8,10},{10,12},{12... | collective-permute-start | bytes 3145736 | tf_op jit(solution)/shard_map/ppermute | solution.py:557
  74.1 26.2 %collective-permute-start.12 = (bf16[128,4096]{1,0:T(8,128)(2,1)}, bf16[128,4096]{1,0:T(8,128)(2,1)S(1)}, u32[]{:S(2)}, u32[]{:S(2)}) collective-permute-start(bf16[128,4096]{1,0:T(8,128)(2,1)} %shard_map.150.refs_1_), channel_id=1, source_target_pairs={{2,0},{4,2},{6,4},{7,6},{5,7},{3,5},{1,3},{0,1},{10,8},{12,10},{14... | collective-permute-start | bytes 3145736 | tf_op jit(solution)/shard_map/ppermute | solution.py:558
  74.9 53.6 %collective-permute-start.4 = (bf16[128,4096]{1,0:T(8,128)(2,1)S(1)}, bf16[128,4096]{1,0:T(8,128)(2,1)S(1)}, u32[]{:S(2)}, u32[]{:S(2)}) collective-permute-start(bf16[128,4096]{1,0:T(8,128)(2,1)S(1)} %copy-done.1), channel_id=1, source_target_pairs={{2,0},{4,2},{6,4},{7,6},{5,7},{3,5},{1,3},{0,1},{10,8},{12,10},{14... | collective-permute-start | bytes 3145736 | tf_op jit(solution)/shard_map/ppermute | solution.py:558
  74.9 54.3 %collective-permute-start.8 = (bf16[128,4096]{1,0:T(8,128)(2,1)}, bf16[128,4096]{1,0:T(8,128)(2,1)}, u32[]{:S(2)}, u32[]{:S(2)}) collective-permute-start(bf16[128,4096]{1,0:T(8,128)(2,1)} %shard_map.150.refs_1_), channel_id=1, source_target_pairs={{0,2},{2,4},{4,6},{6,7},{7,5},{5,3},{3,1},{1,0},{8,10},{10,12},{12... | collective-permute-start | bytes 3145736 | tf_op jit(solution)/shard_map/ppermute | solution.py:557
  91.8 38.6 %collective-permute-start.35 = (bf16[1,2,128,512]{3,2,1,0:T(8,128)(2,1)}, bf16[1,2,128,512]{3,2,1,0:T(8,128)(2,1)}, u32[]{:S(2)}, u32[]{:S(2)}) collective-permute-start(bf16[1,2,128,512]{3,2,1,0:T(8,128)(2,1)} %shard_map.156), channel_id=1, source_target_pairs={{0,7},{2,5},{4,3},{6,1},{7,0},{5,2},{3,4},{1,6},{8,15},{10,13},{12... | collective-permute-start | bytes 786440 | tf_op jit(solution)/shard_map/ppermute | solution.py:614
  93.5 57.0 %collective-permute-start.1 = (bf16[128,4096]{1,0:T(8,128)(2,1)}, bf16[128,4096]{1,0:T(8,128)(2,1)}, u32[]{:S(2)}, u32[]{:S(2)}) collective-permute-start(bf16[128,4096]{1,0:T(8,128)(2,1)} %collective-permute-done.refs_0_.refs_2_), channel_id=1, source_target_pairs={{0,2},{2,4},{4,6},{6,7},{7,5},{5,3},{3,1},{1,0},{8,10},{10,12},{12... | collective-permute-start | bytes 3145736 | tf_op jit(solution)/shard_map/ppermute | solution.py:605
  100.3 50.7 %collective-permute-start.13 = (bf16[128,4096]{1,0:T(8,128)(2,1)S(1)}, bf16[128,4096]{1,0:T(8,128)(2,1)}, u32[]{:S(2)}, u32[]{:S(2)}) collective-permute-start(bf16[128,4096]{1,0:T(8,128)(2,1)S(1)} %collective-permute-done.12.refs_4_.refs_5_), channel_id=1, source_target_pairs={{2,0},{4,2},{6,4},{7,6},{5,7},{3,5},{1,3},{0,1},{10,8},{12,10},{14... | collective-permute-start | bytes 3145736 | tf_op jit(solution)/shard_map/ppermute | solution.py:606
  128.4 44.1 %collective-permute-start.5 = (bf16[128,4096]{1,0:T(8,128)(2,1)S(1)}, bf16[128,4096]{1,0:T(8,128)(2,1)S(1)}, u32[]{:S(2)}, u32[]{:S(2)}) collective-permute-start(bf16[128,4096]{1,0:T(8,128)(2,1)S(1)} %collective-permute-done.4.refs_3_.refs_4_), channel_id=1, source_target_pairs={{2,0},{4,2},{6,4},{7,6},{5,7},{3,5},{1,3},{0,1},{10,8},{12,10},{14... | collective-permute-start | bytes 3145736 | tf_op jit(solution)/shard_map/ppermute | solution.py:606
  129.2 43.3 %collective-permute-start.9 = (bf16[128,4096]{1,0:T(8,128)(2,1)}, bf16[128,4096]{1,0:T(8,128)(2,1)}, u32[]{:S(2)}, u32[]{:S(2)}) collective-permute-start(bf16[128,4096]{1,0:T(8,128)(2,1)} %collective-permute-done.8.refs_1_.refs_3_), channel_id=1, source_target_pairs={{0,2},{2,4},{4,6},{6,7},{7,5},{5,3},{3,1},{1,0},{8,10},{10,12},{12... | collective-permute-start | bytes 3145736 | tf_op jit(solution)/shard_map/ppermute | solution.py:605
  150.5 26.1 %collective-permute-start.22 = (bf16[1,2,128,512]{3,2,1,0:T(8,128)(2,1)S(1)}, bf16[1,2,128,512]{3,2,1,0:T(8,128)(2,1)}, u32[]{:S(2)}, u32[]{:S(2)}) collective-permute-start(bf16[1,2,128,512]{3,2,1,0:T(8,128)(2,1)S(1)} %collective-permute-done.20.refs_11_.refs_5_.refs_9_), channel_id=1, source_target_pairs={{0,8},{8,0},{16,24},{24,16},{1,9},{9,1},{17,25},{25,17},{2,10},{10... | collective-permute-start | bytes 786440 | tf_op jit(solution)/shard_map/ppermute | solution.py:529
  150.5 27.4 %collective-permute-start.37 = (bf16[1,2,128,512]{3,2,1,0:T(8,128)(2,1)}, bf16[1,2,128,512]{3,2,1,0:T(8,128)(2,1)}, u32[]{:S(2)}, u32[]{:S(2)}) collective-permute-start(bf16[1,2,128,512]{3,2,1,0:T(8,128)(2,1)} %collective-permute-done.35.refs_8_.refs_28_), channel_id=1, source_target_pairs={{0,8},{8,0},{16,24},{24,16},{1,9},{9,1},{17,25},{25,17},{2,10},{10... | collective-permute-start | bytes 786440 | tf_op jit(solution)/shard_map/ppermute | solution.py:529
  151.0 32.4 %collective-permute-start.38 = (bf16[1,2,128,512]{3,2,1,0:T(8,128)(2,1)}, bf16[1,2,128,512]{3,2,1,0:T(8,128)(2,1)}, u32[]{:S(2)}, u32[]{:S(2)}) collective-permute-start(bf16[1,2,128,512]{3,2,1,0:T(8,128)(2,1)} %collective-permute-done.36.refs_9_.refs_29_), channel_id=1, source_target_pairs={{0,8},{8,0},{16,24},{24,16},{1,9},{9,1},{17,25},{25,17},{2,10},{10... | collective-permute-start | bytes 786440 | tf_op jit(solution)/shard_map/ppermute | solution.py:529
  176.5 13.9 %collective-permute-start.26 = (bf16[2,2,128,512]{3,2,1,0:T(8,128)(2,1)}, bf16[2,2,128,512]{3,2,1,0:T(8,128)(2,1)}, u32[]{:S(2)}, u32[]{:S(2)}) collective-permute-start(bf16[2,2,128,512]{3,2,1,0:T(8,128)(2,1)} %shard_map.153.refs_18_.refs_12_.refs_16_), channel_id=1, source_target_pairs={{0,16},{8,24},{16,0},{24,8},{1,17},{9,25},{17,1},{25,9},{2,18},{10... | collective-permute-start | bytes 1572872 | tf_op jit(solution)/shard_map/ppermute | solution.py:529
  177.9 29.3 %collective-permute-start.10 = (bf16[128,4096]{1,0:T(8,128)(2,1)}, bf16[128,4096]{1,0:T(8,128)(2,1)S(1)}, u32[]{:S(2)}, u32[]{:S(2)}) collective-permute-start(bf16[128,4096]{1,0:T(8,128)(2,1)} %collective-permute-done.9.refs_1_.refs_7_), channel_id=1, source_target_pairs={{0,2},{2,4},{4,6},{6,7},{7,5},{5,3},{3,1},{1,0},{8,10},{10,12},{12... | collective-permute-start | bytes 3145736 | tf_op jit(solution)/shard_map/ppermute | solution.py:605
  183.4 26.2 %collective-permute-start.14 = (bf16[128,4096]{1,0:T(8,128)(2,1)}, bf16[128,4096]{1,0:T(8,128)(2,1)S(1)}, u32[]{:S(2)}, u32[]{:S(2)}) collective-permute-start(bf16[128,4096]{1,0:T(8,128)(2,1)} %collective-permute-done.13.refs_4_.refs_9_), channel_id=1, source_target_pairs={{2,0},{4,2},{6,4},{7,6},{5,7},{3,5},{1,3},{0,1},{10,8},{12,10},{14... | collective-permute-start | bytes 3145736 | tf_op jit(solution)/shard_map/ppermute | solution.py:606
  183.4 44.7 %collective-permute-start.2 = (bf16[128,4096]{1,0:T(8,128)(2,1)}, bf16[128,4096]{1,0:T(8,128)(2,1)S(1)}, u32[]{:S(2)}, u32[]{:S(2)}) collective-permute-start(bf16[128,4096]{1,0:T(8,128)(2,1)} %collective-permute-done.1.refs_0_.refs_6_), channel_id=1, source_target_pairs={{0,2},{2,4},{4,6},{6,7},{7,5},{5,3},{3,1},{1,0},{8,10},{10,12},{12... | collective-permute-start | bytes 3145736 | tf_op jit(solution)/shard_map/ppermute | solution.py:605
  185.4 44.9 %collective-permute-start.6 = (bf16[128,4096]{1,0:T(8,128)(2,1)}, bf16[128,4096]{1,0:T(8,128)(2,1)}, u32[]{:S(2)}, u32[]{:S(2)}) collective-permute-start(bf16[128,4096]{1,0:T(8,128)(2,1)} %copy-done.13), channel_id=1, source_target_pairs={{2,0},{4,2},{6,4},{7,6},{5,7},{3,5},{1,3},{0,1},{10,8},{12,10},{14... | collective-permute-start | bytes 3145736 | tf_op jit(solution)/shard_map/ppermute | solution.py:606
  190.4 47.7 %collective-permute-start.16 = (bf16[128,4096]{1,0:T(8,128)(2,1)}, bf16[128,4096]{1,0:T(8,128)(2,1)}, u32[]{:S(2)}, u32[]{:S(2)}) collective-permute-start(bf16[128,4096]{1,0:T(8,128)(2,1)} %collective-permute-done.refs_0_.refs_2_), channel_id=1, source_target_pairs={{3,2},{4,5},{11,10},{12,13},{19,18},{20,21},{27,26},{28,29}} | collective-permute-start | bytes 3145736 | tf_op jit(solution)/shard_map/ppermute | solution.py:505
  207.2 32.7 %collective-permute-start.27 = (bf16[2,2,128,512]{3,2,1,0:T(8,128)(2,1)}, bf16[2,2,128,512]{3,2,1,0:T(8,128)(2,1)}, u32[]{:S(2)}, u32[]{:S(2)}) collective-permute-start(bf16[2,2,128,512]{3,2,1,0:T(8,128)(2,1)} %shard_map.153.refs_18_.refs_12_.refs_16_), channel_id=1, source_target_pairs={{0,8},{8,0},{16,24},{24,16},{1,9},{9,1},{17,25},{25,17},{2,10},{10... | collective-permute-start | bytes 1572872 | tf_op jit(solution)/shard_map/ppermute | solution.py:529
  209.6 31.8 %collective-permute-start.28 = (bf16[2,2,128,512]{3,2,1,0:T(8,128)(2,1)}, bf16[2,2,128,512]{3,2,1,0:T(8,128)(2,1)}, u32[]{:S(2)}, u32[]{:S(2)}) collective-permute-start(bf16[2,2,128,512]{3,2,1,0:T(8,128)(2,1)} %collective-permute-done.26.refs_19_.refs_13_.refs_17_), channel_id=1, source_target_pairs={{0,8},{8,0},{16,24},{24,16},{1,9},{9,1},{17,25},{25,17},{2,10},{10... | collective-permute-start | bytes 1572872 | tf_op jit(solution)/shard_map/ppermute | solution.py:529
  228.1 35.1 %collective-permute-start.17 = (bf16[128,4096]{1,0:T(8,128)(2,1)}, bf16[128,4096]{1,0:T(8,128)(2,1)}, u32[]{:S(2)}, u32[]{:S(2)}) collective-permute-start(bf16[128,4096]{1,0:T(8,128)(2,1)} %collective-permute-done.8.refs_1_.refs_3_), channel_id=1, source_target_pairs={{3,2},{4,5},{11,10},{12,13},{19,18},{20,21},{27,26},{28,29}} | collective-permute-start | bytes 3145736 | tf_op jit(solution)/shard_map/ppermute | solution.py:505
  230.3 33.0 %collective-permute-start.18 = (bf16[128,4096]{1,0:T(8,128)(2,1)}, bf16[128,4096]{1,0:T(8,128)(2,1)}, u32[]{:S(2)}, u32[]{:S(2)}) collective-permute-start(bf16[128,4096]{1,0:T(8,128)(2,1)} %copy-done.12), channel_id=1, source_target_pairs={{5,4},{2,3},{13,12},{10,11},{21,20},{18,19},{29,28},{26,27}} | collective-permute-start | bytes 3145736 | tf_op jit(solution)/shard_map/ppermute | solution.py:505
  238.1 58.4 %collective-permute-start.19 = (bf16[128,4096]{1,0:T(8,128)(2,1)}, bf16[128,4096]{1,0:T(8,128)(2,1)}, u32[]{:S(2)}, u32[]{:S(2)}) collective-permute-start(bf16[128,4096]{1,0:T(8,128)(2,1)} %copy-done.11), channel_id=1, source_target_pairs={{5,4},{2,3},{13,12},{10,11},{21,20},{18,19},{29,28},{26,27}} | collective-permute-start | bytes 3145736 | tf_op jit(solution)/shard_map/ppermute | solution.py:505
  239.9 23.9 %collective-permute-start.29 = (bf16[2,1,128,512]{3,2,1,0:T(8,128)(2,1)}, bf16[2,1,128,512]{3,2,1,0:T(8,128)(2,1)S(1)}, u32[]{:S(2)}, u32[]{:S(2)}) collective-permute-start(bf16[2,1,128,512]{3,2,1,0:T(8,128)(2,1)} %shard_map.154.refs_0_.refs_20_), channel_id=1, source_target_pairs={{0,16},{8,24},{16,0},{24,8},{1,17},{9,25},{17,1},{25,9},{2,18},{10... | collective-permute-start | bytes 786440 | tf_op jit(solution)/shard_map/ppermute | solution.py:529
  241.4 22.5 %collective-permute-start.30 = (bf16[2,1,128,512]{3,2,1,0:T(8,128)(2,1)}, bf16[2,1,128,512]{3,2,1,0:T(8,128)(2,1)}, u32[]{:S(2)}, u32[]{:S(2)}) collective-permute-start(bf16[2,1,128,512]{3,2,1,0:T(8,128)(2,1)} %shard_map.155.refs_1_.refs_21_), channel_id=1, source_target_pairs={{0,16},{8,24},{16,0},{24,8},{1,17},{9,25},{17,1},{25,9},{2,18},{10... | collective-permute-start | bytes 786440 | tf_op jit(solution)/shard_map/ppermute | solution.py:529
  263.8 15.8 %collective-permute-start.33 = (bf16[2,1,128,512]{3,2,1,0:T(8,128)(2,1)S(1)}, bf16[2,1,128,512]{3,2,1,0:T(8,128)(2,1)}, u32[]{:S(2)}, u32[]{:S(2)}) collective-permute-start(bf16[2,1,128,512]{3,2,1,0:T(8,128)(2,1)S(1)} %collective-permute-done.29.refs_2_.refs_22_), channel_id=1, source_target_pairs={{0,8},{8,0},{16,24},{24,16},{1,9},{9,1},{17,25},{25,17},{2,10},{10... | collective-permute-start | bytes 786440 | tf_op jit(solution)/shard_map/ppermute | solution.py:529
  263.9 17.0 %collective-permute-start.34 = (bf16[2,1,128,512]{3,2,1,0:T(8,128)(2,1)}, bf16[2,1,128,512]{3,2,1,0:T(8,128)(2,1)}, u32[]{:S(2)}, u32[]{:S(2)}) collective-permute-start(bf16[2,1,128,512]{3,2,1,0:T(8,128)(2,1)} %collective-permute-done.30.refs_3_.refs_23_), channel_id=1, source_target_pairs={{0,8},{8,0},{16,24},{24,16},{1,9},{9,1},{17,25},{25,17},{2,10},{10... | collective-permute-start | bytes 786440 | tf_op jit(solution)/shard_map/ppermute | solution.py:529
  273.7 22.9 %collective-permute-start.11 = (bf16[64,4096]{1,0:T(8,128)(2,1)}, bf16[64,4096]{1,0:T(8,128)(2,1)S(1)}, u32[]{:S(2)}, u32[]{:S(2)}) collective-permute-start(bf16[64,4096]{1,0:T(8,128)(2,1)} %slice.18), channel_id=1, source_target_pairs={{1,0},{4,6},{6,7},{3,1},{9,8},{12,14},{14,15},{11,9},{17,16},{20,2... | collective-permute-start | bytes 1572872 | tf_op jit(solution)/shard_map/ppermute | solution.py:626
  275.0 21.6 %collective-permute-start.15 = (bf16[64,4096]{1,0:T(8,128)(2,1)}, bf16[64,4096]{1,0:T(8,128)(2,1)S(1)}, u32[]{:S(2)}, u32[]{:S(2)}) collective-permute-start(bf16[64,4096]{1,0:T(8,128)(2,1)} %slice.19), channel_id=1, source_target_pairs={{2,0},{7,6},{5,7},{0,1},{10,8},{15,14},{13,15},{8,9},{18,16},{23,2... | collective-permute-start | bytes 1572872 | tf_op jit(solution)/shard_map/ppermute | solution.py:627
  279.6 21.4 %collective-permute-start.3 = (bf16[64,4096]{1,0:T(8,128)(2,1)S(1)}, bf16[64,4096]{1,0:T(8,128)(2,1)S(1)}, u32[]{:S(2)}, u32[]{:S(2)}) collective-permute-start(bf16[64,4096]{1,0:T(8,128)(2,1)S(1)} %slice.16), channel_id=1, source_target_pairs={{1,0},{4,6},{6,7},{3,1},{9,8},{12,14},{14,15},{11,9},{17,16},{20,2... | collective-permute-start | bytes 1572872 | tf_op jit(solution)/shard_map/ppermute | solution.py:626
  280.9 25.6 %collective-permute-start.7 = (bf16[64,4096]{1,0:T(8,128)(2,1)S(1)}, bf16[64,4096]{1,0:T(8,128)(2,1)S(1)}, u32[]{:S(2)}, u32[]{:S(2)}) collective-permute-start(bf16[64,4096]{1,0:T(8,128)(2,1)S(1)} %slice.17), channel_id=1, source_target_pairs={{2,0},{7,6},{5,7},{0,1},{10,8},{15,14},{13,15},{8,9},{18,16},{23,2... | collective-permute-start | bytes 1572872 | tf_op jit(solution)/shard_map/ppermute | solution.py:627
  (29 other events, 656.9 us)
where the time goes:
time: 316 us; the launch traced here: 315 us
  waiting for transfers between devices  151 us (48%)
  Pallas kernels  75 us (24%)
  starting transfers between devices  45.8 us (14%)
  blocking collectives  34.9 us (11%)
  local copies, waits for them, and re-layouts  6.18 us (2%)
    pallas_call x4, Pallas kernels, launch(): pl.pallas_call(kernel, out_shape=out_shape, grid_spec=pltpu.PrefetchScala...  45.8 us
    all_to_all x1, blocking collectives, local(): lax.all_to_all(b, ('src', 'rcv'), split_axis=0, concat_axis=0, tiled=True)  34.9 us
    ppermute x2, waiting for transfers between devices, local(): behind.append(lax.ppermute(own[part], 'rcv', backward))  34.2 us
    ppermute x4, waiting for transfers between devices, local(): moved.append(lax.ppermute(ahead[part], 'rcv', forward))  33.6 us
    ppermute x18, waiting for transfers between devices, exchange(): lax.ppermute(x, 'src', swap)  27 us
    ppermute x4, waiting for transfers between devices, local(): moved.append(lax.ppermute(behind[part], 'rcv', backward))  24.4 us
    all_to_all x1, waiting for transfers between devices, local(): lax.all_to_all(b, ('src', 'rcv'), split_axis=0, concat_axis=0, tiled=True)  21.7 us
    pallas_call x6, Pallas kernels, cut(): pl.pallas_call(cut_kernel, out_shape=jax.ShapeDtypeStruct(shape, jnp.bflo...  17 us
  transfers between devices with their start and end apart: 40, of which 14 were waited for; matrix products, arithmetic and copies ran while one was open for 2% of the time, Pallas kernels for 20%

commit v1 on v0

--- a/solution.py
+++ b/solution.py
@@ -539,14 +539,6 @@
         tiles = tiles_of(blocks, mine)
         note(exchange(tiles), [first for _, first in blocks])
 
-    def collect_apart(blocks):
-        by_part = []
-        for part in range(2):
-            tiles = cut(blocks, mine, gains, device, (part,))
-            by_part.append(exchange(tiles))
-        pairs = [((first, second), mask) for (first, mask), (second, _) in zip(*by_part)]
-        note(pairs, [first for _, first in blocks])
-
     blocks = transposed_blocks(data, devices)
     arrived = [
         lax.all_to_all(b, ("src", "rcv"), split_axis=0, concat_axis=0, tiled=True) for b in blocks
@@ -608,7 +600,7 @@
         rows_of[-step], rows_of[step] = (ahead, origin(-step)), (behind, origin(step))
     taken = [hop(rows_of[offset][0], from_mate(offset)) for offset in (-1, 1)]
     late_from = len(columns)
-    collect_apart([rows_of[-steps], rows_of[steps]])
+    collect([rows_of[-steps], rows_of[steps]])
     across = [(order[i], order[(i + half) % rcv_count]) for i in range(rcv_count)]
     far_pieces = cut([(own, origin(0))], far, gains, device)
     far_pieces = lax.ppermute(far_pieces, "rcv", across)
@@ -635,10 +627,9 @@
     candidates = (*last, *taken[0], *taken[1])
     packed = [(packed_inside, len(inside)), (packed_outside, len(outside))]
     splits = [len(inside) // 2, len(inside)]
-    jobs = [Job(as_rows(inside + outside), late, packed=packed, splits=splits)]
-    out = launch(device, out, jobs, used, span, total)[0]
-    jobs = [Job([(candidates, far * rows)], columns, choice=chosen)]
-    return launch(device, out, jobs, used, span, total)[0]
+    near_rows = Job(as_rows(inside + outside), late, packed=packed, splits=splits)
+    far_rows = Job([(candidates, far * rows)], columns, choice=chosen)
+    return launch(device, out, [near_rows, far_rows], used, span, total)[0]
 
 
 def solution(mesh):

time: 316 us -> 310 us (0.981)
  the two profiles are of different devices: /device:TPU:0 before, /device:TPU:18 now
where the time goes in v1:
time: 310 us; the launch traced here: 304 us
  waiting for transfers between devices  143 us (46%)
  Pallas kernels  69.6 us (22%)
  starting transfers between devices  48.5 us (16%)
  blocking collectives  29.9 us (10%)
  local copies, waits for them, and re-layouts  10.8 us (3%)
    pallas_call x3, Pallas kernels, launch(): pl.pallas_call(kernel, out_shape=out_shape, grid_spec=pltpu.PrefetchScala...  43 us
    ppermute x1, waiting for transfers between devices, local(): far_pieces = lax.ppermute(far_pieces, 'rcv', across)  41.7 us
    ppermute x4, waiting for transfers between devices, local(): moved.append(lax.ppermute(ahead[part], 'rcv', forward))  33.7 us
    ppermute x15, waiting for transfers between devices, exchange(): lax.ppermute(x, 'src', swap)  31.8 us
    all_to_all x1, blocking collectives, local(): lax.all_to_all(b, ('src', 'rcv'), split_axis=0, concat_axis=0, tiled=True)  29.9 us
    all_to_all x1, waiting for transfers between devices, local(): lax.all_to_all(b, ('src', 'rcv'), split_axis=0, concat_axis=0, tiled=True)  18.2 us
    ppermute x4, waiting for transfers between devices, local(): moved.append(lax.ppermute(behind[part], 'rcv', backward))  17.5 us
    pallas_call x5, Pallas kernels, cut(): pl.pallas_call(cut_kernel, out_shape=jax.ShapeDtypeStruct(shape, jnp.bflo...  14.4 us
  transfers between devices with their start and end apart: 37, of which 12 were waited for; matrix products, arithmetic and copies ran while one was open for 3% of the time, Pallas kernels for 17%

profile of v1, /device:TPU:18, one launch (start us, length us, event | category | flops | bytes accessed | tf_op | source)
XLA Modules:
  0.0 303.6 jit_solution(2917744804187376849)
XLA Ops:
  0.0 4.0 %shard_map.130 = (bf16[32,128,128]{2,1,0:T(8,128)(2,1)}, bf16[32,128,128]{2,1,0:T(8,128)(2,1)}) custom-call(bf16[2,128,4096]{2,1,0:T(8,128)(2,1)} %data_ref.5), custom_call_target="tpu_custom_call" | custom-call | tf_op jit(solution)/shard_map/pallas_call | solution.py:30
  4.0 29.9 %all_to_all.10.arrived_ref = bf16[32,128,128]{2,1,0:T(8,128)(2,1)} all-to-all(bf16[32,128,128]{2,1,0:T(8,128)(2,1)} %get-tuple-element.12), channel_id=1, replica_groups=mesh['src'=4,'rcv'=8] {'src','rcv'}, dimensions={0} | all-to-all | bytes 2097152 | tf_op jit(solution)/shard_map/all_to_all | solution.py:544
  34.0 6.2 %all-to-all-start = ((bf16[32,128,128]{2,1,0:T(8,128)(2,1)}), bf16[32,128,128]{2,1,0:T(8,128)(2,1)S(1)}, u32[]{:S(2)}, u32[]{:S(2)}) async-start(bf16[32,128,128]{2,1,0:T(8,128)(2,1)} %get-tuple-element.11), calls=%async_computation | async-start | bytes 2097152 | tf_op jit(solution)/shard_map/all_to_all | solution.py:544
  40.2 4.1 %shard_map.132.refs_1_ = bf16[128,4096]{1,0:T(8,128)(2,1)} custom-call(bf16[2,128,4096]{2,1,0:T(8,128)(2,1)} %data_ref.5, s32[128,4096]{1,0:T(8,128)} %mask_ref.3, bf16[32,128,128]{2,1,0:T(8,128)(2,1)} %all_to_all.10.arrived_ref), custom_call_target="tpu_custom_call" | custom-call | tf_op jit(solution)/shard_map/pallas_call | solution.py:55
  45.8 18.2 %all-to-all-done.arrived_ref = bf16[32,128,128]{2,1,0:T(8,128)(2,1)S(1)} async-done(((bf16[32,128,128]{2,1,0:T(8,128)(2,1)}), bf16[32,128,128]{2,1,0:T(8,128)(2,1)S(1)}, u32[]{:S(2)}, u32[]{:S(2)}) %all-to-all-start) | async-done | bytes 1048608 | tf_op jit(solution)/shard_map/all_to_all | solution.py:544
  64.9 4.1 %shard_map.131.refs_0_ = bf16[128,4096]{1,0:T(8,128)(2,1)} custom-call(bf16[2,128,4096]{2,1,0:T(8,128)(2,1)} %data_ref.5, s32[128,4096]{1,0:T(8,128)} %mask_ref.3, bf16[32,128,128]{2,1,0:T(8,128)(2,1)} %copy-done.2), custom_call_target="tpu_custom_call" | custom-call | tf_op jit(solution)/shard_map/pallas_call | solution.py:55
  71.7 2.7 shard_map.135.refs_10_.refs_4_.refs_18_
  75.9 2.1 collective-permute-start.3
  78.0 4.1 %collective-permute-done.19.refs_11_.refs_5_.refs_19_ = bf16[1,2,128,512]{3,2,1,0:T(8,128)(2,1)S(1)} collective-permute-done((bf16[1,2,128,512]{3,2,1,0:T(8,128)(2,1)}, bf16[1,2,128,512]{3,2,1,0:T(8,128)(2,1)S(1)}, u32[]{:S(2)}, u32[]{:S(2)}) %collective-permute-start.19) | collective-permute-done | bytes 262176 | tf_op jit(solution)/shard_map/ppermute | solution.py:529
  82.2 2.7 shard_map.134
  84.9 2.8 collective-permute-start.15
  87.7 41.7 %collective-permute-done.15.refs_4_.refs_34_ = bf16[1,2,128,512]{3,2,1,0:T(8,128)(2,1)S(1)} collective-permute-done((bf16[1,2,128,512]{3,2,1,0:T(8,128)(2,1)}, bf16[1,2,128,512]{3,2,1,0:T(8,128)(2,1)S(1)}, u32[]{:S(2)}, u32[]{:S(2)}) %collective-permute-start.15) | collective-permute-done | bytes 262176 | tf_op jit(solution)/shard_map/ppermute | solution.py:606
  129.9 2.0 collective-permute-start.1
  131.9 5.4 %collective-permute-done.16.refs_5_.refs_35_ = bf16[1,2,128,512]{3,2,1,0:T(8,128)(2,1)S(1)} collective-permute-done((bf16[1,2,128,512]{3,2,1,0:T(8,128)(2,1)S(1)}, bf16[1,2,128,512]{3,2,1,0:T(8,128)(2,1)S(1)}, u32[]{:S(2)}, u32[]{:S(2)}) %collective-permute-start.16) | collective-permute-done | bytes 262176 | tf_op jit(solution)/shard_map/ppermute | solution.py:529
  137.9 3.0 shard_map.136.refs_14_.refs_8_.refs_22_
  141.4 1.9 collective-permute-start.7
  143.4 12.2 %collective-permute-done.22.refs_15_.refs_9_.refs_23_ = bf16[2,2,128,512]{3,2,1,0:T(8,128)(2,1)S(1)} collective-permute-done((bf16[2,2,128,512]{3,2,1,0:T(8,128)(2,1)}, bf16[2,2,128,512]{3,2,1,0:T(8,128)(2,1)S(1)}, u32[]{:S(2)}, u32[]{:S(2)}) %collective-permute-start.22) | collective-permute-done | bytes 524320 | tf_op jit(solution)/shard_map/ppermute | solution.py:529
  158.3 20.4 %collective-permute-done.4.refs_1_.refs_7_ = bf16[128,4096]{1,0:T(8,128)(2,1)S(1)} collective-permute-done((bf16[128,4096]{1,0:T(8,128)(2,1)}, bf16[128,4096]{1,0:T(8,128)(2,1)S(1)}, u32[]{:S(2)}, u32[]{:S(2)}) %collective-permute-start.4) | collective-permute-done | bytes 1048608 | tf_op jit(solution)/shard_map/ppermute | solution.py:597
  178.7 2.0 collective-permute-start.5
  183.8 17.0 %collective-permute-done.11.refs_4_.refs_3_ = bf16[128,4096]{1,0:T(8,128)(2,1)S(1)} collective-permute-done((bf16[128,4096]{1,0:T(8,128)(2,1)}, bf16[128,4096]{1,0:T(8,128)(2,1)S(1)}, u32[]{:S(2)}, u32[]{:S(2)}) %collective-permute-start.11) | collective-permute-done | bytes 1048608 | tf_op jit(solution)/shard_map/ppermute | solution.py:598
  202.2 6.5 %collective-permute-start.34 = (bf16[128,4096]{1,0:T(8,128)(2,1)}, bf16[128,4096]{1,0:T(8,128)(2,1)}, u32[]{:S(2)}, u32[]{:S(2)}) collective-permute-start(bf16[128,4096]{1,0:T(8,128)(2,1)} %collective-permute-done.6.refs_3_.refs_4_), channel_id=1, source_target_pairs={{5,4},{2,3},{13,12},{10,11},{21,20},{18,19},{29,28},{26,27}} | collective-permute-start | bytes 3145736 | tf_op jit(solution)/shard_map/ppermute | solution.py:505
  208.7 13.2 %collective-permute-done.5.refs_1_ = bf16[128,4096]{1,0:T(8,128)(2,1)S(1)} collective-permute-done((bf16[128,4096]{1,0:T(8,128)(2,1)S(1)}, bf16[128,4096]{1,0:T(8,128)(2,1)S(1)}, u32[]{:S(2)}, u32[]{:S(2)}) %collective-permute-start.5) | collective-permute-done | bytes 1048608 | tf_op jit(solution)/shard_map/ppermute | solution.py:597
  222.0 3.0 collective-permute-start.35
  225.0 3.0 shard_map.137.refs_18_.refs_12_.refs_26_
  229.5 3.0 shard_map.133.refs_0_.refs_30_
  232.6 7.6 %collective-permute-done.25.refs_19_.refs_13_.refs_27_ = bf16[2,2,128,512]{3,2,1,0:T(8,128)(2,1)} collective-permute-done((bf16[2,2,128,512]{3,2,1,0:T(8,128)(2,1)}, bf16[2,2,128,512]{3,2,1,0:T(8,128)(2,1)}, u32[]{:S(2)}, u32[]{:S(2)}) %collective-permute-start.25) | collective-permute-done | bytes 524320 | tf_op jit(solution)/shard_map/ppermute | solution.py:529
  246.6 1.9 slice.18
  248.6 1.9 slice.19
  254.7 4.5 %collective-permute-start.31 = (bf16[64,4096]{1,0:T(8,128)(2,1)}, bf16[64,4096]{1,0:T(8,128)(2,1)}, u32[]{:S(2)}, u32[]{:S(2)}) collective-permute-start(bf16[64,4096]{1,0:T(8,128)(2,1)} %slice.19), channel_id=1, source_target_pairs={{2,0},{7,6},{5,7},{0,1},{10,8},{15,14},{13,15},{8,9},{18,16},{23,2... | collective-permute-start | bytes 1572872 | tf_op jit(solution)/shard_map/ppermute | solution.py:619
  259.2 18.5 %shard_map.138 = (f32[2,1024,512]{2,1,0:T(8,128)}, bf16[2,640,1536]{2,1,0:T(8,128)(2,1)}) custom-call(s32[1]{0:T(128)} %bitcast.device_ref, s32[32,49]{1,0:T(8,128)} %constant.43.clone.plan_ref, s32[2,8]{1,0:T(2,128)} %convert_element_type.3.used_ref, bf16[128,4096]{1,0:T(8,128)(2,1)} %shard_map.131.refs_0_, bf16[128,4096]{1,0:T(8,128)(2,1)} %shard_map.132.refs_1_, ...), custom_call_target="tpu_custom_call" | custom-call | flops 10737418240 | bytes 83886080 | tf_op jit(solution)/shard_map/pallas_call | solution.py:454
  277.8 9.5 %shard_map.139 = (f32[2,1024,512]{2,1,0:T(8,128)}, bf16[2,256,1536]{2,1,0:T(8,128)(2,1)}) custom-call(s32[1]{0:T(128)} %bitcast.device_ref, s32[32,46]{1,0:T(8,128)} %constant.44.clone.plan_ref, s32[2,8]{1,0:T(2,128)} %convert_element_type.3.used_ref, bf16[128,4096]{1,0:T(8,128)(2,1)} %copy-done.4, ...), custom_call_target="tpu_custom_call", output_to_operand_aliasing={{0}: (19, {})} | custom-call | flops 4294967296 | bytes 83886080 | tf_op jit(solution)/shard_map/pallas_call | solution.py:454
  288.5 15.0 %shard_map.140 = f32[2,1024,512]{2,1,0:T(8,128)} custom-call(s32[1]{0:T(128)} %bitcast.device_ref, s32[32,53]{1,0:T(8,128)} %constant.45.clone.plan_ref, s32[2,8]{1,0:T(2,128)} %convert_element_type.3.used_ref, bf16[2,2,128,512]{3,2,1,0:T(8,128)(2,1)} %shard_map.133.refs_0_.refs_30_, ...), custom_call_target="tpu_custom_call", output_to_operand_aliasing={{}: (41, {})} | custom-call | flops 7784628224 | bytes 83886080 | tf_op jit(solution)/shard_map/pallas_call | solution.py:454
  (116 shorter events, 28.9 us)
Async XLA Ops:
  34.0 30.0 %all-to-all-start = ((bf16[32,128,128]{2,1,0:T(8,128)(2,1)}), bf16[32,128,128]{2,1,0:T(8,128)(2,1)S(1)}, u32[]{:S(2)}, u32[]{:S(2)}) async-start(bf16[32,128,128]{2,1,0:T(8,128)(2,1)} %get-tuple-element.11), calls=%async_computation | async-start | bytes 2097152 | tf_op jit(solution)/shard_map/all_to_all | solution.py:544
  44.2 85.6 %collective-permute-start.9 = (bf16[128,4096]{1,0:T(8,128)(2,1)}, bf16[128,4096]{1,0:T(8,128)(2,1)S(1)}, u32[]{:S(2)}, u32[]{:S(2)}) collective-permute-start(bf16[128,4096]{1,0:T(8,128)(2,1)} %shard_map.132.refs_1_), channel_id=1, source_target_pairs={{2,0},{4,2},{6,4},{7,6},{5,7},{3,5},{1,3},{0,1},{10,8},{12,10},{14... | collective-permute-start | bytes 3145736 | tf_op jit(solution)/shard_map/ppermute | solution.py:550
  69.0 60.9 %collective-permute-start = (bf16[128,4096]{1,0:T(8,128)(2,1)}, bf16[128,4096]{1,0:T(8,128)(2,1)}, u32[]{:S(2)}, u32[]{:S(2)}) collective-permute-start(bf16[128,4096]{1,0:T(8,128)(2,1)} %shard_map.131.refs_0_), channel_id=1, source_target_pairs={{0,2},{2,4},{4,6},{6,7},{7,5},{5,3},{3,1},{1,0},{8,10},{10,12},{12... | collective-permute-start | bytes 3145736 | tf_op jit(solution)/shard_map/ppermute | solution.py:549
  74.4 7.8 %collective-permute-start.19 = (bf16[1,2,128,512]{3,2,1,0:T(8,128)(2,1)}, bf16[1,2,128,512]{3,2,1,0:T(8,128)(2,1)S(1)}, u32[]{:S(2)}, u32[]{:S(2)}) collective-permute-start(bf16[1,2,128,512]{3,2,1,0:T(8,128)(2,1)} %shard_map.135.refs_10_.refs_4_.refs_18_), channel_id=1, source_target_pairs={{0,16},{8,24},{16,0},{24,8},{1,17},{9,25},{17,1},{25,9},{2,18},{10... | collective-permute-start | bytes 786440 | tf_op jit(solution)/shard_map/ppermute | solution.py:529
  75.9 61.4 %collective-permute-start.3 = (bf16[128,4096]{1,0:T(8,128)(2,1)S(1)}, bf16[128,4096]{1,0:T(8,128)(2,1)}, u32[]{:S(2)}, u32[]{:S(2)}) collective-permute-start(bf16[128,4096]{1,0:T(8,128)(2,1)S(1)} %copy-done.1), channel_id=1, source_target_pairs={{0,2},{2,4},{4,6},{6,7},{7,5},{5,3},{3,1},{1,0},{8,10},{10,12},{12... | collective-permute-start | bytes 3145736 | tf_op jit(solution)/shard_map/ppermute | solution.py:549
  78.0 59.8 %collective-permute-start.6 = (bf16[128,4096]{1,0:T(8,128)(2,1)}, bf16[128,4096]{1,0:T(8,128)(2,1)}, u32[]{:S(2)}, u32[]{:S(2)}) collective-permute-start(bf16[128,4096]{1,0:T(8,128)(2,1)} %shard_map.131.refs_0_), channel_id=1, source_target_pairs={{2,0},{4,2},{6,4},{7,6},{5,7},{3,5},{1,3},{0,1},{10,8},{12,10},{14... | collective-permute-start | bytes 3145736 | tf_op jit(solution)/shard_map/ppermute | solution.py:550
  84.9 44.5 %collective-permute-start.15 = (bf16[1,2,128,512]{3,2,1,0:T(8,128)(2,1)}, bf16[1,2,128,512]{3,2,1,0:T(8,128)(2,1)S(1)}, u32[]{:S(2)}, u32[]{:S(2)}) collective-permute-start(bf16[1,2,128,512]{3,2,1,0:T(8,128)(2,1)} %shard_map.134), channel_id=1, source_target_pairs={{0,7},{2,5},{4,3},{6,1},{7,0},{5,2},{3,4},{1,6},{8,15},{10,13},{12... | collective-permute-start | bytes 786440 | tf_op jit(solution)/shard_map/ppermute | solution.py:606
  129.4 7.9 %collective-permute-start.16 = (bf16[1,2,128,512]{3,2,1,0:T(8,128)(2,1)S(1)}, bf16[1,2,128,512]{3,2,1,0:T(8,128)(2,1)S(1)}, u32[]{:S(2)}, u32[]{:S(2)}) collective-permute-start(bf16[1,2,128,512]{3,2,1,0:T(8,128)(2,1)S(1)} %collective-permute-done.15.refs_4_.refs_34_), channel_id=1, source_target_pairs={{0,16},{8,24},{16,0},{24,8},{1,17},{9,25},{17,1},{25,9},{2,18},{10... | collective-permute-start | bytes 786440 | tf_op jit(solution)/shard_map/ppermute | solution.py:529
  129.9 26.1 %collective-permute-start.10 = (bf16[128,4096]{1,0:T(8,128)(2,1)S(1)}, bf16[128,4096]{1,0:T(8,128)(2,1)}, u32[]{:S(2)}, u32[]{:S(2)}) collective-permute-start(bf16[128,4096]{1,0:T(8,128)(2,1)S(1)} %collective-permute-done.9.refs_4_.refs_5_), channel_id=1, source_target_pairs={{2,0},{4,2},{6,4},{7,6},{5,7},{3,5},{1,3},{0,1},{10,8},{12,10},{14... | collective-permute-start | bytes 3145736 | tf_op jit(solution)/shard_map/ppermute | solution.py:598
  129.9 27.4 %collective-permute-start.1 = (bf16[128,4096]{1,0:T(8,128)(2,1)}, bf16[128,4096]{1,0:T(8,128)(2,1)}, u32[]{:S(2)}, u32[]{:S(2)}) collective-permute-start(bf16[128,4096]{1,0:T(8,128)(2,1)} %collective-permute-done.refs_0_.refs_2_), channel_id=1, source_target_pairs={{0,2},{2,4},{4,6},{6,7},{7,5},{5,3},{3,1},{1,0},{8,10},{10,12},{12... | collective-permute-start | bytes 3145736 | tf_op jit(solution)/shard_map/ppermute | solution.py:597
  140.9 37.8 %collective-permute-start.4 = (bf16[128,4096]{1,0:T(8,128)(2,1)}, bf16[128,4096]{1,0:T(8,128)(2,1)S(1)}, u32[]{:S(2)}, u32[]{:S(2)}) collective-permute-start(bf16[128,4096]{1,0:T(8,128)(2,1)} %collective-permute-done.3.refs_1_.refs_3_), channel_id=1, source_target_pairs={{0,2},{2,4},{4,6},{6,7},{7,5},{5,3},{3,1},{1,0},{8,10},{10,12},{12... | collective-permute-start | bytes 3145736 | tf_op jit(solution)/shard_map/ppermute | solution.py:597
  141.0 14.5 %collective-permute-start.22 = (bf16[2,2,128,512]{3,2,1,0:T(8,128)(2,1)}, bf16[2,2,128,512]{3,2,1,0:T(8,128)(2,1)S(1)}, u32[]{:S(2)}, u32[]{:S(2)}) collective-permute-start(bf16[2,2,128,512]{3,2,1,0:T(8,128)(2,1)} %shard_map.136.refs_14_.refs_8_.refs_22_), channel_id=1, source_target_pairs={{0,16},{8,24},{16,0},{24,8},{1,17},{9,25},{17,1},{25,9},{2,18},{10... | collective-permute-start | bytes 1572872 | tf_op jit(solution)/shard_map/ppermute | solution.py:529
  141.4 39.2 %collective-permute-start.7 = (bf16[128,4096]{1,0:T(8,128)(2,1)}, bf16[128,4096]{1,0:T(8,128)(2,1)}, u32[]{:S(2)}, u32[]{:S(2)}) collective-permute-start(bf16[128,4096]{1,0:T(8,128)(2,1)} %collective-permute-done.6.refs_3_.refs_4_), channel_id=1, source_target_pairs={{2,0},{4,2},{6,4},{7,6},{5,7},{3,5},{1,3},{0,1},{10,8},{12,10},{14... | collective-permute-start | bytes 3145736 | tf_op jit(solution)/shard_map/ppermute | solution.py:598
  155.5 25.1 %collective-permute-start.23 = (bf16[2,2,128,512]{3,2,1,0:T(8,128)(2,1)}, bf16[2,2,128,512]{3,2,1,0:T(8,128)(2,1)S(1)}, u32[]{:S(2)}, u32[]{:S(2)}) collective-permute-start(bf16[2,2,128,512]{3,2,1,0:T(8,128)(2,1)} %shard_map.136.refs_14_.refs_8_.refs_22_), channel_id=1, source_target_pairs={{0,8},{8,0},{16,24},{24,16},{1,9},{9,1},{17,25},{25,17},{2,10},{10... | collective-permute-start | bytes 1572872 | tf_op jit(solution)/shard_map/ppermute | solution.py:529
  156.0 44.8 %collective-permute-start.11 = (bf16[128,4096]{1,0:T(8,128)(2,1)}, bf16[128,4096]{1,0:T(8,128)(2,1)S(1)}, u32[]{:S(2)}, u32[]{:S(2)}) collective-permute-start(bf16[128,4096]{1,0:T(8,128)(2,1)} %collective-permute-done.10.refs_4_.refs_9_), channel_id=1, source_target_pairs={{2,0},{4,2},{6,4},{7,6},{5,7},{3,5},{1,3},{0,1},{10,8},{12,10},{14... | collective-permute-start | bytes 3145736 | tf_op jit(solution)/shard_map/ppermute | solution.py:598
  157.3 44.9 %collective-permute-start.2 = (bf16[128,4096]{1,0:T(8,128)(2,1)}, bf16[128,4096]{1,0:T(8,128)(2,1)S(1)}, u32[]{:S(2)}, u32[]{:S(2)}) collective-permute-start(bf16[128,4096]{1,0:T(8,128)(2,1)} %collective-permute-done.1.refs_0_.refs_6_), channel_id=1, source_target_pairs={{0,2},{2,4},{4,6},{6,7},{7,5},{5,3},{3,1},{1,0},{8,10},{10,12},{12... | collective-permute-start | bytes 3145736 | tf_op jit(solution)/shard_map/ppermute | solution.py:597
  178.7 43.3 %collective-permute-start.5 = (bf16[128,4096]{1,0:T(8,128)(2,1)S(1)}, bf16[128,4096]{1,0:T(8,128)(2,1)S(1)}, u32[]{:S(2)}, u32[]{:S(2)}) collective-permute-start(bf16[128,4096]{1,0:T(8,128)(2,1)S(1)} %collective-permute-done.4.refs_1_.refs_7_), channel_id=1, source_target_pairs={{0,2},{2,4},{4,6},{6,7},{7,5},{5,3},{3,1},{1,0},{8,10},{10,12},{12... | collective-permute-start | bytes 3145736 | tf_op jit(solution)/shard_map/ppermute | solution.py:597
  180.7 47.3 %collective-permute-start.8 = (bf16[128,4096]{1,0:T(8,128)(2,1)}, bf16[128,4096]{1,0:T(8,128)(2,1)}, u32[]{:S(2)}, u32[]{:S(2)}) collective-permute-start(bf16[128,4096]{1,0:T(8,128)(2,1)} %collective-permute-done.7.refs_3_.refs_8_), channel_id=1, source_target_pairs={{2,0},{4,2},{6,4},{7,6},{5,7},{3,5},{1,3},{0,1},{10,8},{12,10},{14... | collective-permute-start | bytes 3145736 | tf_op jit(solution)/shard_map/ppermute | solution.py:598
  182.6 50.0 %collective-permute-start.32 = (bf16[128,4096]{1,0:T(8,128)(2,1)}, bf16[128,4096]{1,0:T(8,128)(2,1)}, u32[]{:S(2)}, u32[]{:S(2)}) collective-permute-start(bf16[128,4096]{1,0:T(8,128)(2,1)} %collective-permute-done.refs_0_.refs_2_), channel_id=1, source_target_pairs={{3,2},{4,5},{11,10},{12,13},{19,18},{20,21},{27,26},{28,29}} | collective-permute-start | bytes 3145736 | tf_op jit(solution)/shard_map/ppermute | solution.py:505
  200.9 39.3 %collective-permute-start.33 = (bf16[128,4096]{1,0:T(8,128)(2,1)}, bf16[128,4096]{1,0:T(8,128)(2,1)}, u32[]{:S(2)}, u32[]{:S(2)}) collective-permute-start(bf16[128,4096]{1,0:T(8,128)(2,1)} %collective-permute-done.3.refs_1_.refs_3_), channel_id=1, source_target_pairs={{3,2},{4,5},{11,10},{12,13},{19,18},{20,21},{27,26},{28,29}} | collective-permute-start | bytes 3145736 | tf_op jit(solution)/shard_map/ppermute | solution.py:505
  202.2 39.7 %collective-permute-start.34 = (bf16[128,4096]{1,0:T(8,128)(2,1)}, bf16[128,4096]{1,0:T(8,128)(2,1)}, u32[]{:S(2)}, u32[]{:S(2)}) collective-permute-start(bf16[128,4096]{1,0:T(8,128)(2,1)} %collective-permute-done.6.refs_3_.refs_4_), channel_id=1, source_target_pairs={{5,4},{2,3},{13,12},{10,11},{21,20},{18,19},{29,28},{26,27}} | collective-permute-start | bytes 3145736 | tf_op jit(solution)/shard_map/ppermute | solution.py:505
  222.0 28.5 %collective-permute-start.35 = (bf16[128,4096]{1,0:T(8,128)(2,1)}, bf16[128,4096]{1,0:T(8,128)(2,1)}, u32[]{:S(2)}, u32[]{:S(2)}) collective-permute-start(bf16[128,4096]{1,0:T(8,128)(2,1)} %copy-done.13), channel_id=1, source_target_pairs={{5,4},{2,3},{13,12},{10,11},{21,20},{18,19},{29,28},{26,27}} | collective-permute-start | bytes 3145736 | tf_op jit(solution)/shard_map/ppermute | solution.py:505
  228.0 12.2 %collective-permute-start.25 = (bf16[2,2,128,512]{3,2,1,0:T(8,128)(2,1)}, bf16[2,2,128,512]{3,2,1,0:T(8,128)(2,1)}, u32[]{:S(2)}, u32[]{:S(2)}) collective-permute-start(bf16[2,2,128,512]{3,2,1,0:T(8,128)(2,1)} %shard_map.137.refs_18_.refs_12_.refs_26_), channel_id=1, source_target_pairs={{0,16},{8,24},{16,0},{24,8},{1,17},{9,25},{17,1},{25,9},{2,18},{10... | collective-permute-start | bytes 1572872 | tf_op jit(solution)/shard_map/ppermute | solution.py:529
  232.6 18.6 %collective-permute-start.26 = (bf16[2,2,128,512]{3,2,1,0:T(8,128)(2,1)}, bf16[2,2,128,512]{3,2,1,0:T(8,128)(2,1)S(1)}, u32[]{:S(2)}, u32[]{:S(2)}) collective-permute-start(bf16[2,2,128,512]{3,2,1,0:T(8,128)(2,1)} %shard_map.137.refs_18_.refs_12_.refs_26_), channel_id=1, source_target_pairs={{0,8},{8,0},{16,24},{24,16},{1,9},{9,1},{17,25},{25,17},{2,10},{10... | collective-permute-start | bytes 1572872 | tf_op jit(solution)/shard_map/ppermute | solution.py:529
  240.2 12.4 %collective-permute-start.27 = (bf16[2,2,128,512]{3,2,1,0:T(8,128)(2,1)}, bf16[2,2,128,512]{3,2,1,0:T(8,128)(2,1)S(1)}, u32[]{:S(2)}, u32[]{:S(2)}) collective-permute-start(bf16[2,2,128,512]{3,2,1,0:T(8,128)(2,1)} %collective-permute-done.25.refs_19_.refs_13_.refs_27_), channel_id=1, source_target_pairs={{0,8},{8,0},{16,24},{24,16},{1,9},{9,1},{17,25},{25,17},{2,10},{10... | collective-permute-start | bytes 1572872 | tf_op jit(solution)/shard_map/ppermute | solution.py:529
  240.2 14.5 %collective-permute-start.12 = (bf16[2,2,128,512]{3,2,1,0:T(8,128)(2,1)}, bf16[2,2,128,512]{3,2,1,0:T(8,128)(2,1)S(1)}, u32[]{:S(2)}, u32[]{:S(2)}) collective-permute-start(bf16[2,2,128,512]{3,2,1,0:T(8,128)(2,1)} %shard_map.133.refs_0_.refs_30_), channel_id=1, source_target_pairs={{0,16},{8,24},{16,0},{24,8},{1,17},{9,25},{17,1},{25,9},{2,18},{10... | collective-permute-start | bytes 1572872 | tf_op jit(solution)/shard_map/ppermute | solution.py:529
  241.9 17.3 %collective-permute-start.13 = (bf16[2,2,128,512]{3,2,1,0:T(8,128)(2,1)}, bf16[2,2,128,512]{3,2,1,0:T(8,128)(2,1)S(1)}, u32[]{:S(2)}, u32[]{:S(2)}) collective-permute-start(bf16[2,2,128,512]{3,2,1,0:T(8,128)(2,1)} %shard_map.133.refs_0_.refs_30_), channel_id=1, source_target_pairs={{0,8},{8,0},{16,24},{24,16},{1,9},{9,1},{17,25},{25,17},{2,10},{10... | collective-permute-start | bytes 1572872 | tf_op jit(solution)/shard_map/ppermute | solution.py:529
  250.5 36.8 %collective-permute-start.28 = (bf16[64,4096]{1,0:T(8,128)(2,1)}, bf16[64,4096]{1,0:T(8,128)(2,1)S(1)}, u32[]{:S(2)}, u32[]{:S(2)}) collective-permute-start(bf16[64,4096]{1,0:T(8,128)(2,1)} %slice.16), channel_id=1, source_target_pairs={{1,0},{4,6},{6,7},{3,1},{9,8},{12,14},{14,15},{11,9},{17,16},{20,2... | collective-permute-start | bytes 1572872 | tf_op jit(solution)/shard_map/ppermute | solution.py:618
  251.2 36.1 %collective-permute-start.29 = (bf16[64,4096]{1,0:T(8,128)(2,1)}, bf16[64,4096]{1,0:T(8,128)(2,1)S(1)}, u32[]{:S(2)}, u32[]{:S(2)}) collective-permute-start(bf16[64,4096]{1,0:T(8,128)(2,1)} %slice.17), channel_id=1, source_target_pairs={{2,0},{7,6},{5,7},{0,1},{10,8},{15,14},{13,15},{8,9},{18,16},{23,2... | collective-permute-start | bytes 1572872 | tf_op jit(solution)/shard_map/ppermute | solution.py:619
  252.5 34.8 %collective-permute-start.30 = (bf16[64,4096]{1,0:T(8,128)(2,1)}, bf16[64,4096]{1,0:T(8,128)(2,1)}, u32[]{:S(2)}, u32[]{:S(2)}) collective-permute-start(bf16[64,4096]{1,0:T(8,128)(2,1)} %slice.18), channel_id=1, source_target_pairs={{1,0},{4,6},{6,7},{3,1},{9,8},{12,14},{14,15},{11,9},{17,16},{20,2... | collective-permute-start | bytes 1572872 | tf_op jit(solution)/shard_map/ppermute | solution.py:618
  254.7 32.6 %collective-permute-start.31 = (bf16[64,4096]{1,0:T(8,128)(2,1)}, bf16[64,4096]{1,0:T(8,128)(2,1)}, u32[]{:S(2)}, u32[]{:S(2)}) collective-permute-start(bf16[64,4096]{1,0:T(8,128)(2,1)} %slice.19), channel_id=1, source_target_pairs={{2,0},{7,6},{5,7},{0,1},{10,8},{15,14},{13,15},{8,9},{18,16},{23,2... | collective-permute-start | bytes 1572872 | tf_op jit(solution)/shard_map/ppermute | solution.py:619
  259.2 28.2 %collective-permute-start.14 = (bf16[2,2,128,512]{3,2,1,0:T(8,128)(2,1)S(1)}, bf16[2,2,128,512]{3,2,1,0:T(8,128)(2,1)S(1)}, u32[]{:S(2)}, u32[]{:S(2)}) collective-permute-start(bf16[2,2,128,512]{3,2,1,0:T(8,128)(2,1)S(1)} %collective-permute-done.12.refs_1_.refs_31_), channel_id=1, source_target_pairs={{0,8},{8,0},{16,24},{24,16},{1,9},{9,1},{17,25},{25,17},{2,10},{10... | collective-permute-start | bytes 1572872 | tf_op jit(solution)/shard_map/ppermute | solution.py:529
  (31 other events, 850.8 us)

commit v2 on v1

--- a/solution.py
+++ b/solution.py
@@ -163,26 +163,24 @@
 
 
 def cut_kernel(device_ref, place_ref, *refs):
-    ins, out_ref = refs[:-1], refs[-1]
-    blocks, parts = out_ref.shape[:2]
-    for block in range(blocks):
-        *planes, gain = ins[(parts + 1) * block : (parts + 1) * (block + 1)]
-        for part, ref in enumerate(planes):
+    planes, out_ref = refs[:-1], refs[-1]
+    for block in range(out_ref.shape[0]):
+        first, second, gain = planes[3 * block : 3 * block + 3]
+        for part, ref in enumerate((first, second)):
             out_ref[block, part] = (ref[...].astype(jnp.float32) * gain[...]).astype(jnp.bfloat16)
 
 
-def cut(blocks, column, gains, device, parts=(0, 1)):
+def cut(blocks, column, gains, device):
     rows = blocks[0][0][0].shape[0]
     place = np.stack([column] + [first for _, first in blocks], axis=1).astype(np.int32)
     specs, operands = [], []
     for index, (planes, _) in enumerate(blocks):
-        spec = pl.BlockSpec((rows, TILE_SIZE), lambda i, me, place: (0, place[me[0], 0]))
-        specs += [spec] * len(parts)
+        specs += [pl.BlockSpec((rows, TILE_SIZE), lambda i, me, place: (0, place[me[0], 0]))] * 2
         specs.append(
             pl.BlockSpec((None, rows, 1), lambda i, me, place, at=index + 1: (place[me[0], at], 0, 0))
         )
-        operands += [*(planes[part] for part in parts), gains]
-    shape = (len(blocks), len(parts), rows, TILE_SIZE)
+        operands += [planes[0], planes[1], gains]
+    shape = (len(blocks), 2, rows, TILE_SIZE)
     return pl.pallas_call(
         cut_kernel,
         out_shape=jax.ShapeDtypeStruct(shape, jnp.bfloat16),
@@ -199,24 +197,13 @@
     def __init__(self, row_blocks, columns, absent=(), choice=None, pack=(), packed=(), splits=()):
         self.row_blocks, self.columns, self.absent = row_blocks, columns, list(absent)
         self.choice, self.pack, self.packed = choice, list(pack), list(packed)
-        self.planes, self.plane_bands = [], []
-        for plane in [] if packed else [p for planes, _ in row_blocks for p in planes]:
-            self.plane_bands.append([])
-            row = 0
-            for array in plane if isinstance(plane, tuple) else (plane,):
-                self.plane_bands[-1].append((len(self.planes), row, array.shape[0]))
-                self.planes.append(array)
-                row += array.shape[0]
+        self.planes = [] if packed else [p for planes, _ in row_blocks for p in planes]
         self.sources, self.source_at = [], []
         for pieces, *_ in columns:
-            apart = isinstance(pieces, tuple)
-            spots = []
-            for part, array in enumerate(pieces if apart else (pieces, pieces)):
-                if not any(array is source for source in self.sources):
-                    self.sources.append(array)
-                spots.append(([array is source for source in self.sources].index(True), 0 if apart else part))
-            self.source_at.append(spots)
-        self.rows = self.sources[0].shape[2]
+            if not any(pieces is source for source in self.sources):
+                self.sources.append(pieces)
+            self.source_at.append([pieces is source for source in self.sources].index(True))
+        self.rows = columns[0][0].shape[2]
         self.count = len(row_blocks)
         self.chunks = 1 if packed else 1 + max(column[3] for column in columns)
         bounds = [0, *splits, self.count]
@@ -279,9 +266,8 @@
         for at in self.members[chunk]:
             row = at * self.rows if self.packed else self.within(self.count + at)
             for part in range(2):
-                source, part_at = self.source_at[at][part]
                 pltpu.make_async_copy(
-                    self.source_refs[source].at[self.columns[at][1], part_at],
+                    self.source_refs[self.source_at[at]].at[self.columns[at][1], part],
                     self.right.at[chunk, part, pl.ds(row, self.rows), :],
                     self.right_sem.at[chunk],
                 ).start()
@@ -304,18 +290,15 @@
         inner = pl.ds(pl.multiple_of(self.start_row(chunk), self.chunk_depth), self.chunk_depth)
         for block in range(first, end):
             for part in range(2):
-                candidates = 1 if self.choice is None else len(self.plane_bands) // 2
+                here = self.left.at[chunk, part, pl.ds(block * rows, rows), :]
+                candidates = 1 if self.choice is None else len(self.planes) // 2
                 for at in range(candidates):
-                    for index, row, size in self.plane_bands[2 * (block + at) + part]:
-                        copy = pltpu.make_async_copy(
-                            self.plane_refs[index].at[:, inner],
-                            self.left.at[chunk, part, pl.ds(block * rows + row, size), :],
-                            sem,
-                        )
-                        if self.choice is None:
-                            copy.start()
-                        else:
-                            pl.when(self.number(len(self.numbers()) - 1) == at)(copy.start)
+                    ref = self.plane_refs[2 * (block + at) + part]
+                    copy = pltpu.make_async_copy(ref.at[:, inner], here, sem)
+                    if self.choice is None:
+                        copy.start()
+                    else:
+                        pl.when(self.number(len(self.numbers()) - 1) == at)(copy.start)
 
     def steps(self):
         return [(self, turn, chunk) for turn in range(len(self.turns)) for chunk in range(self.chunks)]
@@ -521,23 +504,20 @@
 
     columns = []
 
-    def exchange(held):
+    def spread(held, origins):
         held_by = [(held, 0)]
         bit = src_count // 2
         while bit:
             swap = [(i, i ^ bit) for i in range(src_count)]
             held_by += [(lax.ppermute(x, "src", swap), mask ^ bit) for x, mask in held_by]
             bit //= 2
-        return held_by
-
-    def note(held_by, origins):
         for pieces, mask in held_by:
             for index, first in enumerate(origins):
                 columns.append((pieces, index, (owner ^ mask) * span + first * rows, mask))
 
     def collect(blocks):
         tiles = tiles_of(blocks, mine)
-        note(exchange(tiles), [first for _, first in blocks])
+        spread(tiles, [first for _, first in blocks])
 
     blocks = transposed_blocks(data, devices)
     arrived = [
@@ -604,7 +584,7 @@
     across = [(order[i], order[(i + half) % rcv_count]) for i in range(rcv_count)]
     far_pieces = cut([(own, origin(0))], far, gains, device)
     far_pieces = lax.ppermute(far_pieces, "rcv", across)
-    note(exchange(far_pieces), [far])
+    spread(far_pieces, [far])
     early, late = columns[:late_from], columns[late_from:]
     absent = pack = [(c[2], c[3]) for c in late]
     jobs = [Job(as_rows(inside), early, absent, pack=pack)]
@@ -614,10 +594,8 @@
         for d in (-1, 1)
     ]
     last = []
-    for part in range(2):
-        upper = lax.ppermute(ahead[part][: rows // 2], "rcv", turns[0])
-        lower = lax.ppermute(behind[part][rows // 2 :], "rcv", turns[1])
-        last.append((upper, lower))
+    for part, plane in enumerate((ahead[0], behind[1])):
+        last.append(lax.ppermute(plane, "rcv", turns[part]))
     jobs = [Job(as_rows(outside), early, absent, pack=pack)]
     out, packed_outside = launch(device, out, jobs, used, span, total)
     chosen = np.zeros(devices)
@@ -627,9 +605,10 @@
     candidates = (*last, *taken[0], *taken[1])
     packed = [(packed_inside, len(inside)), (packed_outside, len(outside))]
     splits = [len(inside) // 2, len(inside)]
-    near_rows = Job(as_rows(inside + outside), late, packed=packed, splits=splits)
-    far_rows = Job([(candidates, far * rows)], columns, choice=chosen)
-    return launch(device, out, [near_rows, far_rows], used, span, total)[0]
+    jobs = [Job(as_rows(inside + outside), late, packed=packed, splits=splits)]
+    out = launch(device, out, jobs, used, span, total)[0]
+    jobs = [Job([(candidates, far * rows)], columns, choice=chosen)]
+    return launch(device, out, jobs, used, span, total)[0]
 
 
 def solution(mesh):

time: 310 us -> 327 us (1.055)
  the two profiles are of different devices: /device:TPU:18 before, /device:TPU:10 now
where the time goes in v2:
time: 327 us; the launch traced here: 325 us
  waiting for transfers between devices  182 us (56%)
  Pallas kernels  72.9 us (22%)
  starting transfers between devices  34.4 us (11%)
  blocking collectives  30.3 us (9%)
  local copies, waits for them, and re-layouts  3.61 us (1%)
    ppermute x1, waiting for transfers between devices, local(): far_pieces = lax.ppermute(far_pieces, 'rcv', across)  51.1 us
    pallas_call x4, Pallas kernels, launch(): pl.pallas_call(kernel, out_shape=out_shape, grid_spec=pltpu.PrefetchScala...  46.1 us
    all_to_all x1, blocking collectives, local(): lax.all_to_all(b, ('src', 'rcv'), split_axis=0, concat_axis=0, tiled=True)  30.3 us
    ppermute x2, waiting for transfers between devices, local(): ahead.append(lax.ppermute(own[part], 'rcv', forward))  29 us
    ppermute x15, waiting for transfers between devices, spread(): lax.ppermute(x, 'src', swap)  27.9 us
    ppermute x4, waiting for transfers between devices, local(): moved.append(lax.ppermute(ahead[part], 'rcv', forward))  21.2 us
    all_to_all x1, waiting for transfers between devices, local(): lax.all_to_all(b, ('src', 'rcv'), split_axis=0, concat_axis=0, tiled=True)  19.6 us
    ppermute x2, waiting for transfers between devices, local(): behind.append(lax.ppermute(own[part], 'rcv', backward))  16.7 us
  transfers between devices with their start and end apart: 35, of which 14 were waited for; matrix products, arithmetic and copies ran while one was open for 1% of the time, Pallas kernels for 19%

profile of v2, /device:TPU:10, one launch (start us, length us, event | category | flops | bytes accessed | tf_op | source)
XLA Modules:
  0.0 325.2 jit_solution(11106885476340566563)
XLA Ops:
  0.0 3.9 %shard_map.139 = (bf16[32,128,128]{2,1,0:T(8,128)(2,1)}, bf16[32,128,128]{2,1,0:T(8,128)(2,1)}) custom-call(bf16[2,128,4096]{2,1,0:T(8,128)(2,1)} %data_ref.5), custom_call_target="tpu_custom_call" | custom-call | tf_op jit(solution)/shard_map/pallas_call | solution.py:30
  3.9 30.3 %all_to_all.10.arrived_ref = bf16[32,128,128]{2,1,0:T(8,128)(2,1)} all-to-all(bf16[32,128,128]{2,1,0:T(8,128)(2,1)} %get-tuple-element.11), channel_id=1, replica_groups=mesh['src'=4,'rcv'=8] {'src','rcv'}, dimensions={0} | all-to-all | bytes 2097152 | tf_op jit(solution)/shard_map/all_to_all | solution.py:524
  34.2 5.9 %all-to-all-start.1 = ((bf16[32,128,128]{2,1,0:T(8,128)(2,1)}), bf16[32,128,128]{2,1,0:T(8,128)(2,1)S(1)}, u32[]{:S(2)}, u32[]{:S(2)}) async-start(bf16[32,128,128]{2,1,0:T(8,128)(2,1)} %get-tuple-element.12), calls=%async_computation.1 | async-start | bytes 2097152 | tf_op jit(solution)/shard_map/all_to_all | solution.py:524
  40.1 4.2 %shard_map.140.refs_0_ = bf16[128,4096]{1,0:T(8,128)(2,1)} custom-call(bf16[2,128,4096]{2,1,0:T(8,128)(2,1)} %data_ref.5, s32[128,4096]{1,0:T(8,128)} %mask_ref.3, bf16[32,128,128]{2,1,0:T(8,128)(2,1)} %all_to_all.10.arrived_ref), custom_call_target="tpu_custom_call" | custom-call | tf_op jit(solution)/shard_map/pallas_call | solution.py:55
  44.8 19.6 %all-to-all-done.1.arrived_ref = bf16[32,128,128]{2,1,0:T(8,128)(2,1)S(1)} async-done(((bf16[32,128,128]{2,1,0:T(8,128)(2,1)}), bf16[32,128,128]{2,1,0:T(8,128)(2,1)S(1)}, u32[]{:S(2)}, u32[]{:S(2)}) %all-to-all-start.1) | async-done | bytes 1048608 | tf_op jit(solution)/shard_map/all_to_all | solution.py:524
  65.3 4.1 %shard_map.141.refs_1_ = bf16[128,4096]{1,0:T(8,128)(2,1)} custom-call(bf16[2,128,4096]{2,1,0:T(8,128)(2,1)} %data_ref.5, s32[128,4096]{1,0:T(8,128)} %mask_ref.3, bf16[32,128,128]{2,1,0:T(8,128)(2,1)} %copy-done.2), custom_call_target="tpu_custom_call" | custom-call | tf_op jit(solution)/shard_map/pallas_call | solution.py:55
  72.8 15.4 %collective-permute-done.refs_0_.refs_2_ = bf16[128,4096]{1,0:T(8,128)(2,1)S(1)} collective-permute-done((bf16[128,4096]{1,0:T(8,128)(2,1)}, bf16[128,4096]{1,0:T(8,128)(2,1)S(1)}, u32[]{:S(2)}, u32[]{:S(2)}) %collective-permute-start) | collective-permute-done | bytes 1048608 | tf_op jit(solution)/shard_map/ppermute | solution.py:529
  88.2 8.4 %collective-permute-done.4.refs_4_.refs_5_ = bf16[128,4096]{1,0:T(8,128)(2,1)} collective-permute-done((bf16[128,4096]{1,0:T(8,128)(2,1)}, bf16[128,4096]{1,0:T(8,128)(2,1)}, u32[]{:S(2)}, u32[]{:S(2)}) %collective-permute-start.4) | collective-permute-done | bytes 1048608 | tf_op jit(solution)/shard_map/ppermute | solution.py:530
  97.2 13.6 %collective-permute-done.9.refs_1_.refs_3_ = bf16[128,4096]{1,0:T(8,128)(2,1)} collective-permute-done((bf16[128,4096]{1,0:T(8,128)(2,1)}, bf16[128,4096]{1,0:T(8,128)(2,1)}, u32[]{:S(2)}, u32[]{:S(2)}) %collective-permute-start.9) | collective-permute-done | bytes 1048608 | tf_op jit(solution)/shard_map/ppermute | solution.py:529
  110.8 8.3 %collective-permute-done.11.refs_3_.refs_4_ = bf16[128,4096]{1,0:T(8,128)(2,1)} collective-permute-done((bf16[128,4096]{1,0:T(8,128)(2,1)S(1)}, bf16[128,4096]{1,0:T(8,128)(2,1)}, u32[]{:S(2)}, u32[]{:S(2)}) %collective-permute-start.11) | collective-permute-done | bytes 1048608 | tf_op jit(solution)/shard_map/ppermute | solution.py:530
  121.3 2.7 shard_map.142.refs_10_.refs_4_.refs_6_
  125.7 7.6 %collective-permute-done.1.refs_0_.refs_6_ = bf16[128,4096]{1,0:T(8,128)(2,1)} collective-permute-done((bf16[128,4096]{1,0:T(8,128)(2,1)S(1)}, bf16[128,4096]{1,0:T(8,128)(2,1)}, u32[]{:S(2)}, u32[]{:S(2)}) %collective-permute-start.1) | collective-permute-done | bytes 1048608 | tf_op jit(solution)/shard_map/ppermute | solution.py:577
  133.3 8.3 %collective-permute-done.5.refs_4_.refs_9_ = bf16[128,4096]{1,0:T(8,128)(2,1)} collective-permute-done((bf16[128,4096]{1,0:T(8,128)(2,1)}, bf16[128,4096]{1,0:T(8,128)(2,1)}, u32[]{:S(2)}, u32[]{:S(2)}) %collective-permute-start.5) | collective-permute-done | bytes 1048608 | tf_op jit(solution)/shard_map/ppermute | solution.py:578
  142.1 13.6 %collective-permute-done.20.refs_1_.refs_7_ = bf16[128,4096]{1,0:T(8,128)(2,1)} collective-permute-done((bf16[128,4096]{1,0:T(8,128)(2,1)}, bf16[128,4096]{1,0:T(8,128)(2,1)}, u32[]{:S(2)}, u32[]{:S(2)}) %collective-permute-start.20) | collective-permute-done | bytes 1048608 | tf_op jit(solution)/shard_map/ppermute | solution.py:577
  155.7 8.2 %collective-permute-done.21.refs_3_.refs_8_ = bf16[128,4096]{1,0:T(8,128)(2,1)S(1)} collective-permute-done((bf16[128,4096]{1,0:T(8,128)(2,1)}, bf16[128,4096]{1,0:T(8,128)(2,1)S(1)}, u32[]{:S(2)}, u32[]{:S(2)}) %collective-permute-start.21) | collective-permute-done | bytes 1048608 | tf_op jit(solution)/shard_map/ppermute | solution.py:578
  164.5 2.7 shard_map.146
  167.2 2.5 collective-permute-start.30
  169.7 51.1 %collective-permute-done.30.refs_4_.refs_22_ = bf16[1,2,128,512]{3,2,1,0:T(8,128)(2,1)} collective-permute-done((bf16[1,2,128,512]{3,2,1,0:T(8,128)(2,1)}, bf16[1,2,128,512]{3,2,1,0:T(8,128)(2,1)}, u32[]{:S(2)}, u32[]{:S(2)}) %collective-permute-start.30) | collective-permute-done | bytes 262176 | tf_op jit(solution)/shard_map/ppermute | solution.py:586
  221.3 3.0 shard_map.143.refs_14_.refs_8_.refs_10_
  224.3 4.7 %collective-permute-done.31.refs_5_.refs_23_ = bf16[1,2,128,512]{3,2,1,0:T(8,128)(2,1)} collective-permute-done((bf16[1,2,128,512]{3,2,1,0:T(8,128)(2,1)}, bf16[1,2,128,512]{3,2,1,0:T(8,128)(2,1)}, u32[]{:S(2)}, u32[]{:S(2)}) %collective-permute-start.31) | collective-permute-done | bytes 262176 | tf_op jit(solution)/shard_map/ppermute | solution.py:512
  230.5 3.0 shard_map.144.refs_18_.refs_12_.refs_14_
  233.6 3.2 shard_map.145.refs_0_.refs_18_
  239.8 2.5 collective-permute-done.17.refs_15_.refs_9_.refs_11_
  242.9 10.7 %collective-permute-done.22.refs_19_.refs_13_.refs_15_ = bf16[2,2,128,512]{3,2,1,0:T(8,128)(2,1)} collective-permute-done((bf16[2,2,128,512]{3,2,1,0:T(8,128)(2,1)S(1)}, bf16[2,2,128,512]{3,2,1,0:T(8,128)(2,1)}, u32[]{:S(2)}, u32[]{:S(2)}) %collective-permute-start.22) | collective-permute-done | bytes 524320 | tf_op jit(solution)/shard_map/ppermute | solution.py:512
  254.5 9.9 %collective-permute-done.27.refs_1_.refs_19_ = bf16[2,2,128,512]{3,2,1,0:T(8,128)(2,1)} collective-permute-done((bf16[2,2,128,512]{3,2,1,0:T(8,128)(2,1)}, bf16[2,2,128,512]{3,2,1,0:T(8,128)(2,1)}, u32[]{:S(2)}, u32[]{:S(2)}) %collective-permute-start.27) | collective-permute-done | bytes 524320 | tf_op jit(solution)/shard_map/ppermute | solution.py:512
  267.8 5.7 %collective-permute-start.8 = (bf16[128,4096]{1,0:T(8,128)(2,1)}, bf16[128,4096]{1,0:T(8,128)(2,1)}, u32[]{:S(2)}, u32[]{:S(2)}) collective-permute-start(bf16[128,4096]{1,0:T(8,128)(2,1)} %copy-done.9), channel_id=1, source_target_pairs={{3,2},{4,5},{11,10},{12,13},{19,18},{20,21},{27,26},{28,29}} | collective-permute-start | bytes 3145736 | tf_op jit(solution)/shard_map/ppermute | solution.py:488
  273.5 2.3 collective-permute-start.3
  275.8 1.7 collective-permute-start.7
  277.5 18.3 %shard_map.147 = (f32[2,1024,512]{2,1,0:T(8,128)}, bf16[2,640,1536]{2,1,0:T(8,128)(2,1)}) custom-call(s32[1]{0:T(128)} %bitcast.device_ref, s32[32,49]{1,0:T(8,128)} %constant.45.clone.plan_ref, s32[2,8]{1,0:T(2,128)} %convert_element_type.3.used_ref, bf16[128,4096]{1,0:T(8,128)(2,1)} %shard_map.140.refs_0_, bf16[128,4096]{1,0:T(8,128)(2,1)} %shard_map.141.refs_1_, ...), custom_call_target="tpu_custom_call" | custom-call | flops 10737418240 | bytes 83886080 | tf_op jit(solution)/shard_map/pallas_call | solution.py:437
  295.8 9.5 %shard_map.148 = (f32[2,1024,512]{2,1,0:T(8,128)}, bf16[2,256,1536]{2,1,0:T(8,128)(2,1)}) custom-call(s32[1]{0:T(128)} %bitcast.device_ref, s32[32,46]{1,0:T(8,128)} %constant.46.clone.plan_ref, s32[2,8]{1,0:T(2,128)} %convert_element_type.3.used_ref, bf16[128,4096]{1,0:T(8,128)(2,1)} %collective-permute-done.2.refs_0_, ...), custom_call_target="tpu_custom_call", output_to_operand_aliasing={{0}: (19, {})} | custom-call | flops 4294967296 | bytes 83886080 | tf_op jit(solution)/shard_map/pallas_call | solution.py:437
  305.4 11.1 %shard_map.149.refs_26_ = f32[2,1024,512]{2,1,0:T(8,128)} custom-call(s32[1]{0:T(128)} %bitcast.device_ref, s32[32,19]{1,0:T(8,128)} %constant.47.clone.plan_ref, s32[2,8]{1,0:T(2,128)} %convert_element_type.3.used_ref, bf16[2,2,128,512]{3,2,1,0:T(8,128)(2,1)} %shard_map.145.refs_0_.refs_18_, ...), custom_call_target="tpu_custom_call", output_to_operand_aliasing={{}: (13, {})} | custom-call | flops 5637144576 | bytes 83886080 | tf_op jit(solution)/shard_map/pallas_call | solution.py:437
  317.8 7.2 %shard_map.150 = f32[2,1024,512]{2,1,0:T(8,128)} custom-call(s32[1]{0:T(128)} %bitcast.device_ref, s32[32,34]{1,0:T(8,128)} %constant.48.clone.plan_ref, s32[2,8]{1,0:T(2,128)} %convert_element_type.3.used_ref, bf16[128,4096]{1,0:T(8,128)(2,1)} %collective-permute-done.3.refs_0_, ...), custom_call_target="tpu_custom_call", output_to_operand_aliasing={{}: (29, {})} | custom-call | flops 2147483648 | bytes 83886080 | tf_op jit(solution)/shard_map/pallas_call | solution.py:437
  (95 shorter events, 21.5 us)
Async XLA Ops:
  34.2 30.1 %all-to-all-start.1 = ((bf16[32,128,128]{2,1,0:T(8,128)(2,1)}), bf16[32,128,128]{2,1,0:T(8,128)(2,1)S(1)}, u32[]{:S(2)}, u32[]{:S(2)}) async-start(bf16[32,128,128]{2,1,0:T(8,128)(2,1)} %get-tuple-element.12), calls=%async_computation.1 | async-start | bytes 2097152 | tf_op jit(solution)/shard_map/all_to_all | solution.py:524
  44.3 43.9 %collective-permute-start = (bf16[128,4096]{1,0:T(8,128)(2,1)}, bf16[128,4096]{1,0:T(8,128)(2,1)S(1)}, u32[]{:S(2)}, u32[]{:S(2)}) collective-permute-start(bf16[128,4096]{1,0:T(8,128)(2,1)} %shard_map.140.refs_0_), channel_id=1, source_target_pairs={{0,2},{2,4},{4,6},{6,7},{7,5},{5,3},{3,1},{1,0},{8,10},{10,12},{12... | collective-permute-start | bytes 3145736 | tf_op jit(solution)/shard_map/ppermute | solution.py:529
  69.4 27.2 %collective-permute-start.4 = (bf16[128,4096]{1,0:T(8,128)(2,1)}, bf16[128,4096]{1,0:T(8,128)(2,1)}, u32[]{:S(2)}, u32[]{:S(2)}) collective-permute-start(bf16[128,4096]{1,0:T(8,128)(2,1)} %shard_map.141.refs_1_), channel_id=1, source_target_pairs={{2,0},{4,2},{6,4},{7,6},{5,7},{3,5},{1,3},{0,1},{10,8},{12,10},{14... | collective-permute-start | bytes 3145736 | tf_op jit(solution)/shard_map/ppermute | solution.py:530
  70.8 40.0 %collective-permute-start.9 = (bf16[128,4096]{1,0:T(8,128)(2,1)}, bf16[128,4096]{1,0:T(8,128)(2,1)}, u32[]{:S(2)}, u32[]{:S(2)}) collective-permute-start(bf16[128,4096]{1,0:T(8,128)(2,1)} %shard_map.141.refs_1_), channel_id=1, source_target_pairs={{0,2},{2,4},{4,6},{6,7},{7,5},{5,3},{3,1},{1,0},{8,10},{10,12},{12... | collective-permute-start | bytes 3145736 | tf_op jit(solution)/shard_map/ppermute | solution.py:529
  72.3 46.8 %collective-permute-start.11 = (bf16[128,4096]{1,0:T(8,128)(2,1)S(1)}, bf16[128,4096]{1,0:T(8,128)(2,1)}, u32[]{:S(2)}, u32[]{:S(2)}) collective-permute-start(bf16[128,4096]{1,0:T(8,128)(2,1)S(1)} %copy-done.1), channel_id=1, source_target_pairs={{2,0},{4,2},{6,4},{7,6},{5,7},{3,5},{1,3},{0,1},{10,8},{12,10},{14... | collective-permute-start | bytes 3145736 | tf_op jit(solution)/shard_map/ppermute | solution.py:530
  88.2 45.0 %collective-permute-start.1 = (bf16[128,4096]{1,0:T(8,128)(2,1)S(1)}, bf16[128,4096]{1,0:T(8,128)(2,1)}, u32[]{:S(2)}, u32[]{:S(2)}) collective-permute-start(bf16[128,4096]{1,0:T(8,128)(2,1)S(1)} %collective-permute-done.refs_0_.refs_2_), channel_id=1, source_target_pairs={{0,2},{2,4},{4,6},{6,7},{7,5},{5,3},{3,1},{1,0},{8,10},{10,12},{12... | collective-permute-start | bytes 3145736 | tf_op jit(solution)/shard_map/ppermute | solution.py:577
  96.7 44.9 %collective-permute-start.5 = (bf16[128,4096]{1,0:T(8,128)(2,1)}, bf16[128,4096]{1,0:T(8,128)(2,1)}, u32[]{:S(2)}, u32[]{:S(2)}) collective-permute-start(bf16[128,4096]{1,0:T(8,128)(2,1)} %collective-permute-done.4.refs_4_.refs_5_), channel_id=1, source_target_pairs={{2,0},{4,2},{6,4},{7,6},{5,7},{3,5},{1,3},{0,1},{10,8},{12,10},{14... | collective-permute-start | bytes 3145736 | tf_op jit(solution)/shard_map/ppermute | solution.py:578
  110.8 44.9 %collective-permute-start.20 = (bf16[128,4096]{1,0:T(8,128)(2,1)}, bf16[128,4096]{1,0:T(8,128)(2,1)}, u32[]{:S(2)}, u32[]{:S(2)}) collective-permute-start(bf16[128,4096]{1,0:T(8,128)(2,1)} %collective-permute-done.9.refs_1_.refs_3_), channel_id=1, source_target_pairs={{0,2},{2,4},{4,6},{6,7},{7,5},{5,3},{3,1},{1,0},{8,10},{10,12},{12... | collective-permute-start | bytes 3145736 | tf_op jit(solution)/shard_map/ppermute | solution.py:577
  119.1 44.8 %collective-permute-start.21 = (bf16[128,4096]{1,0:T(8,128)(2,1)}, bf16[128,4096]{1,0:T(8,128)(2,1)S(1)}, u32[]{:S(2)}, u32[]{:S(2)}) collective-permute-start(bf16[128,4096]{1,0:T(8,128)(2,1)} %collective-permute-done.11.refs_3_.refs_4_), channel_id=1, source_target_pairs={{2,0},{4,2},{6,4},{7,6},{5,7},{3,5},{1,3},{0,1},{10,8},{12,10},{14... | collective-permute-start | bytes 3145736 | tf_op jit(solution)/shard_map/ppermute | solution.py:578
  124.1 43.1 %collective-permute-start.14 = (bf16[1,2,128,512]{3,2,1,0:T(8,128)(2,1)}, bf16[1,2,128,512]{3,2,1,0:T(8,128)(2,1)S(1)}, u32[]{:S(2)}, u32[]{:S(2)}) collective-permute-start(bf16[1,2,128,512]{3,2,1,0:T(8,128)(2,1)} %shard_map.142.refs_10_.refs_4_.refs_6_), channel_id=1, source_target_pairs={{0,16},{8,24},{16,0},{24,8},{1,17},{9,25},{17,1},{25,9},{2,18},{10... | collective-permute-start | bytes 786440 | tf_op jit(solution)/shard_map/ppermute | solution.py:512
  133.3 96.2 %collective-permute-start.2 = (bf16[128,4096]{1,0:T(8,128)(2,1)}, bf16[128,4096]{1,0:T(8,128)(2,1)}, u32[]{:S(2)}, u32[]{:S(2)}) collective-permute-start(bf16[128,4096]{1,0:T(8,128)(2,1)} %collective-permute-done.1.refs_0_.refs_6_), channel_id=1, source_target_pairs={{0,2},{2,4},{4,6},{6,7},{7,5},{5,3},{3,1},{1,0},{8,10},{10,12},{12... | collective-permute-start | bytes 3145736 | tf_op jit(solution)/shard_map/ppermute | solution.py:577
  141.6 87.9 %collective-permute-start.6 = (bf16[128,4096]{1,0:T(8,128)(2,1)}, bf16[128,4096]{1,0:T(8,128)(2,1)}, u32[]{:S(2)}, u32[]{:S(2)}) collective-permute-start(bf16[128,4096]{1,0:T(8,128)(2,1)} %collective-permute-done.5.refs_4_.refs_9_), channel_id=1, source_target_pairs={{2,0},{4,2},{6,4},{7,6},{5,7},{3,5},{1,3},{0,1},{10,8},{12,10},{14... | collective-permute-start | bytes 3145736 | tf_op jit(solution)/shard_map/ppermute | solution.py:578
  155.7 74.3 %collective-permute-start.25 = (bf16[128,4096]{1,0:T(8,128)(2,1)}, bf16[128,4096]{1,0:T(8,128)(2,1)}, u32[]{:S(2)}, u32[]{:S(2)}) collective-permute-start(bf16[128,4096]{1,0:T(8,128)(2,1)} %collective-permute-done.20.refs_1_.refs_7_), channel_id=1, source_target_pairs={{0,2},{2,4},{4,6},{6,7},{7,5},{5,3},{3,1},{1,0},{8,10},{10,12},{12... | collective-permute-start | bytes 3145736 | tf_op jit(solution)/shard_map/ppermute | solution.py:577
  164.0 66.2 %collective-permute-start.26 = (bf16[128,4096]{1,0:T(8,128)(2,1)S(1)}, bf16[128,4096]{1,0:T(8,128)(2,1)}, u32[]{:S(2)}, u32[]{:S(2)}) collective-permute-start(bf16[128,4096]{1,0:T(8,128)(2,1)S(1)} %collective-permute-done.21.refs_3_.refs_8_), channel_id=1, source_target_pairs={{2,0},{4,2},{6,4},{7,6},{5,7},{3,5},{1,3},{0,1},{10,8},{12,10},{14... | collective-permute-start | bytes 3145736 | tf_op jit(solution)/shard_map/ppermute | solution.py:578
  167.2 53.6 %collective-permute-start.30 = (bf16[1,2,128,512]{3,2,1,0:T(8,128)(2,1)}, bf16[1,2,128,512]{3,2,1,0:T(8,128)(2,1)}, u32[]{:S(2)}, u32[]{:S(2)}) collective-permute-start(bf16[1,2,128,512]{3,2,1,0:T(8,128)(2,1)} %shard_map.146), channel_id=1, source_target_pairs={{0,7},{2,5},{4,3},{6,1},{7,0},{5,2},{3,4},{1,6},{8,15},{10,13},{12... | collective-permute-start | bytes 786440 | tf_op jit(solution)/shard_map/ppermute | solution.py:586
  229.0 13.4 %collective-permute-start.17 = (bf16[2,2,128,512]{3,2,1,0:T(8,128)(2,1)}, bf16[2,2,128,512]{3,2,1,0:T(8,128)(2,1)S(1)}, u32[]{:S(2)}, u32[]{:S(2)}) collective-permute-start(bf16[2,2,128,512]{3,2,1,0:T(8,128)(2,1)} %shard_map.143.refs_14_.refs_8_.refs_10_), channel_id=1, source_target_pairs={{0,16},{8,24},{16,0},{24,8},{1,17},{9,25},{17,1},{25,9},{2,18},{10... | collective-permute-start | bytes 1572872 | tf_op jit(solution)/shard_map/ppermute | solution.py:512
  229.5 8.6 %collective-permute-start.16 = (bf16[1,2,128,512]{3,2,1,0:T(8,128)(2,1)S(1)}, bf16[1,2,128,512]{3,2,1,0:T(8,128)(2,1)S(1)}, u32[]{:S(2)}, u32[]{:S(2)}) collective-permute-start(bf16[1,2,128,512]{3,2,1,0:T(8,128)(2,1)S(1)} %collective-permute-done.14.refs_11_.refs_5_.refs_7_), channel_id=1, source_target_pairs={{0,8},{8,0},{16,24},{24,16},{1,9},{9,1},{17,25},{25,17},{2,10},{10... | collective-permute-start | bytes 786440 | tf_op jit(solution)/shard_map/ppermute | solution.py:512
  230.0 8.3 %collective-permute-start.32 = (bf16[1,2,128,512]{3,2,1,0:T(8,128)(2,1)}, bf16[1,2,128,512]{3,2,1,0:T(8,128)(2,1)}, u32[]{:S(2)}, u32[]{:S(2)}) collective-permute-start(bf16[1,2,128,512]{3,2,1,0:T(8,128)(2,1)} %collective-permute-done.30.refs_4_.refs_22_), channel_id=1, source_target_pairs={{0,8},{8,0},{16,24},{24,16},{1,9},{9,1},{17,25},{25,17},{2,10},{10... | collective-permute-start | bytes 786440 | tf_op jit(solution)/shard_map/ppermute | solution.py:512
  230.1 12.2 %collective-permute-start.33 = (bf16[1,2,128,512]{3,2,1,0:T(8,128)(2,1)}, bf16[1,2,128,512]{3,2,1,0:T(8,128)(2,1)}, u32[]{:S(2)}, u32[]{:S(2)}) collective-permute-start(bf16[1,2,128,512]{3,2,1,0:T(8,128)(2,1)} %collective-permute-done.31.refs_5_.refs_23_), channel_id=1, source_target_pairs={{0,8},{8,0},{16,24},{24,16},{1,9},{9,1},{17,25},{25,17},{2,10},{10... | collective-permute-start | bytes 786440 | tf_op jit(solution)/shard_map/ppermute | solution.py:512
  236.8 28.4 %collective-permute-start.10 = (bf16[128,4096]{1,0:T(8,128)(2,1)}, bf16[128,4096]{1,0:T(8,128)(2,1)S(1)}, u32[]{:S(2)}, u32[]{:S(2)}) collective-permute-start(bf16[128,4096]{1,0:T(8,128)(2,1)} %collective-permute-done.9.refs_1_.refs_3_), channel_id=1, source_target_pairs={{3,2},{4,5},{11,10},{12,13},{19,18},{20,21},{27,26},{28,29}} | collective-permute-start | bytes 3145736 | tf_op jit(solution)/shard_map/ppermute | solution.py:488
  238.3 15.4 %collective-permute-start.22 = (bf16[2,2,128,512]{3,2,1,0:T(8,128)(2,1)S(1)}, bf16[2,2,128,512]{3,2,1,0:T(8,128)(2,1)}, u32[]{:S(2)}, u32[]{:S(2)}) collective-permute-start(bf16[2,2,128,512]{3,2,1,0:T(8,128)(2,1)S(1)} %copy-done.4), channel_id=1, source_target_pairs={{0,16},{8,24},{16,0},{24,8},{1,17},{9,25},{17,1},{25,9},{2,18},{10... | collective-permute-start | bytes 1572872 | tf_op jit(solution)/shard_map/ppermute | solution.py:512
  242.3 11.3 %collective-permute-start.19 = (bf16[2,2,128,512]{3,2,1,0:T(8,128)(2,1)S(1)}, bf16[2,2,128,512]{3,2,1,0:T(8,128)(2,1)S(1)}, u32[]{:S(2)}, u32[]{:S(2)}) collective-permute-start(bf16[2,2,128,512]{3,2,1,0:T(8,128)(2,1)S(1)} %collective-permute-done.17.refs_15_.refs_9_.refs_11_), channel_id=1, source_target_pairs={{0,8},{8,0},{16,24},{24,16},{1,9},{9,1},{17,25},{25,17},{2,10},{10... | collective-permute-start | bytes 1572872 | tf_op jit(solution)/shard_map/ppermute | solution.py:512
  242.3 22.1 %collective-permute-start.27 = (bf16[2,2,128,512]{3,2,1,0:T(8,128)(2,1)}, bf16[2,2,128,512]{3,2,1,0:T(8,128)(2,1)}, u32[]{:S(2)}, u32[]{:S(2)}) collective-permute-start(bf16[2,2,128,512]{3,2,1,0:T(8,128)(2,1)} %shard_map.145.refs_0_.refs_18_), channel_id=1, source_target_pairs={{0,16},{8,24},{16,0},{24,8},{1,17},{9,25},{17,1},{25,9},{2,18},{10... | collective-permute-start | bytes 1572872 | tf_op jit(solution)/shard_map/ppermute | solution.py:512
  242.4 24.1 %collective-permute-start.23 = (bf16[2,2,128,512]{3,2,1,0:T(8,128)(2,1)S(1)}, bf16[2,2,128,512]{3,2,1,0:T(8,128)(2,1)S(1)}, u32[]{:S(2)}, u32[]{:S(2)}) collective-permute-start(bf16[2,2,128,512]{3,2,1,0:T(8,128)(2,1)S(1)} %copy-done.4), channel_id=1, source_target_pairs={{0,8},{8,0},{16,24},{24,16},{1,9},{9,1},{17,25},{25,17},{2,10},{10... | collective-permute-start | bytes 1572872 | tf_op jit(solution)/shard_map/ppermute | solution.py:512
  253.7 14.2 %collective-permute-start.24 = (bf16[2,2,128,512]{3,2,1,0:T(8,128)(2,1)}, bf16[2,2,128,512]{3,2,1,0:T(8,128)(2,1)}, u32[]{:S(2)}, u32[]{:S(2)}) collective-permute-start(bf16[2,2,128,512]{3,2,1,0:T(8,128)(2,1)} %collective-permute-done.22.refs_19_.refs_13_.refs_15_), channel_id=1, source_target_pairs={{0,8},{8,0},{16,24},{24,16},{1,9},{9,1},{17,25},{25,17},{2,10},{10... | collective-permute-start | bytes 1572872 | tf_op jit(solution)/shard_map/ppermute | solution.py:512
  253.7 19.8 %collective-permute-start.28 = (bf16[2,2,128,512]{3,2,1,0:T(8,128)(2,1)}, bf16[2,2,128,512]{3,2,1,0:T(8,128)(2,1)}, u32[]{:S(2)}, u32[]{:S(2)}) collective-permute-start(bf16[2,2,128,512]{3,2,1,0:T(8,128)(2,1)} %shard_map.145.refs_0_.refs_18_), channel_id=1, source_target_pairs={{0,8},{8,0},{16,24},{24,16},{1,9},{9,1},{17,25},{25,17},{2,10},{10... | collective-permute-start | bytes 1572872 | tf_op jit(solution)/shard_map/ppermute | solution.py:512
  264.4 11.4 %collective-permute-start.29 = (bf16[2,2,128,512]{3,2,1,0:T(8,128)(2,1)}, bf16[2,2,128,512]{3,2,1,0:T(8,128)(2,1)}, u32[]{:S(2)}, u32[]{:S(2)}) collective-permute-start(bf16[2,2,128,512]{3,2,1,0:T(8,128)(2,1)} %collective-permute-done.27.refs_1_.refs_19_), channel_id=1, source_target_pairs={{0,8},{8,0},{16,24},{24,16},{1,9},{9,1},{17,25},{25,17},{2,10},{10... | collective-permute-start | bytes 1572872 | tf_op jit(solution)/shard_map/ppermute | solution.py:512
  265.2 51.3 %collective-permute-start.12 = (bf16[128,4096]{1,0:T(8,128)(2,1)}, bf16[128,4096]{1,0:T(8,128)(2,1)S(1)}, u32[]{:S(2)}, u32[]{:S(2)}) collective-permute-start(bf16[128,4096]{1,0:T(8,128)(2,1)} %collective-permute-done.11.refs_3_.refs_4_), channel_id=1, source_target_pairs={{5,4},{2,3},{13,12},{10,11},{21,20},{18,19},{29,28},{26,27}} | collective-permute-start | bytes 3145736 | tf_op jit(solution)/shard_map/ppermute | solution.py:488
  266.5 50.0 %collective-permute-start.13 = (bf16[128,4096]{1,0:T(8,128)(2,1)}, bf16[128,4096]{1,0:T(8,128)(2,1)S(1)}, u32[]{:S(2)}, u32[]{:S(2)}) collective-permute-start(bf16[128,4096]{1,0:T(8,128)(2,1)} %collective-permute-done.4.refs_4_.refs_5_), channel_id=1, source_target_pairs={{5,4},{2,3},{13,12},{10,11},{21,20},{18,19},{29,28},{26,27}} | collective-permute-start | bytes 3145736 | tf_op jit(solution)/shard_map/ppermute | solution.py:488
  267.8 48.7 %collective-permute-start.8 = (bf16[128,4096]{1,0:T(8,128)(2,1)}, bf16[128,4096]{1,0:T(8,128)(2,1)}, u32[]{:S(2)}, u32[]{:S(2)}) collective-permute-start(bf16[128,4096]{1,0:T(8,128)(2,1)} %copy-done.9), channel_id=1, source_target_pairs={{3,2},{4,5},{11,10},{12,13},{19,18},{20,21},{27,26},{28,29}} | collective-permute-start | bytes 3145736 | tf_op jit(solution)/shard_map/ppermute | solution.py:488
  273.5 43.0 %collective-permute-start.3 = (bf16[128,4096]{1,0:T(8,128)(2,1)}, bf16[128,4096]{1,0:T(8,128)(2,1)}, u32[]{:S(2)}, u32[]{:S(2)}) collective-permute-start(bf16[128,4096]{1,0:T(8,128)(2,1)} %collective-permute-done.2.refs_0_), channel_id=1, source_target_pairs={{1,0},{4,6},{6,7},{3,1},{9,8},{12,14},{14,15},{11,9},{17,16},{20,2... | collective-permute-start | bytes 3145736 | tf_op jit(solution)/shard_map/ppermute | solution.py:598
  275.8 40.8 %collective-permute-start.7 = (bf16[128,4096]{1,0:T(8,128)(2,1)}, bf16[128,4096]{1,0:T(8,128)(2,1)}, u32[]{:S(2)}, u32[]{:S(2)}) collective-permute-start(bf16[128,4096]{1,0:T(8,128)(2,1)} %collective-permute-done.6.refs_4_.refs_3_), channel_id=1, source_target_pairs={{2,0},{7,6},{5,7},{0,1},{10,8},{15,14},{13,15},{8,9},{18,16},{23,2... | collective-permute-start | bytes 3145736 | tf_op jit(solution)/shard_map/ppermute | solution.py:598
  (22 other events, 852.9 us)

commit v3 on v1

--- a/solution.py
+++ b/solution.py
@@ -601,10 +601,13 @@
     taken = [hop(rows_of[offset][0], from_mate(offset)) for offset in (-1, 1)]
     late_from = len(columns)
     collect([rows_of[-steps], rows_of[steps]])
-    across = [(order[i], order[(i + half) % rcv_count]) for i in range(rcv_count)]
-    far_pieces = cut([(own, origin(0))], far, gains, device)
-    far_pieces = lax.ppermute(far_pieces, "rcv", across)
-    note(exchange(far_pieces), [far])
+    far_by_part = []
+    for part, pairs in enumerate((forward, backward)):
+        block, receiver = rows_of[(-steps, steps)[part]], (place + (1, -1)[part]) % rcv_count
+        piece = cut([block], np.asarray(order)[receiver], gains, device, (part,))
+        piece = lax.ppermute(piece, "rcv", pairs)
+        far_by_part.append(exchange(piece))
+    note([((first, second), mask) for (first, mask), (second, _) in zip(*far_by_part)], [far])
     early, late = columns[:late_from], columns[late_from:]
     absent = pack = [(c[2], c[3]) for c in late]
     jobs = [Job(as_rows(inside), early, absent, pack=pack)]
@@ -615,9 +618,7 @@
     ]
     last = []
     for part in range(2):
-        upper = lax.ppermute(ahead[part][: rows // 2], "rcv", turns[0])
-        lower = lax.ppermute(behind[part][rows // 2 :], "rcv", turns[1])
-        last.append((upper, lower))
+        last.append(lax.ppermute((ahead[0], behind[1])[part], "rcv", turns[part]))
     jobs = [Job(as_rows(outside), early, absent, pack=pack)]
     out, packed_outside = launch(device, out, jobs, used, span, total)
     chosen = np.zeros(devices)

time: 310 us -> 299 us (0.965)
  the two profiles are of different devices: /device:TPU:18 before, /device:TPU:0 now
where the time goes in v3:
time: 299 us; the launch traced here: 297 us
  waiting for transfers between devices  139 us (46%)
  Pallas kernels  72 us (24%)
  starting transfers between devices  46.1 us (15%)
  blocking collectives  34.9 us (12%)
  local copies, waits for them, and re-layouts  3.92 us (1%)
    pallas_call x3, Pallas kernels, launch(): pl.pallas_call(kernel, out_shape=out_shape, grid_spec=pltpu.PrefetchScala...  42.9 us
    all_to_all x1, blocking collectives, local(): lax.all_to_all(b, ('src', 'rcv'), split_axis=0, concat_axis=0, tiled=True)  34.9 us
    ppermute x18, waiting for transfers between devices, exchange(): lax.ppermute(x, 'src', swap)  34.9 us
    ppermute x4, waiting for transfers between devices, local(): moved.append(lax.ppermute(behind[part], 'rcv', backward))  30.9 us
    all_to_all x1, waiting for transfers between devices, local(): lax.all_to_all(b, ('src', 'rcv'), split_axis=0, concat_axis=0, tiled=True)  21.6 us
    ppermute x2, waiting for transfers between devices, local(): behind.append(lax.ppermute(own[part], 'rcv', backward))  20.9 us
    pallas_call x6, Pallas kernels, cut(): pl.pallas_call(cut_kernel, out_shape=jax.ShapeDtypeStruct(shape, jnp.bflo...  16.9 us
    ppermute x2, waiting for transfers between devices, local(): piece = lax.ppermute(piece, 'rcv', pairs)  16.2 us
  transfers between devices with their start and end apart: 39, of which 17 were waited for; matrix products, arithmetic and copies ran while one was open for 1% of the time, Pallas kernels for 18%

profile of v3, /device:TPU:0, one launch (start us, length us, event | category | flops | bytes accessed | tf_op | source)
XLA Modules:
  0.0 297.4 jit_solution(17585286924634937301)
XLA Ops:
  0.0 4.0 %shard_map.139 = (bf16[32,128,128]{2,1,0:T(8,128)(2,1)}, bf16[32,128,128]{2,1,0:T(8,128)(2,1)}) custom-call(bf16[2,128,4096]{2,1,0:T(8,128)(2,1)} %data_ref.5), custom_call_target="tpu_custom_call" | custom-call | tf_op jit(solution)/shard_map/pallas_call | solution.py:30
  4.0 34.9 %all_to_all.10.arrived_ref = bf16[32,128,128]{2,1,0:T(8,128)(2,1)} all-to-all(bf16[32,128,128]{2,1,0:T(8,128)(2,1)} %get-tuple-element.11), channel_id=1, replica_groups=mesh['src'=4,'rcv'=8] {'src','rcv'}, dimensions={0} | all-to-all | bytes 2097152 | tf_op jit(solution)/shard_map/all_to_all | solution.py:544
  38.9 2.6 all-to-all-start.1
  41.6 4.1 %shard_map.140.refs_0_ = bf16[128,4096]{1,0:T(8,128)(2,1)} custom-call(bf16[2,128,4096]{2,1,0:T(8,128)(2,1)} %data_ref.5, s32[128,4096]{1,0:T(8,128)} %mask_ref.3, bf16[32,128,128]{2,1,0:T(8,128)(2,1)} %all_to_all.10.arrived_ref), custom_call_target="tpu_custom_call" | custom-call | tf_op jit(solution)/shard_map/pallas_call | solution.py:55
  47.4 21.6 %all-to-all-done.1.arrived_ref = bf16[32,128,128]{2,1,0:T(8,128)(2,1)S(1)} async-done(((bf16[32,128,128]{2,1,0:T(8,128)(2,1)}), bf16[32,128,128]{2,1,0:T(8,128)(2,1)S(1)}, u32[]{:S(2)}, u32[]{:S(2)}) %all-to-all-start.1) | async-done | bytes 1048608 | tf_op jit(solution)/shard_map/all_to_all | solution.py:544
  70.0 4.1 %shard_map.141.refs_1_ = bf16[128,4096]{1,0:T(8,128)(2,1)} custom-call(bf16[2,128,4096]{2,1,0:T(8,128)(2,1)} %data_ref.5, s32[128,4096]{1,0:T(8,128)} %mask_ref.3, bf16[32,128,128]{2,1,0:T(8,128)(2,1)} %copy-done.4), custom_call_target="tpu_custom_call" | custom-call | tf_op jit(solution)/shard_map/pallas_call | solution.py:55
  78.6 2.7 shard_map.145.refs_10_.refs_4_.refs_20_
  81.8 7.2 %collective-permute-done.23.refs_11_.refs_5_.refs_21_ = bf16[1,2,128,512]{3,2,1,0:T(8,128)(2,1)S(1)} collective-permute-done((bf16[1,2,128,512]{3,2,1,0:T(8,128)(2,1)}, bf16[1,2,128,512]{3,2,1,0:T(8,128)(2,1)S(1)}, u32[]{:S(2)}, u32[]{:S(2)}) %collective-permute-start.23) | collective-permute-done | bytes 262176 | tf_op jit(solution)/shard_map/ppermute | solution.py:529
  91.0 9.4 %collective-permute-done.9.refs_4_.refs_5_ = bf16[128,4096]{1,0:T(8,128)(2,1)S(1)} collective-permute-done((bf16[128,4096]{1,0:T(8,128)(2,1)}, bf16[128,4096]{1,0:T(8,128)(2,1)S(1)}, u32[]{:S(2)}, u32[]{:S(2)}) %collective-permute-start.9) | collective-permute-done | bytes 1048608 | tf_op jit(solution)/shard_map/ppermute | solution.py:550
  101.1 3.4 %collective-permute-done.3.refs_1_.refs_3_ = bf16[128,4096]{1,0:T(8,128)(2,1)} collective-permute-done((bf16[128,4096]{1,0:T(8,128)(2,1)}, bf16[128,4096]{1,0:T(8,128)(2,1)}, u32[]{:S(2)}, u32[]{:S(2)}) %collective-permute-start.3) | collective-permute-done | bytes 1048608 | tf_op jit(solution)/shard_map/ppermute | solution.py:549
  104.5 6.9 %collective-permute-start.4 = (bf16[128,4096]{1,0:T(8,128)(2,1)}, bf16[128,4096]{1,0:T(8,128)(2,1)}, u32[]{:S(2)}, u32[]{:S(2)}) collective-permute-start(bf16[128,4096]{1,0:T(8,128)(2,1)} %collective-permute-done.3.refs_1_.refs_3_), channel_id=1, source_target_pairs={{0,2},{2,4},{4,6},{6,7},{7,5},{5,3},{3,1},{1,0},{8,10},{10,12},{12... | collective-permute-start | bytes 3145736 | tf_op jit(solution)/shard_map/ppermute | solution.py:597
  111.4 11.5 %collective-permute-done.6.refs_3_.refs_4_ = bf16[128,4096]{1,0:T(8,128)(2,1)} collective-permute-done((bf16[128,4096]{1,0:T(8,128)(2,1)S(1)}, bf16[128,4096]{1,0:T(8,128)(2,1)}, u32[]{:S(2)}, u32[]{:S(2)}) %collective-permute-start.6) | collective-permute-done | bytes 1048608 | tf_op jit(solution)/shard_map/ppermute | solution.py:550
  123.7 3.0 %shard_map.146.refs_14_.refs_8_.refs_24_ = bf16[2,2,128,512]{3,2,1,0:T(8,128)(2,1)} custom-call(s32[1]{0:T(128)} %bitcast.device_ref, s32[32,3]{1,0:T(8,128)} %constant.41.clone.place_ref, bf16[128,4096]{1,0:T(8,128)(2,1)} %copy-done.10, bf16[128,4096]{1,0:T(8,128)(2,1)} %collective-permute-done.3.refs_1_.refs_3_, ...), custom_call_target="tpu_custom_call" | custom-call | tf_op jit(solution)/shard_map/pallas_call | solution.py:186
  127.2 11.9 %collective-permute-done.26.refs_15_.refs_9_.refs_25_ = bf16[2,2,128,512]{3,2,1,0:T(8,128)(2,1)} collective-permute-done((bf16[2,2,128,512]{3,2,1,0:T(8,128)(2,1)}, bf16[2,2,128,512]{3,2,1,0:T(8,128)(2,1)}, u32[]{:S(2)}, u32[]{:S(2)}) %collective-permute-start.26) | collective-permute-done | bytes 524320 | tf_op jit(solution)/shard_map/ppermute | solution.py:529
  139.9 5.5 %collective-permute-done.10.refs_4_.refs_9_ = bf16[128,4096]{1,0:T(8,128)(2,1)} collective-permute-done((bf16[128,4096]{1,0:T(8,128)(2,1)S(1)}, bf16[128,4096]{1,0:T(8,128)(2,1)}, u32[]{:S(2)}, u32[]{:S(2)}) %collective-permute-start.10) | collective-permute-done | bytes 1048608 | tf_op jit(solution)/shard_map/ppermute | solution.py:598
  146.1 2.9 collective-permute-done.4.refs_1_.refs_7_
  149.0 7.1 %collective-permute-start.2 = (bf16[128,4096]{1,0:T(8,128)(2,1)}, bf16[128,4096]{1,0:T(8,128)(2,1)S(1)}, u32[]{:S(2)}, u32[]{:S(2)}) collective-permute-start(bf16[128,4096]{1,0:T(8,128)(2,1)} %collective-permute-done.1.refs_0_.refs_6_), channel_id=1, source_target_pairs={{0,2},{2,4},{4,6},{6,7},{7,5},{5,3},{3,1},{1,0},{8,10},{10,12},{12... | collective-permute-start | bytes 3145736 | tf_op jit(solution)/shard_map/ppermute | solution.py:597
  156.1 11.8 %collective-permute-done.7.refs_3_.refs_8_ = bf16[128,4096]{1,0:T(8,128)(2,1)} collective-permute-done((bf16[128,4096]{1,0:T(8,128)(2,1)}, bf16[128,4096]{1,0:T(8,128)(2,1)}, u32[]{:S(2)}, u32[]{:S(2)}) %collective-permute-start.7) | collective-permute-done | bytes 1048608 | tf_op jit(solution)/shard_map/ppermute | solution.py:598
  167.8 3.0 %shard_map.147.refs_18_.refs_12_.refs_28_ = bf16[2,2,128,512]{3,2,1,0:T(8,128)(2,1)} custom-call(s32[1]{0:T(128)} %bitcast.device_ref, s32[32,3]{1,0:T(8,128)} %constant.42.clone.place_ref, bf16[128,4096]{1,0:T(8,128)(2,1)} %collective-permute-done.1.refs_0_.refs_6_, bf16[128,4096]{1,0:T(8,128)(2,1)} %collective-permute-done.4.refs_1_.refs_7_, ...), custom_call_target="tpu_custom_call" | custom-call | tf_op jit(solution)/shard_map/pallas_call | solution.py:186
  173.5 12.0 %collective-permute-done.29.refs_19_.refs_13_.refs_29_ = bf16[2,2,128,512]{3,2,1,0:T(8,128)(2,1)} collective-permute-done((bf16[2,2,128,512]{3,2,1,0:T(8,128)(2,1)}, bf16[2,2,128,512]{3,2,1,0:T(8,128)(2,1)}, u32[]{:S(2)}, u32[]{:S(2)}) %collective-permute-start.29) | collective-permute-done | bytes 524320 | tf_op jit(solution)/shard_map/ppermute | solution.py:529
  187.2 3.0 %collective-permute-done.11.refs_4_.refs_0_.refs_3_ = bf16[128,4096]{1,0:T(8,128)(2,1)S(1)} collective-permute-done((bf16[128,4096]{1,0:T(8,128)(2,1)}, bf16[128,4096]{1,0:T(8,128)(2,1)S(1)}, u32[]{:S(2)}, u32[]{:S(2)}) %collective-permute-start.11) | collective-permute-done | bytes 1048608 | tf_op jit(solution)/shard_map/ppermute | solution.py:598
  193.6 7.7 %collective-permute-done.5.refs_1_ = bf16[128,4096]{1,0:T(8,128)(2,1)} collective-permute-done((bf16[128,4096]{1,0:T(8,128)(2,1)}, bf16[128,4096]{1,0:T(8,128)(2,1)}, u32[]{:S(2)}, u32[]{:S(2)}) %collective-permute-start.5) | collective-permute-done | bytes 1048608 | tf_op jit(solution)/shard_map/ppermute | solution.py:597
  201.3 10.6 %collective-permute-done.8.refs_3_.refs_2_ = bf16[128,4096]{1,0:T(8,128)(2,1)} collective-permute-done((bf16[128,4096]{1,0:T(8,128)(2,1)}, bf16[128,4096]{1,0:T(8,128)(2,1)}, u32[]{:S(2)}, u32[]{:S(2)}) %collective-permute-start.8) | collective-permute-done | bytes 1048608 | tf_op jit(solution)/shard_map/ppermute | solution.py:598
  211.9 3.0 %shard_map.142.refs_0_.refs_32_ = bf16[2,2,128,512]{3,2,1,0:T(8,128)(2,1)} custom-call(s32[1]{0:T(128)} %bitcast.device_ref, s32[32,3]{1,0:T(8,128)} %constant.43.clone.place_ref, bf16[128,4096]{1,0:T(8,128)(2,1)} %copy-done.3, bf16[128,4096]{1,0:T(8,128)(2,1)} %collective-permute-done.5.refs_1_, f32[8,128,1]{2,1,0:T(8,128)} %copy.26.refs_2_.refs_5_.refs_1_, ...), custom_call_target="tpu_custom_call" | custom-call | tf_op jit(solution)/shard_map/pallas_call | solution.py:186
  219.0 2.6 shard_map.144
  223.6 3.6 %collective-permute-done.15.refs_4_.refs_36_ = bf16[1,1,128,512]{3,2,1,0:T(8,128)(2,1)S(1)} collective-permute-done((bf16[1,1,128,512]{3,2,1,0:T(8,128)(2,1)}, bf16[1,1,128,512]{3,2,1,0:T(8,128)(2,1)S(1)}, u32[]{:S(2)}, u32[]{:S(2)}) %collective-permute-start.15) | collective-permute-done | bytes 131104 | tf_op jit(solution)/shard_map/ppermute | solution.py:608
  227.9 12.6 %collective-permute-done.16.refs_5_.refs_37_ = bf16[1,1,128,512]{3,2,1,0:T(8,128)(2,1)S(1)} collective-permute-done((bf16[1,1,128,512]{3,2,1,0:T(8,128)(2,1)}, bf16[1,1,128,512]{3,2,1,0:T(8,128)(2,1)S(1)}, u32[]{:S(2)}, u32[]{:S(2)}) %collective-permute-start.16) | collective-permute-done | bytes 131104 | tf_op jit(solution)/shard_map/ppermute | solution.py:608
  242.2 3.3 %collective-permute-done.18.refs_7_.refs_39_ = bf16[1,1,128,512]{3,2,1,0:T(8,128)(2,1)S(1)} collective-permute-done((bf16[1,1,128,512]{3,2,1,0:T(8,128)(2,1)S(1)}, bf16[1,1,128,512]{3,2,1,0:T(8,128)(2,1)S(1)}, u32[]{:S(2)}, u32[]{:S(2)}) %collective-permute-start.18) | collective-permute-done | bytes 131104 | tf_op jit(solution)/shard_map/ppermute | solution.py:529
  246.8 4.8 %collective-permute-start.33 = (bf16[128,4096]{1,0:T(8,128)(2,1)}, bf16[128,4096]{1,0:T(8,128)(2,1)}, u32[]{:S(2)}, u32[]{:S(2)}) collective-permute-start(bf16[128,4096]{1,0:T(8,128)(2,1)} %copy-done.2), channel_id=1, source_target_pairs={{2,0},{7,6},{5,7},{0,1},{10,8},{15,14},{13,15},{8,9},{18,16},{23,2... | collective-permute-start | bytes 3145736 | tf_op jit(solution)/shard_map/ppermute | solution.py:621
  252.3 18.4 %shard_map.148 = (f32[2,1024,512]{2,1,0:T(8,128)}, bf16[2,640,1536]{2,1,0:T(8,128)(2,1)}) custom-call(s32[1]{0:T(128)} %bitcast.device_ref, s32[32,49]{1,0:T(8,128)} %constant.46.clone.plan_ref, s32[2,8]{1,0:T(2,128)} %convert_element_type.3.used_ref, bf16[128,4096]{1,0:T(8,128)(2,1)} %shard_map.140.refs_0_, bf16[128,4096]{1,0:T(8,128)(2,1)} %shard_map.141.refs_1_, ...), custom_call_target="tpu_custom_call" | custom-call | flops 10737418240 | bytes 83886080 | tf_op jit(solution)/shard_map/pallas_call | solution.py:454
  271.3 9.6 %shard_map.149 = (f32[2,1024,512]{2,1,0:T(8,128)}, bf16[2,256,1536]{2,1,0:T(8,128)(2,1)}) custom-call(s32[1]{0:T(128)} %bitcast.device_ref, s32[32,46]{1,0:T(8,128)} %constant.47.clone.plan_ref, s32[2,8]{1,0:T(2,128)} %convert_element_type.3.used_ref, bf16[128,4096]{1,0:T(8,128)(2,1)} %copy-done.3, ...), custom_call_target="tpu_custom_call", output_to_operand_aliasing={{0}: (19, {})} | custom-call | flops 4294967296 | bytes 83886080 | tf_op jit(solution)/shard_map/pallas_call | solution.py:454
  282.3 15.0 %shard_map.150 = f32[2,1024,512]{2,1,0:T(8,128)} custom-call(s32[1]{0:T(128)} %bitcast.device_ref, s32[32,53]{1,0:T(8,128)} %constant.48.clone.plan_ref, s32[2,8]{1,0:T(2,128)} %convert_element_type.3.used_ref, bf16[2,2,128,512]{3,2,1,0:T(8,128)(2,1)} %shard_map.142.refs_0_.refs_32_, ...), custom_call_target="tpu_custom_call", output_to_operand_aliasing={{}: (47, {})} | custom-call | flops 7784628224 | bytes 83886080 | tf_op jit(solution)/shard_map/pallas_call | solution.py:454
  (109 shorter events, 33.1 us)
Async XLA Ops:
  38.9 30.1 %all-to-all-start.1 = ((bf16[32,128,128]{2,1,0:T(8,128)(2,1)}), bf16[32,128,128]{2,1,0:T(8,128)(2,1)S(1)}, u32[]{:S(2)}, u32[]{:S(2)}) async-start(bf16[32,128,128]{2,1,0:T(8,128)(2,1)} %get-tuple-element.12), calls=%async_computation.1 | async-start | bytes 2097152 | tf_op jit(solution)/shard_map/all_to_all | solution.py:544
  45.7 43.4 %collective-permute-start = (bf16[128,4096]{1,0:T(8,128)(2,1)}, bf16[128,4096]{1,0:T(8,128)(2,1)S(1)}, u32[]{:S(2)}, u32[]{:S(2)}) collective-permute-start(bf16[128,4096]{1,0:T(8,128)(2,1)} %shard_map.140.refs_0_), channel_id=1, source_target_pairs={{0,2},{2,4},{4,6},{6,7},{7,5},{5,3},{3,1},{1,0},{8,10},{10,12},{12... | collective-permute-start | bytes 3145736 | tf_op jit(solution)/shard_map/ppermute | solution.py:549
  74.1 26.2 %collective-permute-start.9 = (bf16[128,4096]{1,0:T(8,128)(2,1)}, bf16[128,4096]{1,0:T(8,128)(2,1)S(1)}, u32[]{:S(2)}, u32[]{:S(2)}) collective-permute-start(bf16[128,4096]{1,0:T(8,128)(2,1)} %shard_map.141.refs_1_), channel_id=1, source_target_pairs={{2,0},{4,2},{6,4},{7,6},{5,7},{3,5},{1,3},{0,1},{10,8},{12,10},{14... | collective-permute-start | bytes 3145736 | tf_op jit(solution)/shard_map/ppermute | solution.py:550
  74.8 29.7 %collective-permute-start.3 = (bf16[128,4096]{1,0:T(8,128)(2,1)}, bf16[128,4096]{1,0:T(8,128)(2,1)}, u32[]{:S(2)}, u32[]{:S(2)}) collective-permute-start(bf16[128,4096]{1,0:T(8,128)(2,1)} %shard_map.141.refs_1_), channel_id=1, source_target_pairs={{0,2},{2,4},{4,6},{6,7},{7,5},{5,3},{3,1},{1,0},{8,10},{10,12},{12... | collective-permute-start | bytes 3145736 | tf_op jit(solution)/shard_map/ppermute | solution.py:549
  76.1 46.8 %collective-permute-start.6 = (bf16[128,4096]{1,0:T(8,128)(2,1)S(1)}, bf16[128,4096]{1,0:T(8,128)(2,1)}, u32[]{:S(2)}, u32[]{:S(2)}) collective-permute-start(bf16[128,4096]{1,0:T(8,128)(2,1)S(1)} %copy-done.1), channel_id=1, source_target_pairs={{2,0},{4,2},{6,4},{7,6},{5,7},{3,5},{1,3},{0,1},{10,8},{12,10},{14... | collective-permute-start | bytes 3145736 | tf_op jit(solution)/shard_map/ppermute | solution.py:550
  89.1 50.7 %collective-permute-start.1 = (bf16[128,4096]{1,0:T(8,128)(2,1)S(1)}, bf16[128,4096]{1,0:T(8,128)(2,1)}, u32[]{:S(2)}, u32[]{:S(2)}) collective-permute-start(bf16[128,4096]{1,0:T(8,128)(2,1)S(1)} %collective-permute-done.refs_0_.refs_2_), channel_id=1, source_target_pairs={{0,2},{2,4},{4,6},{6,7},{7,5},{5,3},{3,1},{1,0},{8,10},{10,12},{12... | collective-permute-start | bytes 3145736 | tf_op jit(solution)/shard_map/ppermute | solution.py:597
  90.8 35.9 %collective-permute-start.25 = (bf16[1,2,128,512]{3,2,1,0:T(8,128)(2,1)S(1)}, bf16[1,2,128,512]{3,2,1,0:T(8,128)(2,1)}, u32[]{:S(2)}, u32[]{:S(2)}) collective-permute-start(bf16[1,2,128,512]{3,2,1,0:T(8,128)(2,1)S(1)} %collective-permute-done.23.refs_11_.refs_5_.refs_21_), channel_id=1, source_target_pairs={{0,8},{8,0},{16,24},{24,16},{1,9},{9,1},{17,25},{25,17},{2,10},{10... | collective-permute-start | bytes 786440 | tf_op jit(solution)/shard_map/ppermute | solution.py:529
  100.3 45.0 %collective-permute-start.10 = (bf16[128,4096]{1,0:T(8,128)(2,1)S(1)}, bf16[128,4096]{1,0:T(8,128)(2,1)}, u32[]{:S(2)}, u32[]{:S(2)}) collective-permute-start(bf16[128,4096]{1,0:T(8,128)(2,1)S(1)} %collective-permute-done.9.refs_4_.refs_5_), channel_id=1, source_target_pairs={{2,0},{4,2},{6,4},{7,6},{5,7},{3,5},{1,3},{0,1},{10,8},{12,10},{14... | collective-permute-start | bytes 3145736 | tf_op jit(solution)/shard_map/ppermute | solution.py:598
  104.5 44.5 %collective-permute-start.4 = (bf16[128,4096]{1,0:T(8,128)(2,1)}, bf16[128,4096]{1,0:T(8,128)(2,1)}, u32[]{:S(2)}, u32[]{:S(2)}) collective-permute-start(bf16[128,4096]{1,0:T(8,128)(2,1)} %collective-permute-done.3.refs_1_.refs_3_), channel_id=1, source_target_pairs={{0,2},{2,4},{4,6},{6,7},{7,5},{5,3},{3,1},{1,0},{8,10},{10,12},{12... | collective-permute-start | bytes 3145736 | tf_op jit(solution)/shard_map/ppermute | solution.py:597
  122.9 44.9 %collective-permute-start.7 = (bf16[128,4096]{1,0:T(8,128)(2,1)}, bf16[128,4096]{1,0:T(8,128)(2,1)}, u32[]{:S(2)}, u32[]{:S(2)}) collective-permute-start(bf16[128,4096]{1,0:T(8,128)(2,1)} %collective-permute-done.6.refs_3_.refs_4_), channel_id=1, source_target_pairs={{2,0},{4,2},{6,4},{7,6},{5,7},{3,5},{1,3},{0,1},{10,8},{12,10},{14... | collective-permute-start | bytes 3145736 | tf_op jit(solution)/shard_map/ppermute | solution.py:598
  126.7 12.4 %collective-permute-start.26 = (bf16[2,2,128,512]{3,2,1,0:T(8,128)(2,1)}, bf16[2,2,128,512]{3,2,1,0:T(8,128)(2,1)}, u32[]{:S(2)}, u32[]{:S(2)}) collective-permute-start(bf16[2,2,128,512]{3,2,1,0:T(8,128)(2,1)} %shard_map.146.refs_14_.refs_8_.refs_24_), channel_id=1, source_target_pairs={{0,16},{8,24},{16,0},{24,8},{1,17},{9,25},{17,1},{25,9},{2,18},{10... | collective-permute-start | bytes 1572872 | tf_op jit(solution)/shard_map/ppermute | solution.py:529
  139.1 32.6 %collective-permute-start.34 = (bf16[128,4096]{1,0:T(8,128)(2,1)}, bf16[128,4096]{1,0:T(8,128)(2,1)S(1)}, u32[]{:S(2)}, u32[]{:S(2)}) collective-permute-start(bf16[128,4096]{1,0:T(8,128)(2,1)} %copy-done.10), channel_id=1, source_target_pairs={{3,2},{4,5},{11,10},{12,13},{19,18},{20,21},{27,26},{28,29}} | collective-permute-start | bytes 3145736 | tf_op jit(solution)/shard_map/ppermute | solution.py:505
  139.8 31.1 %collective-permute-start.27 = (bf16[2,2,128,512]{3,2,1,0:T(8,128)(2,1)}, bf16[2,2,128,512]{3,2,1,0:T(8,128)(2,1)}, u32[]{:S(2)}, u32[]{:S(2)}) collective-permute-start(bf16[2,2,128,512]{3,2,1,0:T(8,128)(2,1)} %shard_map.146.refs_14_.refs_8_.refs_24_), channel_id=1, source_target_pairs={{0,8},{8,0},{16,24},{24,16},{1,9},{9,1},{17,25},{25,17},{2,10},{10... | collective-permute-start | bytes 1572872 | tf_op jit(solution)/shard_map/ppermute | solution.py:529
  145.4 44.8 %collective-permute-start.11 = (bf16[128,4096]{1,0:T(8,128)(2,1)}, bf16[128,4096]{1,0:T(8,128)(2,1)S(1)}, u32[]{:S(2)}, u32[]{:S(2)}) collective-permute-start(bf16[128,4096]{1,0:T(8,128)(2,1)} %collective-permute-done.10.refs_4_.refs_9_), channel_id=1, source_target_pairs={{2,0},{4,2},{6,4},{7,6},{5,7},{3,5},{1,3},{0,1},{10,8},{12,10},{14... | collective-permute-start | bytes 3145736 | tf_op jit(solution)/shard_map/ppermute | solution.py:598
  149.0 42.8 %collective-permute-start.2 = (bf16[128,4096]{1,0:T(8,128)(2,1)}, bf16[128,4096]{1,0:T(8,128)(2,1)S(1)}, u32[]{:S(2)}, u32[]{:S(2)}) collective-permute-start(bf16[128,4096]{1,0:T(8,128)(2,1)} %collective-permute-done.1.refs_0_.refs_6_), channel_id=1, source_target_pairs={{0,2},{2,4},{4,6},{6,7},{7,5},{5,3},{3,1},{1,0},{8,10},{10,12},{12... | collective-permute-start | bytes 3145736 | tf_op jit(solution)/shard_map/ppermute | solution.py:597
  170.9 14.7 %collective-permute-start.29 = (bf16[2,2,128,512]{3,2,1,0:T(8,128)(2,1)}, bf16[2,2,128,512]{3,2,1,0:T(8,128)(2,1)}, u32[]{:S(2)}, u32[]{:S(2)}) collective-permute-start(bf16[2,2,128,512]{3,2,1,0:T(8,128)(2,1)} %shard_map.147.refs_18_.refs_12_.refs_28_), channel_id=1, source_target_pairs={{0,16},{8,24},{16,0},{24,8},{1,17},{9,25},{17,1},{25,9},{2,18},{10... | collective-permute-start | bytes 1572872 | tf_op jit(solution)/shard_map/ppermute | solution.py:529
  171.5 29.8 %collective-permute-start.5 = (bf16[128,4096]{1,0:T(8,128)(2,1)}, bf16[128,4096]{1,0:T(8,128)(2,1)}, u32[]{:S(2)}, u32[]{:S(2)}) collective-permute-start(bf16[128,4096]{1,0:T(8,128)(2,1)} %collective-permute-done.4.refs_1_.refs_7_), channel_id=1, source_target_pairs={{0,2},{2,4},{4,6},{6,7},{7,5},{5,3},{3,1},{1,0},{8,10},{10,12},{12... | collective-permute-start | bytes 3145736 | tf_op jit(solution)/shard_map/ppermute | solution.py:597
  171.7 40.2 %collective-permute-start.8 = (bf16[128,4096]{1,0:T(8,128)(2,1)}, bf16[128,4096]{1,0:T(8,128)(2,1)}, u32[]{:S(2)}, u32[]{:S(2)}) collective-permute-start(bf16[128,4096]{1,0:T(8,128)(2,1)} %collective-permute-done.7.refs_3_.refs_8_), channel_id=1, source_target_pairs={{2,0},{4,2},{6,4},{7,6},{5,7},{3,5},{1,3},{0,1},{10,8},{12,10},{14... | collective-permute-start | bytes 3145736 | tf_op jit(solution)/shard_map/ppermute | solution.py:598
  185.5 29.4 %collective-permute-start.35 = (bf16[128,4096]{1,0:T(8,128)(2,1)}, bf16[128,4096]{1,0:T(8,128)(2,1)}, u32[]{:S(2)}, u32[]{:S(2)}) collective-permute-start(bf16[128,4096]{1,0:T(8,128)(2,1)} %collective-permute-done.3.refs_1_.refs_3_), channel_id=1, source_target_pairs={{3,2},{4,5},{11,10},{12,13},{19,18},{20,21},{27,26},{28,29}} | collective-permute-start | bytes 3145736 | tf_op jit(solution)/shard_map/ppermute | solution.py:505
  190.2 31.3 %collective-permute-start.36 = (bf16[128,4096]{1,0:T(8,128)(2,1)}, bf16[128,4096]{1,0:T(8,128)(2,1)}, u32[]{:S(2)}, u32[]{:S(2)}) collective-permute-start(bf16[128,4096]{1,0:T(8,128)(2,1)} %collective-permute-done.6.refs_3_.refs_4_), channel_id=1, source_target_pairs={{5,4},{2,3},{13,12},{10,11},{21,20},{18,19},{29,28},{26,27}} | collective-permute-start | bytes 3145736 | tf_op jit(solution)/shard_map/ppermute | solution.py:505
  191.8 29.7 %collective-permute-start.37 = (bf16[128,4096]{1,0:T(8,128)(2,1)}, bf16[128,4096]{1,0:T(8,128)(2,1)}, u32[]{:S(2)}, u32[]{:S(2)}) collective-permute-start(bf16[128,4096]{1,0:T(8,128)(2,1)} %copy-done.11), channel_id=1, source_target_pairs={{5,4},{2,3},{13,12},{10,11},{21,20},{18,19},{29,28},{26,27}} | collective-permute-start | bytes 3145736 | tf_op jit(solution)/shard_map/ppermute | solution.py:505
  201.3 26.7 %collective-permute-start.30 = (bf16[2,2,128,512]{3,2,1,0:T(8,128)(2,1)}, bf16[2,2,128,512]{3,2,1,0:T(8,128)(2,1)}, u32[]{:S(2)}, u32[]{:S(2)}) collective-permute-start(bf16[2,2,128,512]{3,2,1,0:T(8,128)(2,1)} %shard_map.147.refs_18_.refs_12_.refs_28_), channel_id=1, source_target_pairs={{0,8},{8,0},{16,24},{24,16},{1,9},{9,1},{17,25},{25,17},{2,10},{10... | collective-permute-start | bytes 1572872 | tf_op jit(solution)/shard_map/ppermute | solution.py:529
  211.9 29.1 %collective-permute-start.31 = (bf16[2,2,128,512]{3,2,1,0:T(8,128)(2,1)}, bf16[2,2,128,512]{3,2,1,0:T(8,128)(2,1)}, u32[]{:S(2)}, u32[]{:S(2)}) collective-permute-start(bf16[2,2,128,512]{3,2,1,0:T(8,128)(2,1)} %collective-permute-done.29.refs_19_.refs_13_.refs_29_), channel_id=1, source_target_pairs={{0,8},{8,0},{16,24},{24,16},{1,9},{9,1},{17,25},{25,17},{2,10},{10... | collective-permute-start | bytes 1572872 | tf_op jit(solution)/shard_map/ppermute | solution.py:529
  214.9 37.4 %collective-permute-start.12 = (bf16[2,2,128,512]{3,2,1,0:T(8,128)(2,1)}, bf16[2,2,128,512]{3,2,1,0:T(8,128)(2,1)S(1)}, u32[]{:S(2)}, u32[]{:S(2)}) collective-permute-start(bf16[2,2,128,512]{3,2,1,0:T(8,128)(2,1)} %shard_map.142.refs_0_.refs_32_), channel_id=1, source_target_pairs={{0,16},{8,24},{16,0},{24,8},{1,17},{9,25},{17,1},{25,9},{2,18},{10... | collective-permute-start | bytes 1572872 | tf_op jit(solution)/shard_map/ppermute | solution.py:529
  221.6 19.0 %collective-permute-start.16 = (bf16[1,1,128,512]{3,2,1,0:T(8,128)(2,1)}, bf16[1,1,128,512]{3,2,1,0:T(8,128)(2,1)S(1)}, u32[]{:S(2)}, u32[]{:S(2)}) collective-permute-start(bf16[1,1,128,512]{3,2,1,0:T(8,128)(2,1)} %shard_map.144), channel_id=1, source_target_pairs={{2,0},{4,2},{6,4},{7,6},{5,7},{3,5},{1,3},{0,1},{10,8},{12,10},{14... | collective-permute-start | bytes 393224 | tf_op jit(solution)/shard_map/ppermute | solution.py:608
  227.3 14.5 %collective-permute-start.17 = (bf16[1,1,128,512]{3,2,1,0:T(8,128)(2,1)S(1)}, bf16[1,1,128,512]{3,2,1,0:T(8,128)(2,1)S(1)}, u32[]{:S(2)}, u32[]{:S(2)}) collective-permute-start(bf16[1,1,128,512]{3,2,1,0:T(8,128)(2,1)S(1)} %collective-permute-done.15.refs_4_.refs_36_), channel_id=1, source_target_pairs={{0,16},{8,24},{16,0},{24,8},{1,17},{9,25},{17,1},{25,9},{2,18},{10... | collective-permute-start | bytes 393224 | tf_op jit(solution)/shard_map/ppermute | solution.py:529
  227.9 18.9 %collective-permute-start.19 = (bf16[1,1,128,512]{3,2,1,0:T(8,128)(2,1)S(1)}, bf16[1,1,128,512]{3,2,1,0:T(8,128)(2,1)S(1)}, u32[]{:S(2)}, u32[]{:S(2)}) collective-permute-start(bf16[1,1,128,512]{3,2,1,0:T(8,128)(2,1)S(1)} %collective-permute-done.15.refs_4_.refs_36_), channel_id=1, source_target_pairs={{0,8},{8,0},{16,24},{24,16},{1,9},{9,1},{17,25},{25,17},{2,10},{10... | collective-permute-start | bytes 393224 | tf_op jit(solution)/shard_map/ppermute | solution.py:529
  241.7 39.1 %collective-permute-start.13 = (bf16[2,2,128,512]{3,2,1,0:T(8,128)(2,1)}, bf16[2,2,128,512]{3,2,1,0:T(8,128)(2,1)S(1)}, u32[]{:S(2)}, u32[]{:S(2)}) collective-permute-start(bf16[2,2,128,512]{3,2,1,0:T(8,128)(2,1)} %shard_map.142.refs_0_.refs_32_), channel_id=1, source_target_pairs={{0,8},{8,0},{16,24},{24,16},{1,9},{9,1},{17,25},{25,17},{2,10},{10... | collective-permute-start | bytes 1572872 | tf_op jit(solution)/shard_map/ppermute | solution.py:529
  245.5 35.4 %collective-permute-start.32 = (bf16[128,4096]{1,0:T(8,128)(2,1)}, bf16[128,4096]{1,0:T(8,128)(2,1)S(1)}, u32[]{:S(2)}, u32[]{:S(2)}) collective-permute-start(bf16[128,4096]{1,0:T(8,128)(2,1)} %copy-done.3), channel_id=1, source_target_pairs={{1,0},{4,6},{6,7},{3,1},{9,8},{12,14},{14,15},{11,9},{17,16},{20,2... | collective-permute-start | bytes 3145736 | tf_op jit(solution)/shard_map/ppermute | solution.py:621
  246.8 34.1 %collective-permute-start.33 = (bf16[128,4096]{1,0:T(8,128)(2,1)}, bf16[128,4096]{1,0:T(8,128)(2,1)}, u32[]{:S(2)}, u32[]{:S(2)}) collective-permute-start(bf16[128,4096]{1,0:T(8,128)(2,1)} %copy-done.2), channel_id=1, source_target_pairs={{2,0},{7,6},{5,7},{0,1},{10,8},{15,14},{13,15},{8,9},{18,16},{23,2... | collective-permute-start | bytes 3145736 | tf_op jit(solution)/shard_map/ppermute | solution.py:621
  251.7 19.1 %collective-permute-start.21 = (bf16[1,1,128,512]{3,2,1,0:T(8,128)(2,1)S(1)}, bf16[1,1,128,512]{3,2,1,0:T(8,128)(2,1)}, u32[]{:S(2)}, u32[]{:S(2)}) collective-permute-start(bf16[1,1,128,512]{3,2,1,0:T(8,128)(2,1)S(1)} %collective-permute-done.17.refs_6_.refs_38_), channel_id=1, source_target_pairs={{0,8},{8,0},{16,24},{24,16},{1,9},{9,1},{17,25},{25,17},{2,10},{10... | collective-permute-start | bytes 393224 | tf_op jit(solution)/shard_map/ppermute | solution.py:529
  252.3 28.6 %collective-permute-start.14 = (bf16[2,2,128,512]{3,2,1,0:T(8,128)(2,1)S(1)}, bf16[2,2,128,512]{3,2,1,0:T(8,128)(2,1)S(1)}, u32[]{:S(2)}, u32[]{:S(2)}) collective-permute-start(bf16[2,2,128,512]{3,2,1,0:T(8,128)(2,1)S(1)} %collective-permute-done.12.refs_1_.refs_33_), channel_id=1, source_target_pairs={{0,8},{8,0},{16,24},{24,16},{1,9},{9,1},{17,25},{25,17},{2,10},{10... | collective-permute-start | bytes 1572872 | tf_op jit(solution)/shard_map/ppermute | solution.py:529
  (29 other events, 869.8 us)

commit v4 on v2

--- a/solution.py
+++ b/solution.py
@@ -26,7 +26,7 @@
     _, rows, _ = data.shape
     if rows % 128:
         return tuple(jnp.transpose(p.reshape(rows, devices, rows), (1, 0, 2)) for p in data)
-    group = 8
+    group = 16
     return pl.pallas_call(
         split_kernel,
         out_shape=(jax.ShapeDtypeStruct((devices, rows, rows), data.dtype),) * 2,
@@ -51,7 +51,7 @@
     if rows % 128:
         transposed = jnp.transpose(arrived, (2, 0, 1)).reshape(rows, total)
         return jnp.where(mask == 1, data[part], transposed)
-    group = 8
+    group = 16
     return pl.pallas_call(
         fill_kernel,
         out_shape=jax.ShapeDtypeStruct((rows, total), data.dtype),
@@ -605,10 +605,9 @@
     candidates = (*last, *taken[0], *taken[1])
     packed = [(packed_inside, len(inside)), (packed_outside, len(outside))]
     splits = [len(inside) // 2, len(inside)]
-    jobs = [Job(as_rows(inside + outside), late, packed=packed, splits=splits)]
-    out = launch(device, out, jobs, used, span, total)[0]
-    jobs = [Job([(candidates, far * rows)], columns, choice=chosen)]
-    return launch(device, out, jobs, used, span, total)[0]
+    near_rows = Job(as_rows(inside + outside), late, packed=packed, splits=splits)
+    far_rows = Job([(candidates, far * rows)], columns, choice=chosen)
+    return launch(device, out, [near_rows, far_rows], used, span, total)[0]
 
 
 def solution(mesh):

time: 327 us -> 304 us (0.930)
  the two profiles are of different devices: /device:TPU:10 before, /device:TPU:18 now
where the time goes in v4:
time: 304 us; the launch traced here: 301 us
  waiting for transfers between devices  155 us (51%)
  Pallas kernels  66.6 us (22%)
  starting transfers between devices  44.1 us (15%)
  blocking collectives  29.9 us (10%)
    ppermute x1, waiting for transfers between devices, local(): far_pieces = lax.ppermute(far_pieces, 'rcv', across)  46.5 us
    pallas_call x3, Pallas kernels, launch(): pl.pallas_call(kernel, out_shape=out_shape, grid_spec=pltpu.PrefetchScala...  43 us
    ppermute x4, waiting for transfers between devices, local(): moved.append(lax.ppermute(ahead[part], 'rcv', forward))  34.2 us
    all_to_all x1, blocking collectives, local(): lax.all_to_all(b, ('src', 'rcv'), split_axis=0, concat_axis=0, tiled=True)  29.9 us
    ppermute x15, waiting for transfers between devices, spread(): lax.ppermute(x, 'src', swap)  28.6 us
    ppermute x4, waiting for transfers between devices, local(): moved.append(lax.ppermute(behind[part], 'rcv', backward))  27.1 us
    all_to_all x1, waiting for transfers between devices, local(): lax.all_to_all(b, ('src', 'rcv'), split_axis=0, concat_axis=0, tiled=True)  18.9 us
    pallas_call x5, Pallas kernels, cut(): pl.pallas_call(cut_kernel, out_shape=jax.ShapeDtypeStruct(shape, jnp.bflo...  14.5 us
  transfers between devices with their start and end apart: 35, of which 14 were waited for; matrix products, arithmetic and copies ran while one was open for 1% of the time, Pallas kernels for 14%

profile of v4, /device:TPU:18, one launch (start us, length us, event | category | flops | bytes accessed | tf_op | source)
XLA Modules:
  0.0 300.8 jit_solution(1098744133053096862)
XLA Ops:
  0.0 2.8 shard_map.130
  2.8 29.9 %all_to_all.10.arrived_ref = bf16[32,128,128]{2,1,0:T(8,128)(2,1)} all-to-all(bf16[32,128,128]{2,1,0:T(8,128)(2,1)} %get-tuple-element.11), channel_id=1, replica_groups=mesh['src'=4,'rcv'=8] {'src','rcv'}, dimensions={0} | all-to-all | bytes 2097152 | tf_op jit(solution)/shard_map/all_to_all | solution.py:524
  32.7 6.2 %all-to-all-start.1 = ((bf16[32,128,128]{2,1,0:T(8,128)(2,1)}), bf16[32,128,128]{2,1,0:T(8,128)(2,1)S(1)}, u32[]{:S(2)}, u32[]{:S(2)}) async-start(bf16[32,128,128]{2,1,0:T(8,128)(2,1)} %get-tuple-element.12), calls=%async_computation.1 | async-start | bytes 2097152 | tf_op jit(solution)/shard_map/all_to_all | solution.py:524
  40.7 3.1 %shard_map.131.refs_0_ = bf16[128,4096]{1,0:T(8,128)(2,1)} custom-call(bf16[2,128,4096]{2,1,0:T(8,128)(2,1)} %data_ref.5, s32[128,4096]{1,0:T(8,128)} %mask_ref.3, bf16[32,128,128]{2,1,0:T(8,128)(2,1)} %all_to_all.10.arrived_ref), custom_call_target="tpu_custom_call" | custom-call | tf_op jit(solution)/shard_map/pallas_call | solution.py:55
  43.8 18.9 %all-to-all-done.1.arrived_ref = bf16[32,128,128]{2,1,0:T(8,128)(2,1)S(1)} async-done(((bf16[32,128,128]{2,1,0:T(8,128)(2,1)}), bf16[32,128,128]{2,1,0:T(8,128)(2,1)S(1)}, u32[]{:S(2)}, u32[]{:S(2)}) %all-to-all-start.1) | async-done | bytes 1048608 | tf_op jit(solution)/shard_map/all_to_all | solution.py:524
  63.7 3.2 %shard_map.132.refs_1_ = bf16[128,4096]{1,0:T(8,128)(2,1)} custom-call(bf16[2,128,4096]{2,1,0:T(8,128)(2,1)} %data_ref.5, s32[128,4096]{1,0:T(8,128)} %mask_ref.3, bf16[32,128,128]{2,1,0:T(8,128)(2,1)} %copy-done.2), custom_call_target="tpu_custom_call" | custom-call | tf_op jit(solution)/shard_map/pallas_call | solution.py:55
  66.8 2.7 shard_map.135.refs_10_.refs_4_.refs_16_
  69.6 1.7 collective-permute-start.19
  74.0 4.3 %collective-permute-done.19.refs_11_.refs_5_.refs_17_ = bf16[1,2,128,512]{3,2,1,0:T(8,128)(2,1)S(1)} collective-permute-done((bf16[1,2,128,512]{3,2,1,0:T(8,128)(2,1)}, bf16[1,2,128,512]{3,2,1,0:T(8,128)(2,1)S(1)}, u32[]{:S(2)}, u32[]{:S(2)}) %collective-permute-start.19) | collective-permute-done | bytes 262176 | tf_op jit(solution)/shard_map/ppermute | solution.py:512
  79.7 2.7 shard_map.134
  82.4 2.5 collective-permute-start.15
  84.9 46.5 %collective-permute-done.15.refs_4_.refs_32_ = bf16[1,2,128,512]{3,2,1,0:T(8,128)(2,1)S(1)} collective-permute-done((bf16[1,2,128,512]{3,2,1,0:T(8,128)(2,1)}, bf16[1,2,128,512]{3,2,1,0:T(8,128)(2,1)S(1)}, u32[]{:S(2)}, u32[]{:S(2)}) %collective-permute-start.15) | collective-permute-done | bytes 262176 | tf_op jit(solution)/shard_map/ppermute | solution.py:586
  134.6 2.0 collective-permute-start.1
  138.6 2.9 collective-permute-done.16.refs_5_.refs_33_
  143.2 3.0 %shard_map.136.refs_14_.refs_8_.refs_20_ = bf16[2,2,128,512]{3,2,1,0:T(8,128)(2,1)} custom-call(s32[1]{0:T(128)} %bitcast.device_ref, s32[32,3]{1,0:T(8,128)} %constant.39.clone.place_ref, bf16[128,4096]{1,0:T(8,128)(2,1)} %collective-permute-done.refs_0_.refs_2_, bf16[128,4096]{1,0:T(8,128)(2,1)} %collective-permute-done.3.refs_1_.refs_3_, ...), custom_call_target="tpu_custom_call" | custom-call | tf_op jit(solution)/shard_map/pallas_call | solution.py:184
  147.7 13.2 %collective-permute-done.10.refs_4_.refs_9_ = bf16[128,4096]{1,0:T(8,128)(2,1)} collective-permute-done((bf16[128,4096]{1,0:T(8,128)(2,1)}, bf16[128,4096]{1,0:T(8,128)(2,1)}, u32[]{:S(2)}, u32[]{:S(2)}) %collective-permute-start.10) | collective-permute-done | bytes 1048608 | tf_op jit(solution)/shard_map/ppermute | solution.py:578
  161.0 2.0 collective-permute-start.2
  162.9 20.5 %collective-permute-done.4.refs_1_.refs_7_ = bf16[128,4096]{1,0:T(8,128)(2,1)} collective-permute-done((bf16[128,4096]{1,0:T(8,128)(2,1)}, bf16[128,4096]{1,0:T(8,128)(2,1)}, u32[]{:S(2)}, u32[]{:S(2)}) %collective-permute-start.4) | collective-permute-done | bytes 1048608 | tf_op jit(solution)/shard_map/ppermute | solution.py:577
  183.4 2.0 collective-permute-start.5
  185.5 2.1 collective-permute-done.23.refs_16_.refs_10_.refs_22_
  188.9 3.1 %shard_map.137.refs_18_.refs_12_.refs_24_ = bf16[2,2,128,512]{3,2,1,0:T(8,128)(2,1)} custom-call(s32[1]{0:T(128)} %bitcast.device_ref, s32[32,3]{1,0:T(8,128)} %constant.40.clone.place_ref, bf16[128,4096]{1,0:T(8,128)(2,1)} %collective-permute-done.1.refs_0_.refs_6_, bf16[128,4096]{1,0:T(8,128)(2,1)} %collective-permute-done.4.refs_1_.refs_7_, ...), custom_call_target="tpu_custom_call" | custom-call | tf_op jit(solution)/shard_map/pallas_call | solution.py:184
  192.0 13.8 %collective-permute-done.11.refs_4_.refs_3_ = bf16[128,4096]{1,0:T(8,128)(2,1)} collective-permute-done((bf16[128,4096]{1,0:T(8,128)(2,1)}, bf16[128,4096]{1,0:T(8,128)(2,1)}, u32[]{:S(2)}, u32[]{:S(2)}) %collective-permute-start.11) | collective-permute-done | bytes 1048608 | tf_op jit(solution)/shard_map/ppermute | solution.py:578
  207.1 6.5 %collective-permute-start.32 = (bf16[128,4096]{1,0:T(8,128)(2,1)}, bf16[128,4096]{1,0:T(8,128)(2,1)}, u32[]{:S(2)}, u32[]{:S(2)}) collective-permute-start(bf16[128,4096]{1,0:T(8,128)(2,1)} %collective-permute-done.6.refs_3_.refs_4_), channel_id=1, source_target_pairs={{5,4},{2,3},{13,12},{10,11},{21,20},{18,19},{29,28},{26,27}} | collective-permute-start | bytes 3145736 | tf_op jit(solution)/shard_map/ppermute | solution.py:488
  213.7 13.6 %collective-permute-done.5.refs_1_ = bf16[128,4096]{1,0:T(8,128)(2,1)} collective-permute-done((bf16[128,4096]{1,0:T(8,128)(2,1)}, bf16[128,4096]{1,0:T(8,128)(2,1)}, u32[]{:S(2)}, u32[]{:S(2)}) %collective-permute-start.5) | collective-permute-done | bytes 1048608 | tf_op jit(solution)/shard_map/ppermute | solution.py:577
  227.9 3.0 %shard_map.133.refs_0_.refs_28_ = bf16[2,2,128,512]{3,2,1,0:T(8,128)(2,1)} custom-call(s32[1]{0:T(128)} %bitcast.device_ref, s32[32,3]{1,0:T(8,128)} %constant.41.clone.place_ref, bf16[128,4096]{1,0:T(8,128)(2,1)} %collective-permute-done.2.refs_0_, bf16[128,4096]{1,0:T(8,128)(2,1)} %collective-permute-done.5.refs_1_, f32[8,128,1]{2,1,0:T(8,128)} %copy.24.refs_2_.refs_5_, ...), custom_call_target="tpu_custom_call" | custom-call | tf_op jit(solution)/shard_map/pallas_call | solution.py:184
  231.2 10.7 %collective-permute-done.25.refs_19_.refs_13_.refs_25_ = bf16[2,2,128,512]{3,2,1,0:T(8,128)(2,1)} collective-permute-done((bf16[2,2,128,512]{3,2,1,0:T(8,128)(2,1)}, bf16[2,2,128,512]{3,2,1,0:T(8,128)(2,1)}, u32[]{:S(2)}, u32[]{:S(2)}) %collective-permute-start.25) | collective-permute-done | bytes 524320 | tf_op jit(solution)/shard_map/ppermute | solution.py:512
  243.4 3.8 %collective-permute-start.33 = (bf16[128,4096]{1,0:T(8,128)(2,1)}, bf16[128,4096]{1,0:T(8,128)(2,1)}, u32[]{:S(2)}, u32[]{:S(2)}) collective-permute-start(bf16[128,4096]{1,0:T(8,128)(2,1)} %collective-permute-done.9.refs_4_.refs_5_), channel_id=1, source_target_pairs={{5,4},{2,3},{13,12},{10,11},{21,20},{18,19},{29,28},{26,27}} | collective-permute-start | bytes 3145736 | tf_op jit(solution)/shard_map/ppermute | solution.py:488
  248.9 2.3 collective-permute-start.29
  251.2 5.3 %collective-permute-done.12.refs_1_.refs_29_ = bf16[2,2,128,512]{3,2,1,0:T(8,128)(2,1)S(1)} collective-permute-done((bf16[2,2,128,512]{3,2,1,0:T(8,128)(2,1)}, bf16[2,2,128,512]{3,2,1,0:T(8,128)(2,1)S(1)}, u32[]{:S(2)}, u32[]{:S(2)}) %collective-permute-start.12) | collective-permute-done | bytes 524320 | tf_op jit(solution)/shard_map/ppermute | solution.py:512
  256.6 18.5 %shard_map.138 = (f32[2,1024,512]{2,1,0:T(8,128)}, bf16[2,640,1536]{2,1,0:T(8,128)(2,1)}) custom-call(s32[1]{0:T(128)} %bitcast.device_ref, s32[32,49]{1,0:T(8,128)} %constant.43.clone.plan_ref, s32[2,8]{1,0:T(2,128)} %convert_element_type.3.used_ref, bf16[128,4096]{1,0:T(8,128)(2,1)} %shard_map.131.refs_0_, bf16[128,4096]{1,0:T(8,128)(2,1)} %shard_map.132.refs_1_, ...), custom_call_target="tpu_custom_call" | custom-call | flops 10737418240 | bytes 83886080 | tf_op jit(solution)/shard_map/pallas_call | solution.py:437
  275.1 9.5 %shard_map.139 = (f32[2,1024,512]{2,1,0:T(8,128)}, bf16[2,256,1536]{2,1,0:T(8,128)(2,1)}) custom-call(s32[1]{0:T(128)} %bitcast.device_ref, s32[32,46]{1,0:T(8,128)} %constant.44.clone.plan_ref, s32[2,8]{1,0:T(2,128)} %convert_element_type.3.used_ref, bf16[128,4096]{1,0:T(8,128)(2,1)} %collective-permute-done.2.refs_0_, ...), custom_call_target="tpu_custom_call", output_to_operand_aliasing={{0}: (19, {})} | custom-call | flops 4294967296 | bytes 83886080 | tf_op jit(solution)/shard_map/pallas_call | solution.py:437
  285.6 15.0 %shard_map.140 = f32[2,1024,512]{2,1,0:T(8,128)} custom-call(s32[1]{0:T(128)} %bitcast.device_ref, s32[32,53]{1,0:T(8,128)} %constant.45.clone.plan_ref, s32[2,8]{1,0:T(2,128)} %convert_element_type.3.used_ref, bf16[2,2,128,512]{3,2,1,0:T(8,128)(2,1)} %shard_map.133.refs_0_.refs_28_, ...), custom_call_target="tpu_custom_call", output_to_operand_aliasing={{}: (39, {})} | custom-call | flops 7784628224 | bytes 83886080 | tf_op jit(solution)/shard_map/pallas_call | solution.py:437
  (94 shorter events, 22.8 us)
Async XLA Ops:
  32.7 30.0 %all-to-all-start.1 = ((bf16[32,128,128]{2,1,0:T(8,128)(2,1)}), bf16[32,128,128]{2,1,0:T(8,128)(2,1)S(1)}, u32[]{:S(2)}, u32[]{:S(2)}) async-start(bf16[32,128,128]{2,1,0:T(8,128)(2,1)} %get-tuple-element.12), calls=%async_computation.1 | async-start | bytes 2097152 | tf_op jit(solution)/shard_map/all_to_all | solution.py:524
  69.6 8.8 %collective-permute-start.19 = (bf16[1,2,128,512]{3,2,1,0:T(8,128)(2,1)}, bf16[1,2,128,512]{3,2,1,0:T(8,128)(2,1)S(1)}, u32[]{:S(2)}, u32[]{:S(2)}) collective-permute-start(bf16[1,2,128,512]{3,2,1,0:T(8,128)(2,1)} %shard_map.135.refs_10_.refs_4_.refs_16_), channel_id=1, source_target_pairs={{0,16},{8,24},{16,0},{24,8},{1,17},{9,25},{17,1},{25,9},{2,18},{10... | collective-permute-start | bytes 786440 | tf_op jit(solution)/shard_map/ppermute | solution.py:512
  71.2 63.3 %collective-permute-start.9 = (bf16[128,4096]{1,0:T(8,128)(2,1)}, bf16[128,4096]{1,0:T(8,128)(2,1)}, u32[]{:S(2)}, u32[]{:S(2)}) collective-permute-start(bf16[128,4096]{1,0:T(8,128)(2,1)} %shard_map.132.refs_1_), channel_id=1, source_target_pairs={{2,0},{4,2},{6,4},{7,6},{5,7},{3,5},{1,3},{0,1},{10,8},{12,10},{14... | collective-permute-start | bytes 3145736 | tf_op jit(solution)/shard_map/ppermute | solution.py:530
  72.0 62.5 %collective-permute-start = (bf16[128,4096]{1,0:T(8,128)(2,1)S(1)}, bf16[128,4096]{1,0:T(8,128)(2,1)}, u32[]{:S(2)}, u32[]{:S(2)}) collective-permute-start(bf16[128,4096]{1,0:T(8,128)(2,1)S(1)} %copy-done.1), channel_id=1, source_target_pairs={{0,2},{2,4},{4,6},{6,7},{7,5},{5,3},{3,1},{1,0},{8,10},{10,12},{12... | collective-permute-start | bytes 3145736 | tf_op jit(solution)/shard_map/ppermute | solution.py:529
  73.2 63.3 %collective-permute-start.3 = (bf16[128,4096]{1,0:T(8,128)(2,1)}, bf16[128,4096]{1,0:T(8,128)(2,1)}, u32[]{:S(2)}, u32[]{:S(2)}) collective-permute-start(bf16[128,4096]{1,0:T(8,128)(2,1)} %shard_map.132.refs_1_), channel_id=1, source_target_pairs={{0,2},{2,4},{4,6},{6,7},{7,5},{5,3},{3,1},{1,0},{8,10},{10,12},{12... | collective-permute-start | bytes 3145736 | tf_op jit(solution)/shard_map/ppermute | solution.py:529
  74.0 8.4 %collective-permute-start.20 = (bf16[1,2,128,512]{3,2,1,0:T(8,128)(2,1)}, bf16[1,2,128,512]{3,2,1,0:T(8,128)(2,1)}, u32[]{:S(2)}, u32[]{:S(2)}) collective-permute-start(bf16[1,2,128,512]{3,2,1,0:T(8,128)(2,1)} %shard_map.135.refs_10_.refs_4_.refs_16_), channel_id=1, source_target_pairs={{0,8},{8,0},{16,24},{24,16},{1,9},{9,1},{17,25},{25,17},{2,10},{10... | collective-permute-start | bytes 786440 | tf_op jit(solution)/shard_map/ppermute | solution.py:512
  78.4 58.7 %collective-permute-start.6 = (bf16[128,4096]{1,0:T(8,128)(2,1)S(1)}, bf16[128,4096]{1,0:T(8,128)(2,1)}, u32[]{:S(2)}, u32[]{:S(2)}) collective-permute-start(bf16[128,4096]{1,0:T(8,128)(2,1)S(1)} %copy-done.1), channel_id=1, source_target_pairs={{2,0},{4,2},{6,4},{7,6},{5,7},{3,5},{1,3},{0,1},{10,8},{12,10},{14... | collective-permute-start | bytes 3145736 | tf_op jit(solution)/shard_map/ppermute | solution.py:530
  82.4 49.1 %collective-permute-start.15 = (bf16[1,2,128,512]{3,2,1,0:T(8,128)(2,1)}, bf16[1,2,128,512]{3,2,1,0:T(8,128)(2,1)S(1)}, u32[]{:S(2)}, u32[]{:S(2)}) collective-permute-start(bf16[1,2,128,512]{3,2,1,0:T(8,128)(2,1)} %shard_map.134), channel_id=1, source_target_pairs={{0,7},{2,5},{4,3},{6,1},{7,0},{5,2},{3,4},{1,6},{8,15},{10,13},{12... | collective-permute-start | bytes 786440 | tf_op jit(solution)/shard_map/ppermute | solution.py:586
  133.2 8.3 %collective-permute-start.16 = (bf16[1,2,128,512]{3,2,1,0:T(8,128)(2,1)S(1)}, bf16[1,2,128,512]{3,2,1,0:T(8,128)(2,1)S(1)}, u32[]{:S(2)}, u32[]{:S(2)}) collective-permute-start(bf16[1,2,128,512]{3,2,1,0:T(8,128)(2,1)S(1)} %collective-permute-done.15.refs_4_.refs_32_), channel_id=1, source_target_pairs={{0,16},{8,24},{16,0},{24,8},{1,17},{9,25},{17,1},{25,9},{2,18},{10... | collective-permute-start | bytes 786440 | tf_op jit(solution)/shard_map/ppermute | solution.py:512
  134.6 26.3 %collective-permute-start.10 = (bf16[128,4096]{1,0:T(8,128)(2,1)}, bf16[128,4096]{1,0:T(8,128)(2,1)}, u32[]{:S(2)}, u32[]{:S(2)}) collective-permute-start(bf16[128,4096]{1,0:T(8,128)(2,1)} %collective-permute-done.9.refs_4_.refs_5_), channel_id=1, source_target_pairs={{2,0},{4,2},{6,4},{7,6},{5,7},{3,5},{1,3},{0,1},{10,8},{12,10},{14... | collective-permute-start | bytes 3145736 | tf_op jit(solution)/shard_map/ppermute | solution.py:578
  134.6 26.4 %collective-permute-start.1 = (bf16[128,4096]{1,0:T(8,128)(2,1)}, bf16[128,4096]{1,0:T(8,128)(2,1)}, u32[]{:S(2)}, u32[]{:S(2)}) collective-permute-start(bf16[128,4096]{1,0:T(8,128)(2,1)} %collective-permute-done.refs_0_.refs_2_), channel_id=1, source_target_pairs={{0,2},{2,4},{4,6},{6,7},{7,5},{5,3},{3,1},{1,0},{8,10},{10,12},{12... | collective-permute-start | bytes 3145736 | tf_op jit(solution)/shard_map/ppermute | solution.py:577
  136.6 46.8 %collective-permute-start.4 = (bf16[128,4096]{1,0:T(8,128)(2,1)}, bf16[128,4096]{1,0:T(8,128)(2,1)}, u32[]{:S(2)}, u32[]{:S(2)}) collective-permute-start(bf16[128,4096]{1,0:T(8,128)(2,1)} %collective-permute-done.3.refs_1_.refs_3_), channel_id=1, source_target_pairs={{0,2},{2,4},{4,6},{6,7},{7,5},{5,3},{3,1},{1,0},{8,10},{10,12},{12... | collective-permute-start | bytes 3145736 | tf_op jit(solution)/shard_map/ppermute | solution.py:577
  137.1 48.3 %collective-permute-start.7 = (bf16[128,4096]{1,0:T(8,128)(2,1)}, bf16[128,4096]{1,0:T(8,128)(2,1)}, u32[]{:S(2)}, u32[]{:S(2)}) collective-permute-start(bf16[128,4096]{1,0:T(8,128)(2,1)} %collective-permute-done.6.refs_3_.refs_4_), channel_id=1, source_target_pairs={{2,0},{4,2},{6,4},{7,6},{5,7},{3,5},{1,3},{0,1},{10,8},{12,10},{14... | collective-permute-start | bytes 3145736 | tf_op jit(solution)/shard_map/ppermute | solution.py:578
  143.0 3.2 %collective-permute-start.18 = (bf16[1,2,128,512]{3,2,1,0:T(8,128)(2,1)S(1)}, bf16[1,2,128,512]{3,2,1,0:T(8,128)(2,1)S(1)}, u32[]{:S(2)}, u32[]{:S(2)}) collective-permute-start(bf16[1,2,128,512]{3,2,1,0:T(8,128)(2,1)S(1)} %collective-permute-done.16.refs_5_.refs_33_), channel_id=1, source_target_pairs={{0,8},{8,0},{16,24},{24,16},{1,9},{9,1},{17,25},{25,17},{2,10},{10... | collective-permute-start | bytes 786440 | tf_op jit(solution)/shard_map/ppermute | solution.py:512
  146.2 39.3 %collective-permute-start.22 = (bf16[2,2,128,512]{3,2,1,0:T(8,128)(2,1)}, bf16[2,2,128,512]{3,2,1,0:T(8,128)(2,1)S(1)}, u32[]{:S(2)}, u32[]{:S(2)}) collective-permute-start(bf16[2,2,128,512]{3,2,1,0:T(8,128)(2,1)} %shard_map.136.refs_14_.refs_8_.refs_20_), channel_id=1, source_target_pairs={{0,16},{8,24},{16,0},{24,8},{1,17},{9,25},{17,1},{25,9},{2,18},{10... | collective-permute-start | bytes 1572872 | tf_op jit(solution)/shard_map/ppermute | solution.py:512
  160.9 44.9 %collective-permute-start.11 = (bf16[128,4096]{1,0:T(8,128)(2,1)}, bf16[128,4096]{1,0:T(8,128)(2,1)}, u32[]{:S(2)}, u32[]{:S(2)}) collective-permute-start(bf16[128,4096]{1,0:T(8,128)(2,1)} %collective-permute-done.10.refs_4_.refs_9_), channel_id=1, source_target_pairs={{2,0},{4,2},{6,4},{7,6},{5,7},{3,5},{1,3},{0,1},{10,8},{12,10},{14... | collective-permute-start | bytes 3145736 | tf_op jit(solution)/shard_map/ppermute | solution.py:578
  161.0 46.2 %collective-permute-start.2 = (bf16[128,4096]{1,0:T(8,128)(2,1)}, bf16[128,4096]{1,0:T(8,128)(2,1)}, u32[]{:S(2)}, u32[]{:S(2)}) collective-permute-start(bf16[128,4096]{1,0:T(8,128)(2,1)} %collective-permute-done.1.refs_0_.refs_6_), channel_id=1, source_target_pairs={{0,2},{2,4},{4,6},{6,7},{7,5},{5,3},{3,1},{1,0},{8,10},{10,12},{12... | collective-permute-start | bytes 3145736 | tf_op jit(solution)/shard_map/ppermute | solution.py:577
  183.4 43.8 %collective-permute-start.5 = (bf16[128,4096]{1,0:T(8,128)(2,1)}, bf16[128,4096]{1,0:T(8,128)(2,1)}, u32[]{:S(2)}, u32[]{:S(2)}) collective-permute-start(bf16[128,4096]{1,0:T(8,128)(2,1)} %collective-permute-done.4.refs_1_.refs_7_), channel_id=1, source_target_pairs={{0,2},{2,4},{4,6},{6,7},{7,5},{5,3},{3,1},{1,0},{8,10},{10,12},{12... | collective-permute-start | bytes 3145736 | tf_op jit(solution)/shard_map/ppermute | solution.py:577
  185.4 41.9 %collective-permute-start.8 = (bf16[128,4096]{1,0:T(8,128)(2,1)}, bf16[128,4096]{1,0:T(8,128)(2,1)}, u32[]{:S(2)}, u32[]{:S(2)}) collective-permute-start(bf16[128,4096]{1,0:T(8,128)(2,1)} %collective-permute-done.7.refs_3_.refs_8_), channel_id=1, source_target_pairs={{2,0},{4,2},{6,4},{7,6},{5,7},{3,5},{1,3},{0,1},{10,8},{12,10},{14... | collective-permute-start | bytes 3145736 | tf_op jit(solution)/shard_map/ppermute | solution.py:578
  187.6 54.3 %collective-permute-start.30 = (bf16[128,4096]{1,0:T(8,128)(2,1)}, bf16[128,4096]{1,0:T(8,128)(2,1)S(1)}, u32[]{:S(2)}, u32[]{:S(2)}) collective-permute-start(bf16[128,4096]{1,0:T(8,128)(2,1)} %collective-permute-done.refs_0_.refs_2_), channel_id=1, source_target_pairs={{3,2},{4,5},{11,10},{12,13},{19,18},{20,21},{27,26},{28,29}} | collective-permute-start | bytes 3145736 | tf_op jit(solution)/shard_map/ppermute | solution.py:488
  205.8 37.6 %collective-permute-start.31 = (bf16[128,4096]{1,0:T(8,128)(2,1)}, bf16[128,4096]{1,0:T(8,128)(2,1)}, u32[]{:S(2)}, u32[]{:S(2)}) collective-permute-start(bf16[128,4096]{1,0:T(8,128)(2,1)} %collective-permute-done.3.refs_1_.refs_3_), channel_id=1, source_target_pairs={{3,2},{4,5},{11,10},{12,13},{19,18},{20,21},{27,26},{28,29}} | collective-permute-start | bytes 3145736 | tf_op jit(solution)/shard_map/ppermute | solution.py:488
  207.1 40.1 %collective-permute-start.32 = (bf16[128,4096]{1,0:T(8,128)(2,1)}, bf16[128,4096]{1,0:T(8,128)(2,1)}, u32[]{:S(2)}, u32[]{:S(2)}) collective-permute-start(bf16[128,4096]{1,0:T(8,128)(2,1)} %collective-permute-done.6.refs_3_.refs_4_), channel_id=1, source_target_pairs={{5,4},{2,3},{13,12},{10,11},{21,20},{18,19},{29,28},{26,27}} | collective-permute-start | bytes 3145736 | tf_op jit(solution)/shard_map/ppermute | solution.py:488
  227.3 3.7 %collective-permute-start.24 = (bf16[2,2,128,512]{3,2,1,0:T(8,128)(2,1)S(1)}, bf16[2,2,128,512]{3,2,1,0:T(8,128)(2,1)S(1)}, u32[]{:S(2)}, u32[]{:S(2)}) collective-permute-start(bf16[2,2,128,512]{3,2,1,0:T(8,128)(2,1)S(1)} %collective-permute-done.22.refs_15_.refs_9_.refs_21_), channel_id=1, source_target_pairs={{0,8},{8,0},{16,24},{24,16},{1,9},{9,1},{17,25},{25,17},{2,10},{10... | collective-permute-start | bytes 1572872 | tf_op jit(solution)/shard_map/ppermute | solution.py:512
  227.3 14.7 %collective-permute-start.25 = (bf16[2,2,128,512]{3,2,1,0:T(8,128)(2,1)}, bf16[2,2,128,512]{3,2,1,0:T(8,128)(2,1)}, u32[]{:S(2)}, u32[]{:S(2)}) collective-permute-start(bf16[2,2,128,512]{3,2,1,0:T(8,128)(2,1)} %shard_map.137.refs_18_.refs_12_.refs_24_), channel_id=1, source_target_pairs={{0,16},{8,24},{16,0},{24,8},{1,17},{9,25},{17,1},{25,9},{2,18},{10... | collective-permute-start | bytes 1572872 | tf_op jit(solution)/shard_map/ppermute | solution.py:512
  231.0 16.3 %collective-permute-start.26 = (bf16[2,2,128,512]{3,2,1,0:T(8,128)(2,1)S(1)}, bf16[2,2,128,512]{3,2,1,0:T(8,128)(2,1)S(1)}, u32[]{:S(2)}, u32[]{:S(2)}) collective-permute-start(bf16[2,2,128,512]{3,2,1,0:T(8,128)(2,1)S(1)} %copy-done.6), channel_id=1, source_target_pairs={{0,8},{8,0},{16,24},{24,16},{1,9},{9,1},{17,25},{25,17},{2,10},{10... | collective-permute-start | bytes 1572872 | tf_op jit(solution)/shard_map/ppermute | solution.py:512
  241.9 7.0 %collective-permute-start.27 = (bf16[2,2,128,512]{3,2,1,0:T(8,128)(2,1)}, bf16[2,2,128,512]{3,2,1,0:T(8,128)(2,1)S(1)}, u32[]{:S(2)}, u32[]{:S(2)}) collective-permute-start(bf16[2,2,128,512]{3,2,1,0:T(8,128)(2,1)} %collective-permute-done.25.refs_19_.refs_13_.refs_25_), channel_id=1, source_target_pairs={{0,8},{8,0},{16,24},{24,16},{1,9},{9,1},{17,25},{25,17},{2,10},{10... | collective-permute-start | bytes 1572872 | tf_op jit(solution)/shard_map/ppermute | solution.py:512
  241.9 14.6 %collective-permute-start.12 = (bf16[2,2,128,512]{3,2,1,0:T(8,128)(2,1)}, bf16[2,2,128,512]{3,2,1,0:T(8,128)(2,1)S(1)}, u32[]{:S(2)}, u32[]{:S(2)}) collective-permute-start(bf16[2,2,128,512]{3,2,1,0:T(8,128)(2,1)} %shard_map.133.refs_0_.refs_28_), channel_id=1, source_target_pairs={{0,16},{8,24},{16,0},{24,8},{1,17},{9,25},{17,1},{25,9},{2,18},{10... | collective-permute-start | bytes 1572872 | tf_op jit(solution)/shard_map/ppermute | solution.py:512
  243.4 41.2 %collective-permute-start.33 = (bf16[128,4096]{1,0:T(8,128)(2,1)}, bf16[128,4096]{1,0:T(8,128)(2,1)}, u32[]{:S(2)}, u32[]{:S(2)}) collective-permute-start(bf16[128,4096]{1,0:T(8,128)(2,1)} %collective-permute-done.9.refs_4_.refs_5_), channel_id=1, source_target_pairs={{5,4},{2,3},{13,12},{10,11},{21,20},{18,19},{29,28},{26,27}} | collective-permute-start | bytes 3145736 | tf_op jit(solution)/shard_map/ppermute | solution.py:488
  247.2 37.4 %collective-permute-start.13 = (bf16[2,2,128,512]{3,2,1,0:T(8,128)(2,1)}, bf16[2,2,128,512]{3,2,1,0:T(8,128)(2,1)S(1)}, u32[]{:S(2)}, u32[]{:S(2)}) collective-permute-start(bf16[2,2,128,512]{3,2,1,0:T(8,128)(2,1)} %shard_map.133.refs_0_.refs_28_), channel_id=1, source_target_pairs={{0,8},{8,0},{16,24},{24,16},{1,9},{9,1},{17,25},{25,17},{2,10},{10... | collective-permute-start | bytes 1572872 | tf_op jit(solution)/shard_map/ppermute | solution.py:512
  247.3 37.4 %collective-permute-start.28 = (bf16[128,4096]{1,0:T(8,128)(2,1)}, bf16[128,4096]{1,0:T(8,128)(2,1)}, u32[]{:S(2)}, u32[]{:S(2)}) collective-permute-start(bf16[128,4096]{1,0:T(8,128)(2,1)} %collective-permute-done.2.refs_0_), channel_id=1, source_target_pairs={{1,0},{4,6},{6,7},{3,1},{9,8},{12,14},{14,15},{11,9},{17,16},{20,2... | collective-permute-start | bytes 3145736 | tf_op jit(solution)/shard_map/ppermute | solution.py:598
  248.9 35.8 %collective-permute-start.29 = (bf16[128,4096]{1,0:T(8,128)(2,1)}, bf16[128,4096]{1,0:T(8,128)(2,1)}, u32[]{:S(2)}, u32[]{:S(2)}) collective-permute-start(bf16[128,4096]{1,0:T(8,128)(2,1)} %collective-permute-done.11.refs_4_.refs_3_), channel_id=1, source_target_pairs={{2,0},{7,6},{5,7},{0,1},{10,8},{15,14},{13,15},{8,9},{18,16},{23,2... | collective-permute-start | bytes 3145736 | tf_op jit(solution)/shard_map/ppermute | solution.py:598
  256.5 28.1 %collective-permute-start.14 = (bf16[2,2,128,512]{3,2,1,0:T(8,128)(2,1)S(1)}, bf16[2,2,128,512]{3,2,1,0:T(8,128)(2,1)S(1)}, u32[]{:S(2)}, u32[]{:S(2)}) collective-permute-start(bf16[2,2,128,512]{3,2,1,0:T(8,128)(2,1)S(1)} %collective-permute-done.12.refs_1_.refs_29_), channel_id=1, source_target_pairs={{0,8},{8,0},{16,24},{24,16},{1,9},{9,1},{17,25},{25,17},{2,10},{10... | collective-permute-start | bytes 1572872 | tf_op jit(solution)/shard_map/ppermute | solution.py:512
  (22 other events, 807.4 us)
